TPU v7x, 256 devices: a whole 4x4x8 slice. The times are simulated.
256 devices in a mesh: lat: 32 (over z, x), lon: 2 (over core), ens: 4 (over y).
Axes of the slice: x: 4, y: 4, z: 8, core: 2. Of those that a mesh axis runs over, the one named last changes fastest.
Arguments:
- fields: bfloat16 [1024, 256, 256], P(('ens', 'lat'), 'lon'), parts along dimension 0, may hold values from -6 to 6
- lon_taps: float32 [256, 4, 9], replicated, may hold values from -2 to 2
- lat_taps: bfloat16 [256, 4, 6], P('lat'), may hold values from -2.5 to 2.5
- cycle_taps: bfloat16 [4, 8, 256], replicated, may hold values from -0.375 to 0.375
- band_start: int32 [256], P('lat'), may hold values from -4 to 254, as said below
- band_width: int32 [256], P('lat'), may hold values from 4 to 6, as said below
- mixing: bfloat16 [4, 256, 256], replicated, may hold values from -0.1875 to 0.1875
Outputs:
- layer_out: bfloat16 [1024, 256, 256], P(('ens', 'lat'), 'lon'), parts along dimension 0
There are 4 independent parts, one for each index of `ens`. A program takes and returns all parts, laid end to end along the dimension named above; an argument that names none is the same for every part. Nothing has to cross between parts.
Inputs may be any that keep to these rules, and one draw needn't show every extreme that they name: band_start[i] = i - 4 + s with s in 0 .. 3; s = 0 where i % 8 == 0 and s = 3 where i % 8 == 7. band_width[i] = 6 where i % 8 is 0 or 7.
All inputs are finite; a program needn't handle non-finite values.
Results may differ from a plain program's by a relative error of at most 0.0052.
Values may be sent and summed in bfloat16 or wider, within the bound.
A program may use at most 64 MiB of HBM per device.

v0:
```python
import jax
import jax.numpy as jnp
from jax import lax
from jax.sharding import PartitionSpec as P

HALO = 4


def extended_2(cells, sides, width, closed):
    for axis, dim in sides:
        count = lax.axis_size(axis)
        ends = count if closed else count - 1
        head = lax.slice_in_dim(cells, 0, width, axis=dim)
        tail = lax.slice_in_dim(cells, cells.shape[dim] - width, cells.shape[dim], axis=dim)
        cells = jnp.concatenate(
            [
                lax.ppermute(tail, axis, [(i, (i + 1) % count) for i in range(ends)]),
                cells,
                lax.ppermute(head, axis, [((i + 1) % count, i) for i in range(ends)]),
            ],
            axis=dim,
        )
    return cells


def toeplitz(coef, base, out_count, in_count, cycle_len):
    lead = coef.shape[:-1]
    window_len = out_count + in_count - 1
    tripled = jnp.concatenate([coef, coef, coef], axis=-1)
    begin = (base - in_count + 1) % cycle_len
    window = lax.dynamic_slice_in_dim(tripled, begin, window_len, len(lead))
    flipped = jnp.flip(window, axis=-1)
    rolled = jnp.roll(flipped, -(out_count - 1), axis=-1)
    tiled = jnp.tile(rolled, (1,) * len(lead) + (out_count,))
    cut = tiled[..., : out_count * (window_len - 1)]
    shaped = cut.reshape(lead + (out_count, window_len - 1))
    return shaped[..., :in_count]


def cycle_fold(coef, col_start, col_count, cycle_len, block_in):
    width_in = block_in.shape[1]
    circ = toeplitz(coef, col_start, col_count, width_in, cycle_len)
    return jnp.einsum("kpjm,pmc->kpjc", circ, block_in, preferred_element_type=jnp.float32)


def shards(fields, lon_taps, lat_taps, cycle_taps, band_start, band_width, mixing):
    row_count, col_count, chan_count = fields.shape
    basis_count = lon_taps.shape[1]
    reach_cells = (lon_taps.shape[2] - 1) // 2
    band_len = lat_taps.shape[2]
    polar_rows = row_count // 2
    lat_count = lax.axis_size("lat")
    lon_count = lax.axis_size("lon")
    cycle_len = lon_count * col_count
    lat_pos = lax.axis_index("lat")
    lon_pos = lax.axis_index("lon")
    leading = 0
    source_rows = fields.shape[0]
    padded = extended_2(fields, (("lon", 1),), reach_cells, True)
    taps_padded = jnp.pad(lon_taps, ((HALO, HALO), (0, 0), (0, 0)))
    taps_here = lax.dynamic_slice_in_dim(
        taps_padded, lat_pos * row_count + HALO - leading, source_rows, 0
    )
    accum = jnp.zeros((basis_count, source_rows, col_count, chan_count), jnp.float32)
    for offset in range(2 * reach_cells + 1):
        tap_now = jnp.transpose(taps_here[:, :, offset])
        accum = accum + tap_now[:, :, None, None] * padded[
            None, :, offset : offset + col_count, :
        ].astype(jnp.float32)
    near_rows = accum.astype(jnp.bfloat16)
    at_top = lat_pos == 0
    slot_start = jnp.where(at_top, 0, row_count - polar_rows).astype(jnp.int32)
    slot_rows = lax.dynamic_slice_in_dim(fields, slot_start, polar_rows, 0)
    col_start = lon_pos * col_count
    coef_start = jnp.where(at_top, 0, polar_rows).astype(jnp.int32)
    coef = lax.dynamic_slice_in_dim(cycle_taps, coef_start, polar_rows, 1)
    polar_sum = cycle_fold(
        coef, col_start, col_count, cycle_len, lax.all_gather(slot_rows, "lon", axis=1, tiled=True)
    )
    polar_z = polar_sum.astype(jnp.bfloat16)
    placed = lax.dynamic_update_slice_in_dim(
        jnp.zeros_like(near_rows), polar_z, slot_start + leading, 1
    )
    global_rows = lat_pos * row_count - leading + jnp.arange(source_rows, dtype=jnp.int32)
    is_polar = (global_rows < polar_rows) | (global_rows >= lat_count * row_count - polar_rows)
    filtered = jnp.where(is_polar[None, :, None, None], placed, near_rows)
    extended = extended_2(filtered, (("lat", 1),), HALO, False)
    ext_rows = row_count + 2 * HALO
    base_row = lat_pos * row_count
    steps_band = jnp.arange(band_len, dtype=jnp.int32)
    target = band_start[:, None] - base_row + HALO + steps_band[None, :]
    usable = steps_band[None, :] < band_width[:, None]
    ext_ids = jnp.arange(ext_rows, dtype=jnp.int32)
    select = ((target[:, :, None] == ext_ids[None, None, :]) & usable[:, :, None]).astype(
        jnp.float32
    )
    band_matrix = jnp.einsum("lkt,lte->kle", lat_taps.astype(jnp.float32), select).astype(
        jnp.bfloat16
    )
    hidden = jnp.einsum(
        "kle,kejc->ljkc", band_matrix, extended, preferred_element_type=jnp.float32
    ).astype(jnp.bfloat16)
    flat_hidden = hidden.reshape(row_count * col_count, basis_count * chan_count)
    flat_mix = mixing.reshape(basis_count * chan_count, chan_count)
    mixed = jnp.dot(flat_hidden, flat_mix, preferred_element_type=jnp.float32).reshape(
        row_count, col_count, chan_count
    )
    return (fields.astype(jnp.float32) + mixed).astype(jnp.bfloat16)


def solution(mesh):
    in_specs = (
        P(("ens", "lat"), "lon", None),
        P(),
        P("lat", None, None),
        P(),
        P("lat"),
        P("lat"),
        P(),
    )
    out_specs = P(("ens", "lat"), "lon", None)
    return jax.shard_map(shards, mesh=mesh, in_specs=in_specs, out_specs=out_specs, check_vma=False)
```

profile of v0, /device:TPU:118, one launch (start us, length us, event | category | flops | bytes accessed | tf_op | source)
XLA Modules:
  0.0 103.7 jit_solution(2339712264711648496)
XLA Ops:
  0.0 0.0 copy-start
  0.0 0.8 fusion.43
  0.9 0.1 collective-permute-start
  1.0 0.5 collective-permute-start.1
  1.5 0.7 constant_dynamic-slice_fusion
  2.2 0.1 fusion.32
  2.3 1.0 constant_dynamic-slice_fusion.1
  3.3 0.2 slice.92
  3.5 0.1 slice.94
  3.6 0.1 tile.4
  3.8 4.0 %tile.10 = bf16[4,4,49024]{2,1,0:T(4,128)(2,1)} reshape(bf16[4,4,128,383]{3,2,1,0:T(8,128)(2,1)S(1)} %tile.4) | data formatting | bytes 3137536 | tf_op jit(solution)/shard_map/tile | solution.py:34
  7.7 1.4 %slice-done = bf16[4,4,48896]{2,1,0:T(4,128)(2,1)S(1)} async-done(((bf16[4,4,49024]{2,1,0:T(4,128)(2,1)}), bf16[4,4,48896]{2,1,0:T(4,128)(2,1)S(1)}, s32[]{:S(2)}) %slice-start) | async-done | bytes 1564696 | tf_op jit(solution)/shard_map/slice | solution.py:35
  9.2 4.4 %reshape.90 = bf16[4,4,128,382]{3,2,1,0:T(8,128)(2,1)} reshape(bf16[4,4,48896]{2,1,0:T(4,128)(2,1)S(1)} %slice-done) | data formatting | bytes 3129344 | tf_op jit(solution)/shard_map/reshape | solution.py:36
  13.6 0.2 copy.54
  13.7 2.2 %all_gather.3 = bf16[4,256,256]{1,2,0:T(8,128)(2,1)S(1)} all-gather(bf16[4,128,256]{1,2,0:T(8,128)(2,1)S(1)} %copy.54), channel_id=1, replica_groups=mesh['lat'=32,'lon'=2,'ens'=4] {'lon'}, dimensions={1}, use_global_device_ids=true | all-gather | bytes 786432 | tf_op jit(solution)/shard_map/all_gather | solution.py:78
  15.9 1.8 %broadcast_in_dim.8 = bf16[4,8,128,256]{2,3,0,1:T(8,128)(2,1)} broadcast(bf16[]{:T(256)} %constant.39.clone.1), dimensions={} | broadcast | bytes 2097154 | tf_op jit(solution)/shard_map/broadcast_in_dim | solution.py:82
  17.7 2.7 %fusion.8 = bf16[4,8,128,256]{2,3,0,1:T(8,128)(2,1)} fusion(bf16[4,8,128,256]{2,3,0,1:T(8,128)(2,1)} %broadcast_in_dim.8, s32[]{:T(128)S(6)} %select_n.25, bf16[4,256,256]{1,2,0:T(8,128)(2,1)S(1)} %all_gather.3, bf16[4,4,128,382]{3,2,1,0:T(8,128)(2,1)} %reshape.90), kind=kOutput, calls=%fused_computation.9 | convolution fusion | flops 268959744 | bytes 2621444 | tf_op jit(solution)/shard_map/kpjm,pmc->kpjc/dot_general | solution.py:43
  20.4 0.0 copy-done.2
  20.4 0.1 fusion.33
  20.5 0.0 copy-done.1
  20.5 1.2 %copy.39 = f32[8,128,256]{1,2,0:T(8,128)} copy(bf16[8,128,256]{2,1,0:T(8,128)(2,1)S(1)} %copy-done.1) | data formatting | bytes 1572864 | tf_op jit(solution)/shard_map/convert_element_type | solution.py:108
  21.7 0.1 copy.30
  21.8 0.1 copy.32
  21.9 0.1 copy.34
  21.9 0.1 copy.36
  22.0 0.1 copy.38
  22.1 0.1 copy.40
  22.2 0.1 copy.42
  22.3 0.1 copy.44
  22.3 0.1 copy.46
  22.4 0.0 collective-permute-done
  22.4 1.9 %fusion.20 = (f32[8,128,256]{2,1,0:T(8,128)}, f32[8,128,256]{2,1,0:T(8,128)}, f32[8,128,256]{2,1,0:T(8,128)S(1)}, f32[8,128,256]{2,1,0:T(8,128)S(1)}, bf16[8,132,256]{2,1,0:T(8,128)(2,1)S(1)}) fusion(bf16[8,4,256]{2,1,0:T(4,128)(2,1)S(1)} %collective-permute-done, bf16[8,128,256]{2,1,0:T(8,128)(2,1)S(1)} %copy-done.1), kind=kLoop, calls=%fused_computation.21 | loop fusion | flops 4194303 | bytes 5259264 | tf_op jit(solution)/shard_map/convert_element_type | solution.py:69
  24.3 0.0 collective-permute-done.1
  24.4 2.2 %slice_convert_fusion.3 = (f32[8,128,256]{2,1,0:T(8,128)}, f32[8,128,256]{2,1,0:T(8,128)}, f32[8,128,256]{2,1,0:T(8,128)}, f32[8,128,256]{2,1,0:T(8,128)}) fusion(bf16[8,132,256]{2,1,0:T(8,128)(2,1)S(1)} %constant_dynamic-update-slice_fusion), kind=kLoop, calls=%fused_computation.27 | loop fusion | flops 1048576 | bytes 6291456 | tf_op jit(solution)/shard_map/convert_element_type | solution.py:69
  26.5 2.5 %copy.41 = f32[8,128,256]{1,2,0:T(8,128)} copy(f32[8,128,256]{2,1,0:T(8,128)} %get-tuple-element.7) | data formatting | bytes 2097152 | tf_op jit(solution)/shard_map/convert_element_type | solution.py:69
  29.1 2.6 %copy.43 = f32[8,128,256]{1,2,0:T(8,128)} copy(f32[8,128,256]{2,1,0:T(8,128)} %get-tuple-element.10) | data formatting | bytes 2097152 | tf_op jit(solution)/shard_map/convert_element_type | solution.py:69
  31.6 2.6 %copy.45 = f32[8,128,256]{1,2,0:T(8,128)} copy(f32[8,128,256]{2,1,0:T(8,128)} %get-tuple-element.9) | data formatting | bytes 2097152 | tf_op jit(solution)/shard_map/convert_element_type | solution.py:69
  34.2 2.6 %copy.47 = f32[8,128,256]{1,2,0:T(8,128)} copy(f32[8,128,256]{2,1,0:T(8,128)} %get-tuple-element.8) | data formatting | bytes 2097152 | tf_op jit(solution)/shard_map/convert_element_type | solution.py:69
  36.9 2.5 %copy.31 = f32[8,128,256]{1,2,0:T(8,128)} copy(f32[8,128,256]{2,1,0:T(8,128)} %get-tuple-element.11) | data formatting | bytes 2097152 | tf_op jit(solution)/shard_map/convert_element_type | solution.py:69
  39.4 2.6 %copy.33 = f32[8,128,256]{1,2,0:T(8,128)} copy(f32[8,128,256]{2,1,0:T(8,128)} %get-tuple-element.12) | data formatting | bytes 2097152 | tf_op jit(solution)/shard_map/convert_element_type | solution.py:69
  42.0 1.3 %copy.35 = f32[8,128,256]{1,2,0:T(8,128)} copy(f32[8,128,256]{2,1,0:T(8,128)S(1)} %get-tuple-element.14) | data formatting | bytes 2097152 | tf_op jit(solution)/shard_map/convert_element_type | solution.py:69
  43.3 1.3 %copy.37 = f32[8,128,256]{1,2,0:T(8,128)} copy(f32[8,128,256]{2,1,0:T(8,128)S(1)} %get-tuple-element.13) | data formatting | bytes 2097152 | tf_op jit(solution)/shard_map/convert_element_type | solution.py:69
  44.6 6.3 %fusion = bf16[4,8,128,256]{2,3,0,1:T(8,128)(2,1)S(1)} fusion(bf16[4,8,128,256]{2,3,0,1:T(8,128)(2,1)} %fusion.8, f32[8,128,256]{1,2,0:T(8,128)} %copy.47, f32[4,8]{0,1:T(8,128)S(1)} %copy.46, f32[8,128,256]{1,2,0:T(8,128)} %copy.45, f32[4,8]{0,1:T(8,128)S(1)} %copy.44, f32[8,128,256]{1,2,0:T(8,128)} %copy.43, f32[4,8]{0,1:T(8,128)S(1)} %copy.42, ...), kind=kLoop, calls=%fused_computation.3 | loop fusion | flops 19922944 | bytes 13632648 | tf_op jit(solution)/shard_map/jit(_where)/select_n | solution.py:86
  51.0 0.0 copy-start.3
  51.0 0.0 copy-start.4
  51.0 0.0 copy-start.5
  51.0 1.5 %fusion.42 = (bf16[4,4,128,256]{2,3,0,1:T(8,128)(2,1)}, bf16[4,4,128,256]{2,3,0,1:T(8,128)(2,1)}) fusion(bf16[4,8,128,256]{2,3,0,1:T(8,128)(2,1)S(1)} %fusion), kind=kLoop, calls=%fused_computation.69 | loop fusion | bytes 4194304 | tf_op jit(solution)/shard_map/slice | solution.py:14
  52.5 4.9 %collective-permute-start.2 = (bf16[4,4,128,256]{2,3,0,1:T(8,128)(2,1)}, bf16[4,4,128,256]{2,3,0,1:T(8,128)(2,1)}, u32[]{:S(2)}, u32[]{:S(2)}) collective-permute-start(bf16[4,4,128,256]{2,3,0,1:T(8,128)(2,1)} %get-tuple-element.5), channel_id=1, source_target_pairs={{0,8},{8,16},{16,24},{24,32},{32,40},{40,48},{48,56},{56,64},{64,7... | collective-permute-start | bytes 3145736 | tf_op jit(solution)/shard_map/ppermute | solution.py:17
  57.4 1.9 %collective-permute-start.3 = (bf16[4,4,128,256]{2,3,0,1:T(8,128)(2,1)}, bf16[4,4,128,256]{2,3,0,1:T(8,128)(2,1)}, u32[]{:S(2)}, u32[]{:S(2)}) collective-permute-start(bf16[4,4,128,256]{2,3,0,1:T(8,128)(2,1)} %get-tuple-element.6), channel_id=1, source_target_pairs={{8,0},{16,8},{24,16},{32,24},{40,32},{48,40},{56,48},{64,56},{72,6... | collective-permute-start | bytes 3145736 | tf_op jit(solution)/shard_map/ppermute | solution.py:19
  59.4 0.0 copy-done.3
  59.4 0.1 copy.49
  59.5 0.0 copy-done.4
  59.5 0.0 copy-done.5
  59.5 0.1 iota_compare_fusion.1
  59.6 0.1 iota_add_fusion
  59.7 0.3 fusion.15
  59.9 0.1 copy.51
  60.1 20.4 %collective-permute-done.2 = bf16[4,4,128,256]{2,3,0,1:T(8,128)(2,1)} collective-permute-done((bf16[4,4,128,256]{2,3,0,1:T(8,128)(2,1)}, bf16[4,4,128,256]{2,3,0,1:T(8,128)(2,1)}, u32[]{:S(2)}, u32[]{:S(2)}) %collective-permute-start.2) | collective-permute-done | bytes 1048608 | tf_op jit(solution)/shard_map/ppermute | solution.py:17
  80.4 7.4 %collective-permute-done.3 = bf16[4,4,128,256]{2,3,0,1:T(8,128)(2,1)} collective-permute-done((bf16[4,4,128,256]{2,3,0,1:T(8,128)(2,1)}, bf16[4,4,128,256]{2,3,0,1:T(8,128)(2,1)}, u32[]{:S(2)}, u32[]{:S(2)}) %collective-permute-start.3) | collective-permute-done | bytes 1048608 | tf_op jit(solution)/shard_map/ppermute | solution.py:19
  87.9 3.4 %pad_maximum_fusion = bf16[4,16,128,256]{2,3,0,1:T(8,128)(2,1)} fusion(bf16[4,4,128,256]{2,3,0,1:T(8,128)(2,1)} %collective-permute-done.3, bf16[4,8,128,256]{2,3,0,1:T(8,128)(2,1)S(1)} %fusion, bf16[4,4,128,256]{2,3,0,1:T(8,128)(2,1)} %collective-permute-done.2), kind=kLoop, calls=%fused_computation | loop fusion | flops 4194304 | bytes 8388608 | tf_op jit(solution)/shard_map/concatenate | solution.py:15
  91.3 7.9 %copy.50 = bf16[4,16,128,256]{3,1,2,0:T(8,128)(2,1)} copy(bf16[4,16,128,256]{2,3,0,1:T(8,128)(2,1)} %pad_maximum_fusion) | data formatting | bytes 8388608 | tf_op jit(solution)/shard_map/concatenate | solution.py:15
  99.2 2.9 %fusion.44 = bf16[4,128,256,8]{2,3,1,0:T(8,128)(2,1)S(1)} fusion(bf16[4,16,128,256]{3,1,2,0:T(8,128)(2,1)} %copy.50, bf16[4,8,16,1]{2,1,3,0:T(8,128)(2,1)S(1)} %copy.51), kind=kOutput, calls=%fused_computation.71 | convolution fusion | flops 33554432 | bytes 6292480 | tf_op jit(solution)/shard_map/kle,kejc->ljkc/dot_general | solution.py:100
  102.1 0.0 copy-done
  102.1 1.6 %fusion.12 = bf16[8,128,256]{2,1,0:T(8,128)(2,1)} fusion(bf16[4,128,256,8]{2,3,1,0:T(8,128)(2,1)S(1)} %fusion.44, bf16[4,256,256]{2,1,0:T(8,128)(2,1)S(1)} %copy-done, bf16[8,128,256]{2,1,0:T(8,128)(2,1)S(1)} %copy-done.1), kind=kOutput, calls=%fused_computation.11 | convolution fusion | flops 537657344 | bytes 3670016 | tf_op jit(solution)/shard_map/dot_general | solution.py:105
  (9 shorter events, 0.1 us)
Async XLA Ops:
  0.0 102.1 %copy-start = (bf16[4,256,256]{2,1,0:T(8,128)(2,1)S(1)}, bf16[4,256,256]{2,1,0:T(8,128)(2,1)}, u32[]{:S(2)}) copy-start(bf16[4,256,256]{2,1,0:T(8,128)(2,1)} %param.13) | copy-start | bytes 1572868
  0.9 21.6 %collective-permute-start = (bf16[8,4,256]{2,1,0:T(4,128)(2,1)S(1)}, bf16[8,4,256]{2,1,0:T(4,128)(2,1)S(1)}, u32[]{:S(2)}, u32[]{:S(2)}) collective-permute-start(bf16[8,4,256]{2,1,0:T(4,128)(2,1)S(1)} %get-tuple-element.16), channel_id=1, source_target_pairs={{0,4},{4,0},{1,5},{5,1},{2,6},{6,2},{3,7},{7,3},{8,12},{12,8},{9,1... | collective-permute-start | bytes 49160 | tf_op jit(solution)/shard_map/ppermute | solution.py:17
  1.0 23.4 %collective-permute-start.1 = (bf16[8,4,256]{2,1,0:T(4,128)(2,1)S(1)}, bf16[8,4,256]{2,1,0:T(4,128)(2,1)S(1)}, u32[]{:S(2)}, u32[]{:S(2)}) collective-permute-start(bf16[8,4,256]{2,1,0:T(4,128)(2,1)S(1)} %get-tuple-element.17), channel_id=1, source_target_pairs={{4,0},{0,4},{5,1},{1,5},{6,2},{2,6},{7,3},{3,7},{12,8},{8,12},{13,... | collective-permute-start | bytes 49160 | tf_op jit(solution)/shard_map/ppermute | solution.py:19
  7.7 1.4 %slice-start = ((bf16[4,4,49024]{2,1,0:T(4,128)(2,1)}), bf16[4,4,48896]{2,1,0:T(4,128)(2,1)S(1)}, s32[]{:S(2)}) async-start(bf16[4,4,49024]{2,1,0:T(4,128)(2,1)} %tile.10), calls=%async_computation | async-start | bytes 3129344 | tf_op jit(solution)/shard_map/slice | solution.py:35
  9.1 11.3 %copy-start.2 = (f32[256,4,9]{0,1,2:T(4,128)S(1)}, f32[256,4,9]{0,1,2:T(4,128)}, u32[]{:S(2)}) copy-start(f32[256,4,9]{0,1,2:T(4,128)} %param.8) | copy-start | bytes 110596
  9.2 11.4 %copy-start.1 = (bf16[8,128,256]{2,1,0:T(8,128)(2,1)S(1)}, bf16[8,128,256]{2,1,0:T(8,128)(2,1)}, u32[]{:S(2)}) copy-start(bf16[8,128,256]{2,1,0:T(8,128)(2,1)} %param.7) | copy-start | bytes 1572868
  51.0 8.4 %copy-start.3 = (bf16[8,4,6]{0,1,2:T(4,128)(2,1)S(1)}, bf16[8,4,6]{0,1,2:T(4,128)(2,1)}, u32[]{:S(2)}) copy-start(bf16[8,4,6]{0,1,2:T(4,128)(2,1)} %param.9) | copy-start | bytes 1156
  51.0 8.5 %copy-start.4 = (s32[8]{0:T(128)S(1)}, s32[8]{0:T(128)}, u32[]{:S(2)}) copy-start(s32[8]{0:T(128)} %param.11) | copy-start | bytes 100
  51.0 8.5 %copy-start.5 = (s32[8]{0:T(128)S(1)}, s32[8]{0:T(128)}, u32[]{:S(2)}) copy-start(s32[8]{0:T(128)} %param.12) | copy-start | bytes 100
  52.5 28.0 %collective-permute-start.2 = (bf16[4,4,128,256]{2,3,0,1:T(8,128)(2,1)}, bf16[4,4,128,256]{2,3,0,1:T(8,128)(2,1)}, u32[]{:S(2)}, u32[]{:S(2)}) collective-permute-start(bf16[4,4,128,256]{2,3,0,1:T(8,128)(2,1)} %get-tuple-element.5), channel_id=1, source_target_pairs={{0,8},{8,16},{16,24},{24,32},{32,40},{40,48},{48,56},{56,64},{64,7... | collective-permute-start | bytes 3145736 | tf_op jit(solution)/shard_map/ppermute | solution.py:17
  57.4 30.5 %collective-permute-start.3 = (bf16[4,4,128,256]{2,3,0,1:T(8,128)(2,1)}, bf16[4,4,128,256]{2,3,0,1:T(8,128)(2,1)}, u32[]{:S(2)}, u32[]{:S(2)}) collective-permute-start(bf16[4,4,128,256]{2,3,0,1:T(8,128)(2,1)} %get-tuple-element.6), channel_id=1, source_target_pairs={{8,0},{16,8},{24,16},{32,24},{40,32},{48,40},{56,48},{64,56},{72,6... | collective-permute-start | bytes 3145736 | tf_op jit(solution)/shard_map/ppermute | solution.py:19
where the time goes:
time: 104 us
  local copies, waits for them, and re-layouts  44.6 us (43%)
  waiting for transfers between devices  27.8 us (27%)
  other arithmetic  14.1 us (14%)
  starting transfers between devices  7.45 us (7%)
  matrix products  7.4 us (7%)
  blocking collectives  2.18 us (2%)
    ppermute x2, waiting for transfers between devices, extended_2(): lax.ppermute(tail, axis, [(i, (i + 1) % count) for i in range(ends)])  20.4 us
    convert_element_type x8, local copies, waits for them, and re-layouts, shards(): accum = accum + tap_now[:, :, None, None] * padded[None, :, offset:offset...  18.1 us
    concatenate x2, local copies, waits for them, and re-layouts, extended_2(): jnp.concatenate([lax.ppermute(tail, axis, [(i, (i + 1) % count) for i in...  7.95 us
    ppermute x2, waiting for transfers between devices, extended_2(): lax.ppermute(head, axis, [((i + 1) % count, i) for i in range(ends)])  7.44 us
    select_n x1, other arithmetic, shards(): filtered = jnp.where(is_polar[None, :, None, None], placed, near_rows)  6.33 us
    ppermute x2, starting transfers between devices, extended_2(): lax.ppermute(tail, axis, [(i, (i + 1) % count) for i in range(ends)])  5.03 us
    reshape x1, local copies, waits for them, and re-layouts, toeplitz(): shaped = cut.reshape(lead + (out_count, window_len - 1))  4.41 us
    another operation x2, local copies, waits for them, and re-layouts, toeplitz(): tiled = jnp.tile(rolled, (1,) * len(lead) + (out_count,))  4.11 us
  transfers between devices with their start and end apart: 4, of which 2 were waited for; matrix products, arithmetic and copies ran while one was open for 19% of the time, Pallas kernels for 0%

commit v1 on v0

--- a/solution.py
+++ b/solution.py
@@ -54,21 +54,20 @@
     cycle_len = lon_count * col_count
     lat_pos = lax.axis_index("lat")
     lon_pos = lax.axis_index("lon")
-    leading = 0
-    source_rows = fields.shape[0]
+    ext_rows = row_count + 2 * HALO
     padded = extended_2(fields, (("lon", 1),), reach_cells, True)
+    ext = extended_2(padded, (("lat", 0),), HALO, False)
     taps_padded = jnp.pad(lon_taps, ((HALO, HALO), (0, 0), (0, 0)))
-    taps_here = lax.dynamic_slice_in_dim(
-        taps_padded, lat_pos * row_count + HALO - leading, source_rows, 0
-    )
-    accum = jnp.zeros((basis_count, source_rows, col_count, chan_count), jnp.float32)
+    taps_here = lax.dynamic_slice_in_dim(taps_padded, lat_pos * row_count, ext_rows, 0)
+    accum = jnp.zeros((basis_count, ext_rows, col_count, chan_count), jnp.float32)
     for offset in range(2 * reach_cells + 1):
         tap_now = jnp.transpose(taps_here[:, :, offset])
-        accum = accum + tap_now[:, :, None, None] * padded[
+        accum = accum + tap_now[:, :, None, None] * ext[
             None, :, offset : offset + col_count, :
         ].astype(jnp.float32)
-    near_rows = accum.astype(jnp.bfloat16)
+    filtered = accum.astype(jnp.bfloat16)
     at_top = lat_pos == 0
+    at_bottom = lat_pos == lat_count - 1
     slot_start = jnp.where(at_top, 0, row_count - polar_rows).astype(jnp.int32)
     slot_rows = lax.dynamic_slice_in_dim(fields, slot_start, polar_rows, 0)
     col_start = lon_pos * col_count
@@ -78,14 +77,9 @@
         coef, col_start, col_count, cycle_len, lax.all_gather(slot_rows, "lon", axis=1, tiled=True)
     )
     polar_z = polar_sum.astype(jnp.bfloat16)
-    placed = lax.dynamic_update_slice_in_dim(
-        jnp.zeros_like(near_rows), polar_z, slot_start + leading, 1
-    )
-    global_rows = lat_pos * row_count - leading + jnp.arange(source_rows, dtype=jnp.int32)
-    is_polar = (global_rows < polar_rows) | (global_rows >= lat_count * row_count - polar_rows)
-    filtered = jnp.where(is_polar[None, :, None, None], placed, near_rows)
-    extended = extended_2(filtered, (("lat", 1),), HALO, False)
-    ext_rows = row_count + 2 * HALO
+    current = lax.dynamic_slice_in_dim(filtered, slot_start + HALO, polar_rows, 1)
+    polar_here = jnp.where(at_top | at_bottom, polar_z, current)
+    filtered = lax.dynamic_update_slice_in_dim(filtered, polar_here, slot_start + HALO, 1)
     base_row = lat_pos * row_count
     steps_band = jnp.arange(band_len, dtype=jnp.int32)
     target = band_start[:, None] - base_row + HALO + steps_band[None, :]
@@ -98,13 +92,9 @@
         jnp.bfloat16
     )
     hidden = jnp.einsum(
-        "kle,kejc->ljkc", band_matrix, extended, preferred_element_type=jnp.float32
+        "kle,kejc->kljc", band_matrix, filtered, preferred_element_type=jnp.float32
     ).astype(jnp.bfloat16)
-    flat_hidden = hidden.reshape(row_count * col_count, basis_count * chan_count)
-    flat_mix = mixing.reshape(basis_count * chan_count, chan_count)
-    mixed = jnp.dot(flat_hidden, flat_mix, preferred_element_type=jnp.float32).reshape(
-        row_count, col_count, chan_count
-    )
+    mixed = jnp.einsum("kljc,kco->ljo", hidden, mixing, preferred_element_type=jnp.float32)
     return (fields.astype(jnp.float32) + mixed).astype(jnp.bfloat16)
 
 

time: 104 us -> 43.2 us (0.42)
  the two profiles are of different devices: /device:TPU:118 before, /device:TPU:145 now
where the time goes in v1:
time: 43.2 us; the launch traced here: 42.9 us
  local copies, waits for them, and re-layouts  14.5 us (34%)
  other arithmetic  11.3 us (26%)
  starting transfers between devices  9.45 us (22%)
  matrix products  4.73 us (11%)
  blocking collectives  2.78 us (6%)
    convert_element_type x1, other arithmetic, shards(): filtered = accum.astype(jnp.bfloat16)  6.03 us
    ppermute x2, starting transfers between devices, extended_2(): lax.ppermute(head, axis, [((i + 1) % count, i) for i in range(ends)])  5.59 us
    reshape x1, local copies, waits for them, and re-layouts, toeplitz(): shaped = cut.reshape(lead + (out_count, window_len - 1))  4.44 us
    another operation x2, local copies, waits for them, and re-layouts, toeplitz(): tiled = jnp.tile(rolled, (1,) * len(lead) + (out_count,))  4.13 us
    ppermute x2, starting transfers between devices, extended_2(): lax.ppermute(tail, axis, [(i, (i + 1) % count) for i in range(ends)])  3.86 us
    all_gather x1, blocking collectives, shards(): lax.all_gather(slot_rows, 'lon', axis=1, tiled=True)  2.78 us
    dot_general x1, matrix products, shards(): jnp.einsum('kle,kejc->kljc', band_matrix, filtered, preferred_element_typ...  2.38 us
    convert_element_type x1, other arithmetic, shards(): accum = accum + tap_now[:, :, None, None] * ext[None, :, offset:offset +...  2.3 us
  transfers between devices with their start and end apart: 4, of which 0 were waited for; matrix products, arithmetic and copies ran while one was open for 31% of the time, Pallas kernels for 0%

profile of v1, /device:TPU:145, one launch (start us, length us, event | category | flops | bytes accessed | tf_op | source)
XLA Modules:
  0.0 42.9 jit_solution(14044471257622411911)
XLA Ops:
  0.0 0.0 copy-start
  0.0 0.8 %fusion.30 = (bf16[8,4,256]{2,1,0:T(4,128)(2,1)S(1)}, bf16[8,4,256]{2,1,0:T(4,128)(2,1)S(1)}) fusion(bf16[8,128,256]{2,1,0:T(8,128)(2,1)} %param.7), kind=kLoop, calls=%fused_computation.63 | loop fusion | bytes 65536 | tf_op jit(solution)/shard_map/slice | solution.py:14
  0.9 0.8 %collective-permute-start = (bf16[8,4,256]{2,1,0:T(4,128)(2,1)S(1)}, bf16[8,4,256]{2,1,0:T(4,128)(2,1)S(1)}, u32[]{:S(2)}, u32[]{:S(2)}) collective-permute-start(bf16[8,4,256]{2,1,0:T(4,128)(2,1)S(1)} %get-tuple-element.16), channel_id=1, source_target_pairs={{0,4},{4,0},{1,5},{5,1},{2,6},{6,2},{3,7},{7,3},{8,12},{12,8},{9,1... | collective-permute-start | bytes 49160 | tf_op jit(solution)/shard_map/ppermute | solution.py:17
  1.6 0.1 collective-permute-start.1
  1.7 0.7 %subtract_add_fusion = s32[8]{0:T(128)S(1)} fusion(s32[8]{0:T(128)} %param.11, s32[]{:T(128)S(6)} %mul.58), kind=kLoop, calls=%fused_computation.61 | loop fusion | flops 16 | bytes 68 | tf_op jit(solution)/shard_map/add | solution.py:85
  2.4 0.1 iota_add_fusion
  2.5 0.8 %copy.8 = bf16[8,4,6]{2,1,0:T(4,128)(2,1)S(1)} copy(bf16[8,4,6]{0,1,2:T(4,128)(2,1)} %param.9) | data formatting | bytes 768 | tf_op args[2]
  3.3 0.7 %iota_compare_fusion.1 = pred[8,6]{1,0:T(8,128)(4,1)S(1)} fusion(s32[8]{0:T(128)} %param.12), kind=kLoop, calls=%fused_computation.50 | loop fusion | flops 48 | bytes 80 | tf_op jit(solution)/shard_map/lt | solution.py:86
  4.0 0.7 %constant_dynamic-slice_fusion = bf16[4,4,256]{2,1,0:T(4,128)(2,1)S(1)} fusion(bf16[4,8,256]{2,1,0:T(8,128)(2,1)} %param.10, s32[]{:T(128)S(6)} %select_n.34), kind=kLoop, calls=%fused_computation.48 | loop fusion | bytes 16388 | tf_op jit(solution)/shard_map/dynamic_slice | solution.py:75
  4.7 0.3 fusion.9
  5.0 0.9 %fusion.20 = (f32[4,16]{1,0:T(4,128)S(1)}, f32[4,16]{1,0:T(4,128)S(1)}, f32[4,16]{1,0:T(4,128)S(1)}, f32[4,16]{1,0:T(4,128)S(1)}, f32[4,16]{1,0:T(4,128)S(1)}, /...) fusion(s32[]{:T(128)S(6)} %select_n.32, f32[256,4,9]{0,1,2:T(4,128)} %param.8, ...), kind=kLoop, calls=%fused_computation.52 | loop fusion | bytes 39204 | tf_op jit(solution)/shard_map/transpose | solution.py:64
  5.9 0.1 fusion.19
  6.0 0.2 slice.109
  6.2 0.1 slice.111
  6.3 0.0 collective-permute-done
  6.3 0.0 collective-permute-done.1
  6.4 1.2 %pad_maximum_fusion.1 = bf16[8,136,256]{2,1,0:T(8,128)(2,1)S(1)} fusion(bf16[8,4,256]{2,1,0:T(4,128)(2,1)S(1)} %collective-permute-done.1, bf16[8,128,256]{2,1,0:T(8,128)(2,1)} %param.7, bf16[8,4,256]{2,1,0:T(4,128)(2,1)S(1)} %collective-permute-done), kind=kLoop, calls=%fused_computation.25 | loop fusion | flops 1671168 | bytes 1114112 | tf_op jit(solution)/shard_map/concatenate | solution.py:15
  7.6 0.7 %fusion.29 = (bf16[4,136,256]{2,1,0:T(8,128)(2,1)}, bf16[4,136,256]{2,1,0:T(8,128)(2,1)S(1)}) fusion(bf16[8,136,256]{2,1,0:T(8,128)(2,1)S(1)} %pad_maximum_fusion.1), kind=kLoop, calls=%fused_computation.62 | loop fusion | bytes 1114112 | tf_op jit(solution)/shard_map/slice | solution.py:14
  8.3 3.1 %collective-permute-start.2 = (bf16[4,136,256]{2,1,0:T(8,128)(2,1)}, bf16[4,136,256]{2,1,0:T(8,128)(2,1)S(1)}, u32[]{:S(2)}, u32[]{:S(2)}) collective-permute-start(bf16[4,136,256]{2,1,0:T(8,128)(2,1)} %get-tuple-element.14), channel_id=1, source_target_pairs={{0,8},{8,16},{16,24},{24,32},{32,40},{40,48},{48,56},{56,64},{64,7... | collective-permute-start | bytes 835592 | tf_op jit(solution)/shard_map/ppermute | solution.py:17
  11.4 5.5 %collective-permute-start.3 = (bf16[4,136,256]{2,1,0:T(8,128)(2,1)S(1)}, bf16[4,136,256]{2,1,0:T(8,128)(2,1)S(1)}, u32[]{:S(2)}, u32[]{:S(2)}) collective-permute-start(bf16[4,136,256]{2,1,0:T(8,128)(2,1)S(1)} %get-tuple-element.15), channel_id=1, source_target_pairs={{8,0},{16,8},{24,16},{32,24},{40,32},{48,40},{56,48},{64,56},{72,6... | collective-permute-start | bytes 835592 | tf_op jit(solution)/shard_map/ppermute | solution.py:19
  16.9 0.1 tile.4
  17.1 4.0 %tile.10 = bf16[4,4,49024]{2,1,0:T(4,128)(2,1)} reshape(bf16[4,4,128,383]{3,2,1,0:T(8,128)(2,1)S(1)} %tile.4) | data formatting | bytes 3137536 | tf_op jit(solution)/shard_map/tile | solution.py:34
  21.1 0.0 slice-start
  21.1 1.4 %slice-done = bf16[4,4,48896]{2,1,0:T(4,128)(2,1)S(1)} async-done(((bf16[4,4,49024]{2,1,0:T(4,128)(2,1)}), bf16[4,4,48896]{2,1,0:T(4,128)(2,1)S(1)}, s32[]{:S(2)}) %slice-start) | async-done | bytes 1564696 | tf_op jit(solution)/shard_map/slice | solution.py:35
  22.5 0.0 copy-start.1
  22.5 4.4 %reshape.78 = bf16[4,4,128,382]{3,2,1,0:T(8,128)(2,1)} reshape(bf16[4,4,48896]{2,1,0:T(4,128)(2,1)S(1)} %slice-done) | data formatting | bytes 3129344 | tf_op jit(solution)/shard_map/reshape | solution.py:36
  26.9 0.1 copy.9
  27.0 0.0 copy-done.1
  27.1 2.8 %all_gather.3 = bf16[4,256,256]{2,1,0:T(8,128)(2,1)S(1)} all-gather(bf16[4,128,256]{2,1,0:T(8,128)(2,1)S(1)} %constant_dynamic-slice_fusion.1), channel_id=1, replica_groups=mesh['lat'=32,'lon'=2,'ens'=4] {'lon'}, dimensions={1}, use_global_device_ids=true | all-gather | bytes 786432 | tf_op jit(solution)/shard_map/all_gather | solution.py:77
  29.8 0.0 collective-permute-done.2
  29.9 0.0 collective-permute-done.3
  29.9 0.2 pad_maximum_fusion
  30.0 2.3 %slice_convert_fusion.8 = (f32[16,128,256]{2,1,0:T(8,128)S(1)}, f32[16,128,256]{2,1,0:T(8,128)S(1)}, f32[16,128,256]{2,1,0:T(8,128)S(1)}, f32[16,128,256]{2,1,0:...) fusion(bf16[16,136,256]{2,1,0:T(8,128)(2,1)S(1)} %pad_maximum_f, ...), kind=kLoop, calls=%fused_computation.24 | loop fusion | flops 4718592 | bytes 28311552 | tf_op jit(solution)/shard_map/convert_element_type | solution.py:67
  32.3 0.0 copy-start.2
  32.3 6.0 %add_convert_fusion = bf16[4,16,128,256]{3,2,1,0:T(8,128)(2,1)S(1)} fusion(f32[16,128,256]{2,1,0:T(8,128)S(1)} %get-tuple-element.6, f32[4,16]{1,0:T(4,128)S(1)} %get-tuple-element.26, f32[16,128,256]{2,1,0:T(8,128)S(1)} %get-tuple-element.7, f32[4,16]{1,0:T(4,128)S(1)} %get-tuple-element.19, f32[16,128,256]{2,1,0:T(8,128)S(1)} %get-tuple-element.8, ...), kind=kLoop, calls=%fused_computation | loop fusion | flops 37748736 | bytes 23070976 | tf_op jit(solution)/shard_map/convert_element_type | solution.py:68
  38.4 0.0 copy-done.2
  38.4 0.5 %fusion.6 = bf16[4,16,128,256]{3,2,1,0:T(8,128)(2,1)S(1)} fusion(bf16[4,16,128,256]{3,2,1,0:T(8,128)(2,1)S(1)} %add_convert_fusion, s32[]{:T(128)S(6)} %select_n.37, bf16[4,4,128,382]{3,2,1,0:T(8,128)(2,1)S(1)} %copy-done.2, pred[]{:T(512)S(6)} %or.3, bf16[4,256,256]{2,1,0:T(8,128)(2,1)S(1)} %all_gather.3), kind=kOutput, calls=%fused_computation.9 | convolution fusion | flops 269484032 | bytes 3670021 | tf_op jit(solution)/shard_map/kpjm,pmc->kpjc/dot_general | solution.py:43
  38.9 2.4 %fusion = bf16[4,8,128,256]{3,1,2,0:T(8,128)(2,1)S(1)} fusion(bf16[4,8,16,1]{2,1,3,0:T(8,128)(2,1)S(1)} %copy.9, bf16[4,16,128,256]{3,2,1,0:T(8,128)(2,1)S(1)} %fusion.6), kind=kOutput, calls=%fused_computation.2 | convolution fusion | flops 33554432 | bytes 6292480 | tf_op jit(solution)/shard_map/kle,kejc->kljc/dot_general | solution.py:94
  41.3 0.0 copy-done
  41.3 1.6 %fusion.8 = bf16[8,128,256]{2,1,0:T(8,128)(2,1)} fusion(bf16[4,8,128,256]{3,1,2,0:T(8,128)(2,1)S(1)} %fusion, bf16[8,128,256]{2,1,0:T(8,128)(2,1)S(1)} %copy-done.1, bf16[4,256,256]{2,1,0:T(8,128)(2,1)S(1)} %copy-done), kind=kOutput, calls=%fused_computation.11 | convolution fusion | flops 537657344 | bytes 3670016 | tf_op jit(solution)/shard_map/kljc,kco->ljo/dot_general | solution.py:97
  (4 shorter events, 0.0 us)
Async XLA Ops:
  0.0 41.3 %copy-start = (bf16[4,256,256]{2,1,0:T(8,128)(2,1)S(1)}, bf16[4,256,256]{2,1,0:T(8,128)(2,1)}, u32[]{:S(2)}) copy-start(bf16[4,256,256]{2,1,0:T(8,128)(2,1)} %param.13) | copy-start | bytes 1572868
  0.9 5.5 %collective-permute-start = (bf16[8,4,256]{2,1,0:T(4,128)(2,1)S(1)}, bf16[8,4,256]{2,1,0:T(4,128)(2,1)S(1)}, u32[]{:S(2)}, u32[]{:S(2)}) collective-permute-start(bf16[8,4,256]{2,1,0:T(4,128)(2,1)S(1)} %get-tuple-element.16), channel_id=1, source_target_pairs={{0,4},{4,0},{1,5},{5,1},{2,6},{6,2},{3,7},{7,3},{8,12},{12,8},{9,1... | collective-permute-start | bytes 49160 | tf_op jit(solution)/shard_map/ppermute | solution.py:17
  1.6 4.7 %collective-permute-start.1 = (bf16[8,4,256]{2,1,0:T(4,128)(2,1)S(1)}, bf16[8,4,256]{2,1,0:T(4,128)(2,1)S(1)}, u32[]{:S(2)}, u32[]{:S(2)}) collective-permute-start(bf16[8,4,256]{2,1,0:T(4,128)(2,1)S(1)} %get-tuple-element.17), channel_id=1, source_target_pairs={{4,0},{0,4},{5,1},{1,5},{6,2},{2,6},{7,3},{3,7},{12,8},{8,12},{13,... | collective-permute-start | bytes 49160 | tf_op jit(solution)/shard_map/ppermute | solution.py:19
  8.3 21.6 %collective-permute-start.2 = (bf16[4,136,256]{2,1,0:T(8,128)(2,1)}, bf16[4,136,256]{2,1,0:T(8,128)(2,1)S(1)}, u32[]{:S(2)}, u32[]{:S(2)}) collective-permute-start(bf16[4,136,256]{2,1,0:T(8,128)(2,1)} %get-tuple-element.14), channel_id=1, source_target_pairs={{0,8},{8,16},{16,24},{24,32},{32,40},{40,48},{48,56},{56,64},{64,7... | collective-permute-start | bytes 835592 | tf_op jit(solution)/shard_map/ppermute | solution.py:17
  11.4 18.4 %collective-permute-start.3 = (bf16[4,136,256]{2,1,0:T(8,128)(2,1)S(1)}, bf16[4,136,256]{2,1,0:T(8,128)(2,1)S(1)}, u32[]{:S(2)}, u32[]{:S(2)}) collective-permute-start(bf16[4,136,256]{2,1,0:T(8,128)(2,1)S(1)} %get-tuple-element.15), channel_id=1, source_target_pairs={{8,0},{16,8},{24,16},{32,24},{40,32},{48,40},{56,48},{64,56},{72,6... | collective-permute-start | bytes 835592 | tf_op jit(solution)/shard_map/ppermute | solution.py:19
  21.1 1.4 %slice-start = ((bf16[4,4,49024]{2,1,0:T(4,128)(2,1)}), bf16[4,4,48896]{2,1,0:T(4,128)(2,1)S(1)}, s32[]{:S(2)}) async-start(bf16[4,4,49024]{2,1,0:T(4,128)(2,1)} %tile.10), calls=%async_computation | async-start | bytes 3129344 | tf_op jit(solution)/shard_map/slice | solution.py:35
  22.5 4.6 %copy-start.1 = (bf16[8,128,256]{2,1,0:T(8,128)(2,1)S(1)}, bf16[8,128,256]{2,1,0:T(8,128)(2,1)}, u32[]{:S(2)}) copy-start(bf16[8,128,256]{2,1,0:T(8,128)(2,1)} %param.7) | copy-start | bytes 1572868
  32.3 6.1 %copy-start.2 = (bf16[4,4,128,382]{3,2,1,0:T(8,128)(2,1)S(1)}, bf16[4,4,128,382]{3,2,1,0:T(8,128)(2,1)}, u32[]{:S(2)}) copy-start(bf16[4,4,128,382]{3,2,1,0:T(8,128)(2,1)} %reshape.78) | copy-start | bytes 4694020

commit v2 on v1

--- a/solution.py
+++ b/solution.py
@@ -73,9 +73,10 @@
     col_start = lon_pos * col_count
     coef_start = jnp.where(at_top, 0, polar_rows).astype(jnp.int32)
     coef = lax.dynamic_slice_in_dim(cycle_taps, coef_start, polar_rows, 1)
-    polar_sum = cycle_fold(
-        coef, col_start, col_count, cycle_len, lax.all_gather(slot_rows, "lon", axis=1, tiled=True)
-    )
+    other_rows = lax.ppermute(slot_rows, "lon", [(i, (i + 1) % lon_count) for i in range(lon_count)])
+    pair = [slot_rows, other_rows] if lon_count == 2 else None
+    gathered = jnp.where(lon_pos == 0, jnp.concatenate(pair, axis=1), jnp.concatenate(pair[::-1], axis=1))
+    polar_sum = cycle_fold(coef, col_start, col_count, cycle_len, gathered)
     polar_z = polar_sum.astype(jnp.bfloat16)
     current = lax.dynamic_slice_in_dim(filtered, slot_start + HALO, polar_rows, 1)
     polar_here = jnp.where(at_top | at_bottom, polar_z, current)

time: 43.2 us -> 42.3 us (0.979)
  blocking collectives: 2.78 us -> 0 us
  matrix products: 4.73 us -> 5.96 us
    all_gather x1 -> x0, blocking collectives: 2.78 us -> none  [shards(): lax.all_gather(slot_rows, 'lon', axis=1, tiled=True)]
    dynamic_slice x1, local copies, waits for them, and re-layouts: 0.03 us -> 1.68 us  [shards(): slot_rows = lax.dynamic_slice_in_dim(fields, slot_start, polar_rows, 0)]
    dot_general x1, matrix products: 0.5 us -> 1.73 us  [cycle_fold(): jnp.einsum('kpjm,pmc->kpjc', circ, block_in, preferred_element_type=jnp.f...]
    transpose x1, local copies, waits for them, and re-layouts: 0.9 us -> 0.12 us  [shards(): tap_now = jnp.transpose(taps_here[:, :, offset])]
    unnamed x7 -> x11, local copies, waits for them, and re-layouts: 0.82 us -> 0.14 us
  transfers between devices with their start and end apart: 4 -> 5, of which waited for: 0 -> 0; matrix products, arithmetic and copies ran while one was open for 31% -> 57% of each run, Pallas kernels for 0% -> 0%
where the time goes in v2:
time: 42.3 us; the launch traced here: 41.9 us
  local copies, waits for them, and re-layouts  14.7 us (35%)
  other arithmetic  11.3 us (27%)
  starting transfers between devices  9.88 us (23%)
  matrix products  5.96 us (14%)
    convert_element_type x1, other arithmetic, shards(): filtered = accum.astype(jnp.bfloat16)  6.03 us
    ppermute x2, starting transfers between devices, extended_2(): lax.ppermute(head, axis, [((i + 1) % count, i) for i in range(ends)])  5.58 us
    reshape x1, local copies, waits for them, and re-layouts, toeplitz(): shaped = cut.reshape(lead + (out_count, window_len - 1))  4.43 us
    another operation x2, local copies, waits for them, and re-layouts, toeplitz(): tiled = jnp.tile(rolled, (1,) * len(lead) + (out_count,))  4.13 us
    ppermute x2, starting transfers between devices, extended_2(): lax.ppermute(tail, axis, [(i, (i + 1) % count) for i in range(ends)])  3.89 us
    dot_general x1, matrix products, shards(): jnp.einsum('kle,kejc->kljc', band_matrix, filtered, preferred_element_typ...  2.38 us
    convert_element_type x1, other arithmetic, shards(): accum = accum + tap_now[:, :, None, None] * ext[None, :, offset:offset +...  2.3 us
    dot_general x1, matrix products, cycle_fold(): jnp.einsum('kpjm,pmc->kpjc', circ, block_in, preferred_element_type=jnp.f...  1.73 us
  transfers between devices with their start and end apart: 5, of which 0 were waited for; matrix products, arithmetic and copies ran while one was open for 57% of the time, Pallas kernels for 0%

profile of v2, /device:TPU:145, one launch (start us, length us, event | category | flops | bytes accessed | tf_op | source)
XLA Modules:
  0.0 41.9 jit_solution(9221430991499212165)
XLA Ops:
  0.0 0.0 copy-start
  0.0 0.8 %fusion.38 = (bf16[8,4,256]{2,1,0:T(4,128)(2,1)S(1)}, bf16[8,4,256]{2,1,0:T(4,128)(2,1)S(1)}) fusion(bf16[8,128,256]{2,1,0:T(8,128)(2,1)} %param.7), kind=kLoop, calls=%fused_computation.71 | loop fusion | bytes 65536 | tf_op jit(solution)/shard_map/slice | solution.py:14
  0.9 0.8 %collective-permute-start = (bf16[8,4,256]{2,1,0:T(4,128)(2,1)S(1)}, bf16[8,4,256]{2,1,0:T(4,128)(2,1)S(1)}, u32[]{:S(2)}, u32[]{:S(2)}) collective-permute-start(bf16[8,4,256]{2,1,0:T(4,128)(2,1)S(1)} %get-tuple-element.16), channel_id=1, source_target_pairs={{0,4},{4,0},{1,5},{5,1},{2,6},{6,2},{3,7},{7,3},{8,12},{12,8},{9,1... | collective-permute-start | bytes 49160 | tf_op jit(solution)/shard_map/ppermute | solution.py:17
  1.6 0.1 collective-permute-start.1
  1.7 1.7 %constant_dynamic-slice_fusion.1 = bf16[4,128,256]{2,1,0:T(8,128)(2,1)} fusion(bf16[8,128,256]{2,1,0:T(8,128)(2,1)} %param.7, s32[]{:T(128)S(6)} %select_n.43), kind=kLoop, calls=%fused_computation.56 | loop fusion | bytes 524292 | tf_op jit(solution)/shard_map/dynamic_slice | solution.py:72
  3.4 0.4 collective-permute-start.4
  3.8 0.7 %constant_dynamic-slice_fusion = bf16[4,4,256]{2,1,0:T(4,128)(2,1)S(1)} fusion(bf16[4,8,256]{2,1,0:T(8,128)(2,1)} %param.10, s32[]{:T(128)S(6)} %select_n.43), kind=kLoop, calls=%fused_computation.55 | loop fusion | bytes 16388 | tf_op jit(solution)/shard_map/dynamic_slice | solution.py:75
  4.5 0.7 %subtract_add_fusion = s32[8]{0:T(128)S(1)} fusion(s32[8]{0:T(128)} %param.11, s32[]{:T(128)S(6)} %mul.58), kind=kLoop, calls=%fused_computation.68 | loop fusion | flops 16 | bytes 68 | tf_op jit(solution)/shard_map/add | solution.py:86
  5.2 0.1 iota_add_fusion
  5.3 0.7 %iota_compare_fusion.1 = pred[8,6]{1,0:T(8,128)(4,1)S(1)} fusion(s32[8]{0:T(128)} %param.12), kind=kLoop, calls=%fused_computation.57 | loop fusion | flops 48 | bytes 80 | tf_op jit(solution)/shard_map/lt | solution.py:87
  6.0 0.1 fusion.26
  6.1 0.2 slice.109
  6.3 0.1 slice.111
  6.4 0.0 collective-permute-done
  6.4 0.0 collective-permute-done.1
  6.5 1.2 %pad_maximum_fusion.1 = bf16[8,136,256]{2,1,0:T(8,128)(2,1)S(1)} fusion(bf16[8,4,256]{2,1,0:T(4,128)(2,1)S(1)} %collective-permute-done.1, bf16[8,128,256]{2,1,0:T(8,128)(2,1)} %param.7, bf16[8,4,256]{2,1,0:T(4,128)(2,1)S(1)} %collective-permute-done), kind=kLoop, calls=%fused_computation.25 | loop fusion | flops 1671168 | bytes 1114112 | tf_op jit(solution)/shard_map/concatenate | solution.py:15
  7.6 0.7 %fusion.37 = (bf16[4,136,256]{2,1,0:T(8,128)(2,1)}, bf16[4,136,256]{2,1,0:T(8,128)(2,1)S(1)}) fusion(bf16[8,136,256]{2,1,0:T(8,128)(2,1)S(1)} %pad_maximum_fusion.1), kind=kLoop, calls=%fused_computation.70 | loop fusion | bytes 1114112 | tf_op jit(solution)/shard_map/slice | solution.py:14
  8.4 3.1 %collective-permute-start.2 = (bf16[4,136,256]{2,1,0:T(8,128)(2,1)}, bf16[4,136,256]{2,1,0:T(8,128)(2,1)S(1)}, u32[]{:S(2)}, u32[]{:S(2)}) collective-permute-start(bf16[4,136,256]{2,1,0:T(8,128)(2,1)} %get-tuple-element.14), channel_id=1, source_target_pairs={{0,8},{8,16},{16,24},{24,32},{32,40},{40,48},{48,56},{56,64},{64,7... | collective-permute-start | bytes 835592 | tf_op jit(solution)/shard_map/ppermute | solution.py:17
  11.5 5.5 %collective-permute-start.3 = (bf16[4,136,256]{2,1,0:T(8,128)(2,1)S(1)}, bf16[4,136,256]{2,1,0:T(8,128)(2,1)S(1)}, u32[]{:S(2)}, u32[]{:S(2)}) collective-permute-start(bf16[4,136,256]{2,1,0:T(8,128)(2,1)S(1)} %get-tuple-element.15), channel_id=1, source_target_pairs={{8,0},{16,8},{24,16},{32,24},{40,32},{48,40},{56,48},{64,56},{72,6... | collective-permute-start | bytes 835592 | tf_op jit(solution)/shard_map/ppermute | solution.py:19
  17.0 0.1 tile.4
  17.2 4.0 %tile.10 = bf16[4,4,49024]{2,1,0:T(4,128)(2,1)} reshape(bf16[4,4,128,383]{3,2,1,0:T(8,128)(2,1)S(1)} %tile.4) | data formatting | bytes 3137536 | tf_op jit(solution)/shard_map/tile | solution.py:34
  21.2 0.0 slice-start
  21.2 1.4 %slice-done = bf16[4,4,48896]{2,1,0:T(4,128)(2,1)S(1)} async-done(((bf16[4,4,49024]{2,1,0:T(4,128)(2,1)}), bf16[4,4,48896]{2,1,0:T(4,128)(2,1)S(1)}, s32[]{:S(2)}) %slice-start) | async-done | bytes 1564696 | tf_op jit(solution)/shard_map/slice | solution.py:35
  22.6 0.0 copy-start.4
  22.6 0.0 copy-start.3
  22.6 0.0 copy-start.1
  22.6 4.4 %reshape.78 = bf16[4,4,128,382]{3,2,1,0:T(8,128)(2,1)} reshape(bf16[4,4,48896]{2,1,0:T(4,128)(2,1)S(1)} %slice-done) | data formatting | bytes 3129344 | tf_op jit(solution)/shard_map/reshape | solution.py:36
  27.0 0.0 copy-done.4
  27.0 0.1 copy.8
  27.1 0.3 fusion.9
  27.4 0.1 copy.9
  27.6 0.0 copy-done.3
  27.6 0.1 fusion.27
  27.7 0.0 collective-permute-done.2
  27.7 0.0 collective-permute-done.3
  27.7 0.0 copy-done.1
  27.7 0.2 pad_maximum_fusion
  27.9 2.3 %slice_convert_fusion.8 = (f32[16,128,256]{2,1,0:T(8,128)S(1)}, f32[16,128,256]{2,1,0:T(8,128)S(1)}, f32[16,128,256]{2,1,0:T(8,128)S(1)}, f32[16,128,256]{2,1,0:...) fusion(bf16[16,136,256]{2,1,0:T(8,128)(2,1)S(1)} %pad_maximum_f, ...), kind=kLoop, calls=%fused_computation.24 | loop fusion | flops 4718592 | bytes 28311552 | tf_op jit(solution)/shard_map/convert_element_type | solution.py:67
  30.2 0.0 copy-start.2
  30.2 6.0 %add_convert_fusion = bf16[4,16,128,256]{3,2,1,0:T(8,128)(2,1)S(1)} fusion(f32[16,128,256]{2,1,0:T(8,128)S(1)} %get-tuple-element.6, f32[4,16]{1,0:T(4,128)S(1)} %get-tuple-element.26, f32[16,128,256]{2,1,0:T(8,128)S(1)} %get-tuple-element.7, f32[4,16]{1,0:T(4,128)S(1)} %get-tuple-element.19, f32[16,128,256]{2,1,0:T(8,128)S(1)} %get-tuple-element.8, ...), kind=kLoop, calls=%fused_computation | loop fusion | flops 37748736 | bytes 23070976 | tf_op jit(solution)/shard_map/convert_element_type | solution.py:68
  36.2 0.0 collective-permute-done.4
  36.2 0.0 copy-done.2
  36.2 1.7 %fusion.6 = bf16[4,16,128,256]{3,2,1,0:T(8,128)(2,1)S(1)} fusion(bf16[4,16,128,256]{3,2,1,0:T(8,128)(2,1)S(1)} %add_convert_fusion, s32[]{:T(128)S(6)} %select_n.47, bf16[4,4,128,382]{3,2,1,0:T(8,128)(2,1)S(1)} %copy-done.2, pred[]{:T(512)S(6)} %or.3, bf16[4,128,256]{2,1,0:T(8,128)(2,1)} %collective-permute-done.4, ...), kind=kOutput, calls=%fused_computation.9 | convolution fusion | flops 271843328 | bytes 3670022 | tf_op jit(solution)/shard_map/kpjm,pmc->kpjc/dot_general | solution.py:43
  38.0 2.4 %fusion = bf16[4,8,128,256]{3,1,2,0:T(8,128)(2,1)S(1)} fusion(bf16[4,8,16,1]{2,1,3,0:T(8,128)(2,1)S(1)} %copy.9, bf16[4,16,128,256]{3,2,1,0:T(8,128)(2,1)S(1)} %fusion.6), kind=kOutput, calls=%fused_computation.2 | convolution fusion | flops 33554432 | bytes 6292480 | tf_op jit(solution)/shard_map/kle,kejc->kljc/dot_general | solution.py:95
  40.4 0.0 copy-done
  40.4 1.6 %fusion.8 = bf16[8,128,256]{2,1,0:T(8,128)(2,1)} fusion(bf16[4,8,128,256]{3,1,2,0:T(8,128)(2,1)S(1)} %fusion, bf16[8,128,256]{2,1,0:T(8,128)(2,1)S(1)} %copy-done.1, bf16[4,256,256]{2,1,0:T(8,128)(2,1)S(1)} %copy-done), kind=kOutput, calls=%fused_computation.11 | convolution fusion | flops 537657344 | bytes 3670016 | tf_op jit(solution)/shard_map/kljc,kco->ljo/dot_general | solution.py:98
  (3 shorter events, 0.0 us)
Async XLA Ops:
  0.0 40.4 %copy-start = (bf16[4,256,256]{2,1,0:T(8,128)(2,1)S(1)}, bf16[4,256,256]{2,1,0:T(8,128)(2,1)}, u32[]{:S(2)}) copy-start(bf16[4,256,256]{2,1,0:T(8,128)(2,1)} %param.13) | copy-start | bytes 1572868
  0.9 5.6 %collective-permute-start = (bf16[8,4,256]{2,1,0:T(4,128)(2,1)S(1)}, bf16[8,4,256]{2,1,0:T(4,128)(2,1)S(1)}, u32[]{:S(2)}, u32[]{:S(2)}) collective-permute-start(bf16[8,4,256]{2,1,0:T(4,128)(2,1)S(1)} %get-tuple-element.16), channel_id=1, source_target_pairs={{0,4},{4,0},{1,5},{5,1},{2,6},{6,2},{3,7},{7,3},{8,12},{12,8},{9,1... | collective-permute-start | bytes 49160 | tf_op jit(solution)/shard_map/ppermute | solution.py:17
  1.6 4.8 %collective-permute-start.1 = (bf16[8,4,256]{2,1,0:T(4,128)(2,1)S(1)}, bf16[8,4,256]{2,1,0:T(4,128)(2,1)S(1)}, u32[]{:S(2)}, u32[]{:S(2)}) collective-permute-start(bf16[8,4,256]{2,1,0:T(4,128)(2,1)S(1)} %get-tuple-element.17), channel_id=1, source_target_pairs={{4,0},{0,4},{5,1},{1,5},{6,2},{2,6},{7,3},{3,7},{12,8},{8,12},{13,... | collective-permute-start | bytes 49160 | tf_op jit(solution)/shard_map/ppermute | solution.py:19
  3.4 32.8 %collective-permute-start.4 = (bf16[4,128,256]{2,1,0:T(8,128)(2,1)}, bf16[4,128,256]{2,1,0:T(8,128)(2,1)}, u32[]{:S(2)}, u32[]{:S(2)}) collective-permute-start(bf16[4,128,256]{2,1,0:T(8,128)(2,1)} %constant_dynamic-slice_fusion.1), channel_id=1, source_target_pairs={{0,4},{4,0},{1,5},{5,1},{2,6},{6,2},{3,7},{7,3},{8,12},{12,8},{9,1... | collective-permute-start | bytes 786440 | tf_op jit(solution)/shard_map/ppermute | solution.py:76
  8.4 19.3 %collective-permute-start.2 = (bf16[4,136,256]{2,1,0:T(8,128)(2,1)}, bf16[4,136,256]{2,1,0:T(8,128)(2,1)S(1)}, u32[]{:S(2)}, u32[]{:S(2)}) collective-permute-start(bf16[4,136,256]{2,1,0:T(8,128)(2,1)} %get-tuple-element.14), channel_id=1, source_target_pairs={{0,8},{8,16},{16,24},{24,32},{32,40},{40,48},{48,56},{56,64},{64,7... | collective-permute-start | bytes 835592 | tf_op jit(solution)/shard_map/ppermute | solution.py:17
  11.5 16.2 %collective-permute-start.3 = (bf16[4,136,256]{2,1,0:T(8,128)(2,1)S(1)}, bf16[4,136,256]{2,1,0:T(8,128)(2,1)S(1)}, u32[]{:S(2)}, u32[]{:S(2)}) collective-permute-start(bf16[4,136,256]{2,1,0:T(8,128)(2,1)S(1)} %get-tuple-element.15), channel_id=1, source_target_pairs={{8,0},{16,8},{24,16},{32,24},{40,32},{48,40},{56,48},{64,56},{72,6... | collective-permute-start | bytes 835592 | tf_op jit(solution)/shard_map/ppermute | solution.py:19
  21.2 1.4 %slice-start = ((bf16[4,4,49024]{2,1,0:T(4,128)(2,1)}), bf16[4,4,48896]{2,1,0:T(4,128)(2,1)S(1)}, s32[]{:S(2)}) async-start(bf16[4,4,49024]{2,1,0:T(4,128)(2,1)} %tile.10), calls=%async_computation | async-start | bytes 3129344 | tf_op jit(solution)/shard_map/slice | solution.py:35
  22.6 4.4 %copy-start.4 = (bf16[8,4,6]{0,1,2:T(4,128)(2,1)S(1)}, bf16[8,4,6]{0,1,2:T(4,128)(2,1)}, u32[]{:S(2)}) copy-start(bf16[8,4,6]{0,1,2:T(4,128)(2,1)} %param.9) | copy-start | bytes 1156
  22.6 5.0 %copy-start.3 = (f32[256,4,9]{0,1,2:T(4,128)S(1)}, f32[256,4,9]{0,1,2:T(4,128)}, u32[]{:S(2)}) copy-start(f32[256,4,9]{0,1,2:T(4,128)} %param.8) | copy-start | bytes 110596
  22.6 5.1 %copy-start.1 = (bf16[8,128,256]{2,1,0:T(8,128)(2,1)S(1)}, bf16[8,128,256]{2,1,0:T(8,128)(2,1)}, u32[]{:S(2)}) copy-start(bf16[8,128,256]{2,1,0:T(8,128)(2,1)} %param.7) | copy-start | bytes 1572868
  30.2 6.1 %copy-start.2 = (bf16[4,4,128,382]{3,2,1,0:T(8,128)(2,1)S(1)}, bf16[4,4,128,382]{3,2,1,0:T(8,128)(2,1)}, u32[]{:S(2)}) copy-start(bf16[4,4,128,382]{3,2,1,0:T(8,128)(2,1)} %reshape.78) | copy-start | bytes 4694020

commit v3 on v1

v3 whole, which is shorter than its diff:
```python
import functools

import jax
import jax.numpy as jnp
from jax import lax
from jax.experimental import pallas as pl
from jax.experimental.pallas import tpu as pltpu
from jax.sharding import PartitionSpec as P

HALO = 4
LANES = 128


def extended_2(cells, sides, width, closed):
    for axis, dim in sides:
        count = lax.axis_size(axis)
        ends = count if closed else count - 1
        head = lax.slice_in_dim(cells, 0, width, axis=dim)
        tail = lax.slice_in_dim(cells, cells.shape[dim] - width, cells.shape[dim], axis=dim)
        cells = jnp.concatenate(
            [
                lax.ppermute(tail, axis, [(i, (i + 1) % count) for i in range(ends)]),
                cells,
                lax.ppermute(head, axis, [((i + 1) % count, i) for i in range(ends)]),
            ],
            axis=dim,
        )
    return cells


def banded(vec, rows, upper):
    rolled = pltpu.roll(jnp.broadcast_to(vec, (rows, LANES)), 0, 1, stride=1, stride_axis=0)
    row = lax.broadcasted_iota(jnp.int32, (rows, LANES), 0)
    col = lax.broadcasted_iota(jnp.int32, (rows, LANES), 1)
    keep = col >= row if upper else col < row
    return jnp.where(keep, rolled, 0.0)


def conv_kernel(basis, ext_rows, out_rows, band_len,
                ctl_ref, idx_ref, wgt_ref, ext_ref, tap_ref, fields_ref, mix_ref,
                polar_ref, crev_ref, out_ref, f_ref, h_ref):
    cols = out_ref.shape[1]
    chans = out_ref.shape[2]
    polar_count = polar_ref.shape[0]

    def filter_row(r, carry):
        x = ext_ref[r]
        parts = []
        for k in range(basis):
            for half in range(2):
                u = tap_ref[k, half, pl.ds(r, 1), :]
                left = banded(u, cols, True)
                right = banded(u, cols, False)
                parts.append(jnp.concatenate([left, right], axis=1).astype(jnp.bfloat16))
        tall = jnp.concatenate(parts, axis=0)
        y = jnp.dot(tall, x, preferred_element_type=jnp.float32)
        for k in range(basis):
            lo = 2 * k * cols
            v = y[lo : lo + cols] + y[lo + cols : lo + 2 * cols]
            f_ref[k, r] = v.astype(jnp.bfloat16).astype(jnp.float32)
        return carry

    lax.fori_loop(0, ext_rows, filter_row, 0)

    @pl.when(ctl_ref[0] == 1)
    def _polar():
        slot = ctl_ref[1]
        for k in range(basis):
            for p in range(polar_count):
                va = crev_ref[k, p, pl.ds(0, 1), :]
                vb = crev_ref[k, p, pl.ds(1, 1), :]
                ra_u, ra_w = banded(va, cols, True), banded(va, cols, False)
                rb_u, rb_w = banded(vb, cols, True), banded(vb, cols, False)
                circ = jnp.concatenate([ra_u + rb_w, rb_u + ra_w], axis=1).astype(jnp.bfloat16)
                y = jnp.dot(circ, polar_ref[p], preferred_element_type=jnp.float32)
                f_ref[k, slot + p] = y.astype(jnp.bfloat16).astype(jnp.float32)

    for k in range(basis):
        def band_row(i, carry):
            acc = jnp.zeros((cols, chans), jnp.float32)
            for t in range(band_len):
                r = idx_ref[i * band_len + t]
                w = wgt_ref[(k * out_rows + i) * band_len + t]
                acc = acc + w * f_ref[k, r]
            h_ref[i, :, k * chans : (k + 1) * chans] = acc.astype(jnp.bfloat16)
            return carry

        lax.fori_loop(0, out_rows, band_row, 0)

    def mix_row(i, carry):
        mixed = jnp.dot(h_ref[i], mix_ref[...], preferred_element_type=jnp.float32)
        out_ref[i] = (fields_ref[i].astype(jnp.float32) + mixed).astype(out_ref.dtype)
        return carry

    lax.fori_loop(0, out_rows, mix_row, 0)


def shards(fields, lon_taps, lat_taps, cycle_taps, band_start, band_width, mixing):
    row_count, col_count, chan_count = fields.shape
    basis_count = lon_taps.shape[1]
    taps_count = lon_taps.shape[2]
    reach_cells = (taps_count - 1) // 2
    band_len = lat_taps.shape[2]
    polar_rows = row_count // 2
    lat_count = lax.axis_size("lat")
    lon_count = lax.axis_size("lon")
    cycle_len = lon_count * col_count
    lat_pos = lax.axis_index("lat")
    lon_pos = lax.axis_index("lon")
    ext_rows = row_count + 2 * HALO
    total_rows = lat_count * row_count
    padded = extended_2(fields, (("lon", 1),), reach_cells, True)
    ext = extended_2(padded, (("lat", 0),), HALO, False)
    ext = jnp.pad(ext, ((0, 0), (0, 2 * col_count - ext.shape[1]), (0, 0)))
    taps_padded = jnp.pad(lon_taps, ((HALO, HALO), (0, 0), (0, 0)))
    taps_here = lax.dynamic_slice_in_dim(taps_padded, lat_pos * row_count, ext_rows, 0)
    taps_here = jnp.transpose(taps_here, (1, 0, 2))
    taps_hi = taps_here.astype(jnp.bfloat16).astype(jnp.float32)
    taps_lo = (taps_here - taps_hi).astype(jnp.bfloat16).astype(jnp.float32)
    tap_vec = jnp.stack([taps_hi, taps_lo], axis=1)
    tap_vec = jnp.pad(tap_vec, ((0, 0), (0, 0), (0, 0), (0, LANES - taps_count)))

    at_top = lat_pos == 0
    at_bottom = lat_pos == lat_count - 1
    slot_start = jnp.where(at_top, 0, row_count - polar_rows).astype(jnp.int32)
    slot_rows = lax.dynamic_slice_in_dim(fields, slot_start, polar_rows, 0)
    other_rows = lax.ppermute(slot_rows, "lon", [(i, (i + 1) % lon_count) for i in range(lon_count)])
    pair = [slot_rows, other_rows]
    gathered = jnp.where(lon_pos == 0, jnp.concatenate(pair, axis=1), jnp.concatenate(pair[::-1], axis=1))
    col_start = lon_pos * col_count
    coef_start = jnp.where(at_top, 0, polar_rows).astype(jnp.int32)
    coef = lax.dynamic_slice_in_dim(cycle_taps, coef_start, polar_rows, 1).astype(jnp.float32)
    rev = jnp.roll(jnp.flip(coef, axis=-1), 1, axis=-1)
    rev = jnp.roll(rev, col_start, axis=-1)
    crev = rev.reshape(basis_count, polar_rows, cycle_len // LANES, LANES)

    base_row = lat_pos * row_count
    steps_band = jnp.arange(band_len, dtype=jnp.int32)
    source = band_start[:, None] + steps_band[None, :]
    usable = (steps_band[None, :] < band_width[:, None]) & (source >= 0) & (source < total_rows)
    idx = jnp.clip(source - base_row + HALO, 0, ext_rows - 1).reshape(-1)
    wgt = jnp.where(usable[:, None, :], lat_taps.astype(jnp.float32), 0.0)
    wgt = jnp.transpose(wgt, (1, 0, 2)).reshape(-1)
    is_polar = (at_top | at_bottom).astype(jnp.int32)
    ctl = jnp.stack([is_polar, slot_start + HALO]).astype(jnp.int32)
    mix_flat = mixing.reshape(basis_count * chan_count, chan_count)

    smem = pl.BlockSpec(memory_space=pltpu.SMEM)
    vmem = pl.BlockSpec(memory_space=pltpu.VMEM)
    kernel = functools.partial(conv_kernel, basis_count, ext_rows, row_count, band_len)
    return pl.pallas_call(
        kernel,
        out_shape=jax.ShapeDtypeStruct(fields.shape, fields.dtype),
        in_specs=[smem, smem, smem] + [vmem] * 6,
        out_specs=vmem,
        scratch_shapes=[
            pltpu.VMEM((basis_count, ext_rows, col_count, chan_count), jnp.float32),
            pltpu.VMEM((row_count, col_count, basis_count * chan_count), jnp.bfloat16),
        ],
        compiler_params=pltpu.CompilerParams(vmem_limit_bytes=48 * 1024 * 1024),
    )(ctl, idx, wgt, ext, tap_vec, fields, mix_flat, gathered, crev)


def solution(mesh):
    in_specs = (
        P(("ens", "lat"), "lon", None),
        P(),
        P("lat", None, None),
        P(),
        P("lat"),
        P("lat"),
        P(),
    )
    out_specs = P(("ens", "lat"), "lon", None)
    return jax.shard_map(shards, mesh=mesh, in_specs=in_specs, out_specs=out_specs, check_vma=False)
```

time: 43.2 us -> 34.3 us (0.79)
  the two profiles are of different devices: /device:TPU:145 before, /device:TPU:136 now
where the time goes in v3:
time: 34.3 us; the launch traced here: 34.1 us
  waiting for transfers between devices  11.3 us (33%)
  Pallas kernels  10.7 us (31%)
  starting transfers between devices  6.91 us (20%)
  local copies, waits for them, and re-layouts  3.59 us (10%)
  other arithmetic  1.25 us (4%)
    pallas_call x1, Pallas kernels, shards(): pl.pallas_call(kernel, out_shape=jax.ShapeDtypeStruct(fields.shape, field...  10.7 us
    ppermute x2, waiting for transfers between devices, extended_2(): lax.ppermute(tail, axis, [(i, (i + 1) % count) for i in range(ends)])  7.26 us
    ppermute x2, starting transfers between devices, extended_2(): lax.ppermute(head, axis, [((i + 1) % count, i) for i in range(ends)])  4.3 us
    ppermute x2, waiting for transfers between devices, extended_2(): lax.ppermute(head, axis, [((i + 1) % count, i) for i in range(ends)])  4.09 us
    ppermute x2, starting transfers between devices, extended_2(): lax.ppermute(tail, axis, [(i, (i + 1) % count) for i in range(ends)])  2.42 us
    unnamed x15, local copies, waits for them, and re-layouts  1.26 us
    dynamic_slice x1, local copies, waits for them, and re-layouts, shards(): slot_rows = lax.dynamic_slice_in_dim(fields, slot_start, polar_rows, 0)  0.97 us
    slice x2, local copies, waits for them, and re-layouts, extended_2(): lax.slice_in_dim(cells, cells.shape[dim] - width, cells.shape[dim], axis=...  0.88 us
  transfers between devices with their start and end apart: 5, of which 2 were waited for; matrix products, arithmetic and copies ran while one was open for 10% of the time, Pallas kernels for 0%

profile of v3, /device:TPU:136, one launch (start us, length us, event | category | flops | bytes accessed | tf_op | source)
XLA Modules:
  0.0 34.1 jit_solution(9726262757309070773)
XLA Ops:
  0.0 0.0 copy-start
  0.0 0.0 copy-start.3
  0.0 0.0 copy-start.4
  0.0 0.0 copy-start.5
  0.0 0.0 copy-start.2
  0.0 0.8 %fusion.20 = (bf16[8,4,256]{2,1,0:T(4,128)(2,1)S(1)}, bf16[8,4,256]{2,1,0:T(4,128)(2,1)S(1)}) fusion(bf16[8,128,256]{2,1,0:T(8,128)(2,1)} %fields_ref.1), kind=kLoop, calls=%fused_computation.40 | loop fusion | bytes 65536 | tf_op jit(solution)/shard_map/slice | solution.py:19
  0.9 0.1 collective-permute-start.1
  1.0 0.5 %collective-permute-start = (bf16[8,4,256]{2,1,0:T(4,128)(2,1)S(1)}, bf16[8,4,256]{2,1,0:T(4,128)(2,1)S(1)}, u32[]{:S(2)}, u32[]{:S(2)}) collective-permute-start(bf16[8,4,256]{2,1,0:T(4,128)(2,1)S(1)} %get-tuple-element.7), channel_id=1, source_target_pairs={{0,4},{4,0},{1,5},{5,1},{2,6},{6,2},{3,7},{7,3},{8,12},{12,8},{9,1... | collective-permute-start | bytes 49160 | tf_op jit(solution)/shard_map/ppermute | solution.py:22
  1.5 1.0 %constant_dynamic-slice_fusion = bf16[4,128,256]{2,1,0:T(8,128)(2,1)S(1)} fusion(bf16[8,128,256]{2,1,0:T(8,128)(2,1)} %fields_ref.1, s32[]{:T(128)S(6)} %select_n.35), kind=kLoop, calls=%fused_computation.37 | loop fusion | bytes 524292 | tf_op jit(solution)/shard_map/dynamic_slice | solution.py:126
  2.4 0.2 collective-permute-start.4
  2.6 1.0 %copy.13 = f32[256,4,9]{2,0,1:T(8,128)S(1)} copy(f32[256,4,9]{0,1,2:T(4,128)} %param.8) | data formatting | bytes 73728 | tf_op args[1]
  3.7 0.0 copy-done.3
  3.7 0.1 slice.34
  3.8 0.0 copy-done.4
  3.8 0.1 add_clamp_fusion
  3.9 0.0 copy-done.5
  3.9 0.1 fusion.18
  4.0 0.1 copy.11
  4.1 0.2 reverse.2
  4.2 0.1 slice.35
  4.3 0.0 copy-done.2
  4.4 0.1 fusion.12
  4.5 0.0 collective-permute-done.1
  4.5 0.0 collective-permute-done
  4.5 0.0 copy-done
  4.5 0.1 pad_maximum_fusion
  4.7 4.2 %collective-permute-start.3 = (bf16[4,136,256]{2,1,0:T(8,128)(2,1)S(1)}, bf16[4,136,256]{2,1,0:T(8,128)(2,1)S(1)}, u32[]{:S(2)}, u32[]{:S(2)}) collective-permute-start(bf16[4,136,256]{2,1,0:T(8,128)(2,1)S(1)} %get-tuple-element.6), channel_id=1, source_target_pairs={{8,0},{16,8},{24,16},{32,24},{40,32},{48,40},{56,48},{64,56},{72,6... | collective-permute-start | bytes 835592 | tf_op jit(solution)/shard_map/ppermute | solution.py:24
  8.9 1.9 %collective-permute-start.2 = (bf16[4,136,256]{2,1,0:T(8,128)(2,1)S(1)}, bf16[4,136,256]{2,1,0:T(8,128)(2,1)S(1)}, u32[]{:S(2)}, u32[]{:S(2)}) collective-permute-start(bf16[4,136,256]{2,1,0:T(8,128)(2,1)S(1)} %get-tuple-element.5), channel_id=1, source_target_pairs={{0,8},{8,16},{16,24},{24,32},{32,40},{40,48},{48,56},{56,64},{64,7... | collective-permute-start | bytes 835592 | tf_op jit(solution)/shard_map/ppermute | solution.py:22
  10.8 0.1 pad_add_fusion.ctl_ref
  10.9 0.1 min.12.idx_ref
  11.0 0.1 copy.12
  11.1 0.1 reshape.57.wgt_ref
  11.2 0.0 copy-start.1
  11.3 0.0 collective-permute-done.4
  11.3 0.2 maximum_select_fusion.polar_ref
  11.5 4.1 %collective-permute-done.3 = bf16[4,136,256]{2,1,0:T(8,128)(2,1)S(1)} collective-permute-done((bf16[4,136,256]{2,1,0:T(8,128)(2,1)S(1)}, bf16[4,136,256]{2,1,0:T(8,128)(2,1)S(1)}, u32[]{:S(2)}, u32[]{:S(2)}) %collective-permute-start.3) | collective-permute-done | bytes 278560 | tf_op jit(solution)/shard_map/ppermute | solution.py:24
  15.6 7.3 %collective-permute-done.2 = bf16[4,136,256]{2,1,0:T(8,128)(2,1)S(1)} collective-permute-done((bf16[4,136,256]{2,1,0:T(8,128)(2,1)S(1)}, bf16[4,136,256]{2,1,0:T(8,128)(2,1)S(1)}, u32[]{:S(2)}, u32[]{:S(2)}) %collective-permute-start.2) | collective-permute-done | bytes 278560 | tf_op jit(solution)/shard_map/ppermute | solution.py:22
  22.8 0.5 %fusion.6.ext_ref = bf16[16,256,256]{2,1,0:T(8,128)(2,1)S(1)} fusion(bf16[4,136,256]{2,1,0:T(8,128)(2,1)S(1)} %collective-permute-done.3, bf16[4,136,256]{2,1,0:T(8,128)(2,1)S(1)} %collective-permute-done.2, bf16[8,4,256]{2,1,0:T(4,128)(2,1)S(1)} %collective-permute-done.1, bf16[8,128,256]{2,1,0:T(8,128)(2,1)S(1)} %copy-done, ...), kind=kLoop, calls=%fused_computation.7 | loop fusion | flops 16777216 | bytes 3211264 | tf_op jit(solution)/shard_map/concatenate | solution.py:20
  23.3 0.0 copy-done.1
  23.3 10.7 %shard_map.73 = bf16[8,128,256]{2,1,0:T(8,128)(2,1)} custom-call(s32[2]{0:T(128)S(1)} %pad_add_fusion.ctl_ref, s32[48]{0:T(128)S(1)} %min.12.idx_ref, f32[192]{0:T(256)S(1)} %reshape.57.wgt_ref, bf16[16,256,256]{2,1,0:T(8,128)(2,1)S(1)} %fusion.6.ext_ref, f32[4,2,16,128]{3,2,1,0:T(8,128)S(1)} %select_maximum_fusion.tap_ref, ...), custom_call_target="tpu_custom_call" | custom-call | tf_op jit(solution)/shard_map/pallas_call | solution.py:151
  (8 shorter events, 0.1 us)
Async XLA Ops:
  0.0 4.5 %copy-start = (bf16[8,128,256]{2,1,0:T(8,128)(2,1)S(1)}, bf16[8,128,256]{2,1,0:T(8,128)(2,1)}, u32[]{:S(2)}) copy-start(bf16[8,128,256]{2,1,0:T(8,128)(2,1)} %fields_ref.1) | copy-start | bytes 1572868
  0.0 3.7 %copy-start.3 = (bf16[4,8,256]{2,1,0:T(8,128)(2,1)S(1)}, bf16[4,8,256]{2,1,0:T(8,128)(2,1)}, u32[]{:S(2)}) copy-start(bf16[4,8,256]{2,1,0:T(8,128)(2,1)} %param.10) | copy-start | bytes 49156
  0.0 3.8 %copy-start.4 = (s32[8]{0:T(128)S(1)}, s32[8]{0:T(128)}, u32[]{:S(2)}) copy-start(s32[8]{0:T(128)} %param.11) | copy-start | bytes 100
  0.0 3.9 %copy-start.5 = (s32[8]{0:T(128)S(1)}, s32[8]{0:T(128)}, u32[]{:S(2)}) copy-start(s32[8]{0:T(128)} %param.12) | copy-start | bytes 100
  0.0 4.3 %copy-start.2 = (bf16[8,4,6]{0,1,2:T(4,128)(2,1)S(1)}, bf16[8,4,6]{0,1,2:T(4,128)(2,1)}, u32[]{:S(2)}) copy-start(bf16[8,4,6]{0,1,2:T(4,128)(2,1)} %param.9) | copy-start | bytes 1156
  0.9 3.6 %collective-permute-start.1 = (bf16[8,4,256]{2,1,0:T(4,128)(2,1)S(1)}, bf16[8,4,256]{2,1,0:T(4,128)(2,1)S(1)}, u32[]{:S(2)}, u32[]{:S(2)}) collective-permute-start(bf16[8,4,256]{2,1,0:T(4,128)(2,1)S(1)} %get-tuple-element.8), channel_id=1, source_target_pairs={{4,0},{0,4},{5,1},{1,5},{6,2},{2,6},{7,3},{3,7},{12,8},{8,12},{13,... | collective-permute-start | bytes 49160 | tf_op jit(solution)/shard_map/ppermute | solution.py:24
  1.0 3.5 %collective-permute-start = (bf16[8,4,256]{2,1,0:T(4,128)(2,1)S(1)}, bf16[8,4,256]{2,1,0:T(4,128)(2,1)S(1)}, u32[]{:S(2)}, u32[]{:S(2)}) collective-permute-start(bf16[8,4,256]{2,1,0:T(4,128)(2,1)S(1)} %get-tuple-element.7), channel_id=1, source_target_pairs={{0,4},{4,0},{1,5},{5,1},{2,6},{6,2},{3,7},{7,3},{8,12},{12,8},{9,1... | collective-permute-start | bytes 49160 | tf_op jit(solution)/shard_map/ppermute | solution.py:22
  2.4 8.8 %collective-permute-start.4 = (bf16[4,128,256]{2,1,0:T(8,128)(2,1)S(1)}, bf16[4,128,256]{2,1,0:T(8,128)(2,1)S(1)}, u32[]{:S(2)}, u32[]{:S(2)}) collective-permute-start(bf16[4,128,256]{2,1,0:T(8,128)(2,1)S(1)} %constant_dynamic-slice_fusion), channel_id=1, source_target_pairs={{0,4},{4,0},{1,5},{5,1},{2,6},{6,2},{3,7},{7,3},{8,12},{12,8},{9,1... | collective-permute-start | bytes 786440 | tf_op jit(solution)/shard_map/ppermute | solution.py:127
  4.7 10.9 %collective-permute-start.3 = (bf16[4,136,256]{2,1,0:T(8,128)(2,1)S(1)}, bf16[4,136,256]{2,1,0:T(8,128)(2,1)S(1)}, u32[]{:S(2)}, u32[]{:S(2)}) collective-permute-start(bf16[4,136,256]{2,1,0:T(8,128)(2,1)S(1)} %get-tuple-element.6), channel_id=1, source_target_pairs={{8,0},{16,8},{24,16},{32,24},{40,32},{48,40},{56,48},{64,56},{72,6... | collective-permute-start | bytes 835592 | tf_op jit(solution)/shard_map/ppermute | solution.py:24
  8.9 13.9 %collective-permute-start.2 = (bf16[4,136,256]{2,1,0:T(8,128)(2,1)S(1)}, bf16[4,136,256]{2,1,0:T(8,128)(2,1)S(1)}, u32[]{:S(2)}, u32[]{:S(2)}) collective-permute-start(bf16[4,136,256]{2,1,0:T(8,128)(2,1)S(1)} %get-tuple-element.5), channel_id=1, source_target_pairs={{0,8},{8,16},{16,24},{24,32},{32,40},{40,48},{48,56},{56,64},{64,7... | collective-permute-start | bytes 835592 | tf_op jit(solution)/shard_map/ppermute | solution.py:22
  11.2 12.1 %copy-start.1 = (bf16[4,256,256]{2,1,0:T(8,128)(2,1)S(1)}, bf16[4,256,256]{2,1,0:T(8,128)(2,1)}, u32[]{:S(2)}) copy-start(bf16[4,256,256]{2,1,0:T(8,128)(2,1)} %param.13) | copy-start | bytes 1572868

commit v4 on v3

--- a/solution.py
+++ b/solution.py
@@ -47,10 +47,11 @@
         x = ext_ref[r]
         parts = []
         for k in range(basis):
-            for half in range(2):
-                u = tap_ref[k, half, pl.ds(r, 1), :]
-                left = banded(u, cols, True)
-                right = banded(u, cols, False)
+            u = tap_ref[k, pl.ds(r, 1), :]
+            u_hi = u.astype(jnp.bfloat16).astype(jnp.float32)
+            for piece in (u_hi, u - u_hi):
+                left = banded(piece, cols, True)
+                right = banded(piece, cols, False)
                 parts.append(jnp.concatenate([left, right], axis=1).astype(jnp.bfloat16))
         tall = jnp.concatenate(parts, axis=0)
         y = jnp.dot(tall, x, preferred_element_type=jnp.float32)
@@ -110,15 +111,35 @@
     ext_rows = row_count + 2 * HALO
     total_rows = lat_count * row_count
     padded = extended_2(fields, (("lon", 1),), reach_cells, True)
-    ext = extended_2(padded, (("lat", 0),), HALO, False)
+    edges = jnp.concatenate(
+        [fields[:, col_count - reach_cells :], fields[:, :reach_cells]], axis=1
+    )
+    up = [(i, i + 1) for i in range(lat_count - 1)]
+    down = [(i + 1, i) for i in range(lat_count - 1)]
+    top_mid = lax.ppermute(fields[row_count - HALO :], "lat", up)
+    bot_mid = lax.ppermute(fields[:HALO], "lat", down)
+
+    def diag(pairs):
+        return [
+            (a * lon_count + o, b * lon_count + (o + 1) % lon_count)
+            for a, b in pairs
+            for o in range(lon_count)
+        ]
+
+    top_edge = lax.ppermute(edges[row_count - HALO :], ("lat", "lon"), diag(up))
+    bot_edge = lax.ppermute(edges[:HALO], ("lat", "lon"), diag(down))
+
+    def halo_rows(mid, edge):
+        return jnp.concatenate([edge[:, :reach_cells], mid, edge[:, reach_cells:]], axis=1)
+
+    ext = jnp.concatenate(
+        [halo_rows(top_mid, top_edge), padded, halo_rows(bot_mid, bot_edge)], axis=0
+    )
     ext = jnp.pad(ext, ((0, 0), (0, 2 * col_count - ext.shape[1]), (0, 0)))
     taps_padded = jnp.pad(lon_taps, ((HALO, HALO), (0, 0), (0, 0)))
     taps_here = lax.dynamic_slice_in_dim(taps_padded, lat_pos * row_count, ext_rows, 0)
     taps_here = jnp.transpose(taps_here, (1, 0, 2))
-    taps_hi = taps_here.astype(jnp.bfloat16).astype(jnp.float32)
-    taps_lo = (taps_here - taps_hi).astype(jnp.bfloat16).astype(jnp.float32)
-    tap_vec = jnp.stack([taps_hi, taps_lo], axis=1)
-    tap_vec = jnp.pad(tap_vec, ((0, 0), (0, 0), (0, 0), (0, LANES - taps_count)))
+    tap_vec = jnp.pad(taps_here, ((0, 0), (0, 0), (0, LANES - taps_count)))
 
     at_top = lat_pos == 0
     at_bottom = lat_pos == lat_count - 1

time: 34.3 us -> 43.1 us (1.26)
  the two profiles are of different devices: /device:TPU:136 before, /device:TPU:144 now
where the time goes in v4:
time: 43.1 us; the launch traced here: 42.7 us
  starting transfers between devices  12.5 us (29%)
  waiting for transfers between devices  12.2 us (28%)
  Pallas kernels  10.7 us (25%)
  local copies, waits for them, and re-layouts  3.82 us (9%)
  other arithmetic  3.33 us (8%)
    ppermute x1, waiting for transfers between devices, shards(): top_mid = lax.ppermute(fields[row_count - HALO:], 'lat', up)  11.3 us
    pallas_call x1, Pallas kernels, shards(): pl.pallas_call(kernel, out_shape=jax.ShapeDtypeStruct(fields.shape, field...  10.7 us
    ppermute x1, starting transfers between devices, shards(): bot_edge = lax.ppermute(edges[:HALO], ('lat', 'lon'), diag(down))  3.91 us
    ppermute x1, starting transfers between devices, shards(): top_edge = lax.ppermute(edges[row_count - HALO:], ('lat', 'lon'), diag(up))  2.86 us
    ppermute x1, starting transfers between devices, shards(): bot_mid = lax.ppermute(fields[:HALO], 'lat', down)  2.74 us
    ppermute x1, starting transfers between devices, shards(): top_mid = lax.ppermute(fields[row_count - HALO:], 'lat', up)  1.91 us
    unnamed x9, local copies, waits for them, and re-layouts  1.27 us
    dynamic_slice x1, local copies, waits for them, and re-layouts, shards(): slot_rows = lax.dynamic_slice_in_dim(fields, slot_start, polar_rows, 0)  1.22 us
  transfers between devices with their start and end apart: 7, of which 2 were waited for; matrix products, arithmetic and copies ran while one was open for 13% of the time, Pallas kernels for 0%

profile of v4, /device:TPU:144, one launch (start us, length us, event | category | flops | bytes accessed | tf_op | source)
XLA Modules:
  0.0 42.7 jit_solution(13824642374779969306)
XLA Ops:
  0.0 0.0 copy-start.2
  0.0 0.8 %fusion.26 = (bf16[8,4,256]{2,1,0:T(4,128)(2,1)S(1)}, bf16[8,4,256]{2,1,0:T(4,128)(2,1)S(1)}) fusion(bf16[8,128,256]{2,1,0:T(8,128)(2,1)} %fields_ref.1), kind=kLoop, calls=%fused_computation.43 | loop fusion | bytes 65536 | tf_op jit(solution)/shard_map/slice | solution.py:115
  0.8 0.1 collective-permute-start.3
  0.9 0.5 %collective-permute-start.2 = (bf16[8,4,256]{2,1,0:T(4,128)(2,1)S(1)}, bf16[8,4,256]{2,1,0:T(4,128)(2,1)S(1)}, u32[]{:S(2)}, u32[]{:S(2)}) collective-permute-start(bf16[8,4,256]{2,1,0:T(4,128)(2,1)S(1)} %get-tuple-element.8), channel_id=1, source_target_pairs={{0,4},{4,0},{1,5},{5,1},{2,6},{6,2},{3,7},{7,3},{8,12},{12,8},{9,1... | collective-permute-start | bytes 49160 | tf_op jit(solution)/shard_map/ppermute | solution.py:22
  1.4 3.9 %collective-permute-start.4 = (bf16[4,8,256]{2,1,0:T(8,128)(2,1)S(1)}, bf16[4,8,256]{2,1,0:T(8,128)(2,1)S(1)}, u32[]{:S(2)}, u32[]{:S(2)}) collective-permute-start(bf16[4,8,256]{2,1,0:T(8,128)(2,1)S(1)} %get-tuple-element.11), channel_id=1, source_target_pairs={{8,4},{12,0},{16,12},{20,8},{24,20},{28,16},{32,28},{36,24},{40,36... | collective-permute-start | bytes 49160 | tf_op jit(solution)/shard_map/ppermute | solution.py:130
  5.4 0.0 copy-start
  5.4 1.2 %constant_dynamic-slice_fusion = (bf16[4,128,256]{2,1,0:T(8,128)(2,1)S(1)}, bf16[4,128,256]{2,1,0:T(8,128)(2,1)S(1)}, bf16[4,128,256]{2,1,0:T(8,128)(2,1)S(1)}) fusion(bf16[8,128,256]{2,1,0:T(8,128)(2,1)} %fields_ref.1, s32[]{:T(128)S(6)} %select_n.35), kind=kLoop, calls=%fused_computation.41 | loop fusion | bytes 1572868 | tf_op jit(solution)/shard_map/dynamic_slice | solution.py:147
  6.6 2.7 %collective-permute-start.5 = (bf16[4,128,256]{2,1,0:T(8,128)(2,1)S(1)}, bf16[4,128,256]{2,1,0:T(8,128)(2,1)S(1)}, u32[]{:S(2)}, u32[]{:S(2)}) collective-permute-start(bf16[4,128,256]{2,1,0:T(8,128)(2,1)S(1)} %get-tuple-element.6), channel_id=1, source_target_pairs={{8,0},{16,8},{24,16},{32,24},{40,32},{48,40},{56,48},{64,56},{72,6... | collective-permute-start | bytes 786440 | tf_op jit(solution)/shard_map/ppermute | solution.py:120
  9.3 2.9 %collective-permute-start = (bf16[4,8,256]{2,1,0:T(8,128)(2,1)S(1)}, bf16[4,8,256]{2,1,0:T(8,128)(2,1)S(1)}, u32[]{:S(2)}, u32[]{:S(2)}) collective-permute-start(bf16[4,8,256]{2,1,0:T(8,128)(2,1)S(1)} %get-tuple-element.10), channel_id=1, source_target_pairs={{0,12},{4,8},{8,20},{12,16},{16,28},{20,24},{24,36},{28,32},{32,44... | collective-permute-start | bytes 49160 | tf_op jit(solution)/shard_map/ppermute | solution.py:129
  12.2 0.7 %dynamic-slice_convert_fusion = f32[4,4,256]{2,1,0:T(4,128)S(1)} fusion(bf16[4,8,256]{2,1,0:T(8,128)(2,1)} %param.10, s32[]{:T(128)S(6)} %select_n.35), kind=kLoop, calls=%fused_computation.33 | loop fusion | flops 4096 | bytes 24580 | tf_op jit(solution)/shard_map/convert_element_type | solution.py:153
  13.0 0.1 slice.64
  13.0 0.7 %add_clamp_fusion = s32[8,6]{1,0:T(8,128)S(1)} fusion(s32[]{:T(128)S(6)} %mul.7, s32[8]{0:T(128)} %param.11), kind=kLoop, calls=%fused_computation.35 | loop fusion | flops 192 | bytes 228 | tf_op jit(solution)/shard_map/jit(clip)/min | solution.py:162
  13.8 0.7 %fusion.25 = pred[8,6]{1,0:T(8,128)(4,1)S(1)} fusion(s32[8]{0:T(128)} %param.12, s32[8]{0:T(128)} %param.11), kind=kLoop, calls=%fused_computation.40 | loop fusion | flops 288 | bytes 112 | tf_op jit(solution)/shard_map/and | solution.py:161
  14.5 0.1 copy.10
  14.6 1.0 %copy.12 = f32[256,4,9]{2,0,1:T(8,128)S(1)} copy(f32[256,4,9]{0,1,2:T(4,128)} %param.8) | data formatting | bytes 73728 | tf_op args[1]
  15.6 0.2 reverse.2
  15.8 0.1 slice.71
  15.9 0.0 copy-done.2
  15.9 0.1 fusion.20
  16.0 0.1 pad_add_fusion.ctl_ref
  16.1 0.1 min.12.idx_ref
  16.2 0.1 copy.11
  16.3 0.1 reshape.57.wgt_ref
  16.5 0.0 collective-permute-done.4
  16.5 0.4 %collective-permute-start.6 = (bf16[4,128,256]{2,1,0:T(8,128)(2,1)S(1)}, bf16[4,128,256]{2,1,0:T(8,128)(2,1)S(1)}, u32[]{:S(2)}, u32[]{:S(2)}) collective-permute-start(bf16[4,128,256]{2,1,0:T(8,128)(2,1)S(1)} %get-tuple-element.5), channel_id=1, source_target_pairs={{0,4},{4,0},{1,5},{5,1},{2,6},{6,2},{3,7},{7,3},{8,12},{12,8},{9,1... | collective-permute-start | bytes 786440 | tf_op jit(solution)/shard_map/ppermute | solution.py:148
  16.9 0.8 %collective-permute-done = bf16[4,8,256]{2,1,0:T(8,128)(2,1)S(1)} collective-permute-done((bf16[4,8,256]{2,1,0:T(8,128)(2,1)S(1)}, bf16[4,8,256]{2,1,0:T(8,128)(2,1)S(1)}, u32[]{:S(2)}, u32[]{:S(2)}) %collective-permute-start) | collective-permute-done | bytes 16416 | tf_op jit(solution)/shard_map/ppermute | solution.py:129
  17.7 1.9 %collective-permute-start.1 = (bf16[4,128,256]{2,1,0:T(8,128)(2,1)S(1)}, bf16[4,128,256]{2,1,0:T(8,128)(2,1)S(1)}, u32[]{:S(2)}, u32[]{:S(2)}) collective-permute-start(bf16[4,128,256]{2,1,0:T(8,128)(2,1)S(1)} %get-tuple-element.7), channel_id=1, source_target_pairs={{0,8},{8,16},{16,24},{24,32},{32,40},{40,48},{48,56},{56,64},{64,7... | collective-permute-start | bytes 786440 | tf_op jit(solution)/shard_map/ppermute | solution.py:119
  19.7 0.0 copy-start.1
  19.7 0.0 collective-permute-done.6
  19.7 0.2 maximum_select_fusion.polar_ref
  19.9 0.0 collective-permute-done.3
  19.9 0.0 collective-permute-done.2
  19.9 0.0 collective-permute-done.5
  19.9 11.3 %collective-permute-done.1 = bf16[4,128,256]{2,1,0:T(8,128)(2,1)S(1)} collective-permute-done((bf16[4,128,256]{2,1,0:T(8,128)(2,1)S(1)}, bf16[4,128,256]{2,1,0:T(8,128)(2,1)S(1)}, u32[]{:S(2)}, u32[]{:S(2)}) %collective-permute-start.1) | collective-permute-done | bytes 262176 | tf_op jit(solution)/shard_map/ppermute | solution.py:119
  31.3 0.0 copy-done
  31.3 0.7 %fusion.12.ext_ref = bf16[16,256,256]{2,1,0:T(8,128)(2,1)S(1)} fusion(bf16[4,4,256]{2,1,0:T(4,128)(2,1)S(1)} %get-tuple-element.15, bf16[4,128,256]{2,1,0:T(8,128)(2,1)S(1)} %collective-permute-done.5, bf16[4,4,256]{2,1,0:T(4,128)(2,1)S(1)} %get-tuple-element.14, bf16[8,4,256]{2,1,0:T(4,128)(2,1)S(1)} %collective-permute-done.3, ...), kind=kLoop, calls=%fused_computation.13 | loop fusion | flops 29360128 | bytes 3211264 | tf_op jit(solution)/shard_map/concatenate | solution.py:135
  32.0 0.0 copy-done.1
  32.0 10.7 %shard_map.73 = bf16[8,128,256]{2,1,0:T(8,128)(2,1)} custom-call(s32[2]{0:T(128)S(1)} %pad_add_fusion.ctl_ref, s32[48]{0:T(128)S(1)} %min.12.idx_ref, f32[192]{0:T(256)S(1)} %reshape.57.wgt_ref, bf16[16,256,256]{2,1,0:T(8,128)(2,1)S(1)} %fusion.12.ext_ref, f32[4,16,128]{2,1,0:T(8,128)S(1)} %pad.14.tap_ref, bf16[8,128,256]{2,1,0:T(8,128)(2,1)S(1)} %copy-done, ...), custom_call_target="tpu_custom_call" | custom-call | tf_op jit(solution)/shard_map/pallas_call | solution.py:172
  (8 shorter events, 0.1 us)
Async XLA Ops:
  0.0 15.9 %copy-start.2 = (bf16[8,4,6]{0,1,2:T(4,128)(2,1)S(1)}, bf16[8,4,6]{0,1,2:T(4,128)(2,1)}, u32[]{:S(2)}) copy-start(bf16[8,4,6]{0,1,2:T(4,128)(2,1)} %param.9) | copy-start | bytes 1156
  0.8 19.1 %collective-permute-start.3 = (bf16[8,4,256]{2,1,0:T(4,128)(2,1)S(1)}, bf16[8,4,256]{2,1,0:T(4,128)(2,1)S(1)}, u32[]{:S(2)}, u32[]{:S(2)}) collective-permute-start(bf16[8,4,256]{2,1,0:T(4,128)(2,1)S(1)} %get-tuple-element.9), channel_id=1, source_target_pairs={{4,0},{0,4},{5,1},{1,5},{6,2},{2,6},{7,3},{3,7},{12,8},{8,12},{13,... | collective-permute-start | bytes 49160 | tf_op jit(solution)/shard_map/ppermute | solution.py:24
  0.9 19.0 %collective-permute-start.2 = (bf16[8,4,256]{2,1,0:T(4,128)(2,1)S(1)}, bf16[8,4,256]{2,1,0:T(4,128)(2,1)S(1)}, u32[]{:S(2)}, u32[]{:S(2)}) collective-permute-start(bf16[8,4,256]{2,1,0:T(4,128)(2,1)S(1)} %get-tuple-element.8), channel_id=1, source_target_pairs={{0,4},{4,0},{1,5},{5,1},{2,6},{6,2},{3,7},{7,3},{8,12},{12,8},{9,1... | collective-permute-start | bytes 49160 | tf_op jit(solution)/shard_map/ppermute | solution.py:22
  1.4 15.0 %collective-permute-start.4 = (bf16[4,8,256]{2,1,0:T(8,128)(2,1)S(1)}, bf16[4,8,256]{2,1,0:T(8,128)(2,1)S(1)}, u32[]{:S(2)}, u32[]{:S(2)}) collective-permute-start(bf16[4,8,256]{2,1,0:T(8,128)(2,1)S(1)} %get-tuple-element.11), channel_id=1, source_target_pairs={{8,4},{12,0},{16,12},{20,8},{24,20},{28,16},{32,28},{36,24},{40,36... | collective-permute-start | bytes 49160 | tf_op jit(solution)/shard_map/ppermute | solution.py:130
  5.4 25.9 %copy-start = (bf16[8,128,256]{2,1,0:T(8,128)(2,1)S(1)}, bf16[8,128,256]{2,1,0:T(8,128)(2,1)}, u32[]{:S(2)}) copy-start(bf16[8,128,256]{2,1,0:T(8,128)(2,1)} %fields_ref.1) | copy-start | bytes 1572868
  6.6 13.3 %collective-permute-start.5 = (bf16[4,128,256]{2,1,0:T(8,128)(2,1)S(1)}, bf16[4,128,256]{2,1,0:T(8,128)(2,1)S(1)}, u32[]{:S(2)}, u32[]{:S(2)}) collective-permute-start(bf16[4,128,256]{2,1,0:T(8,128)(2,1)S(1)} %get-tuple-element.6), channel_id=1, source_target_pairs={{8,0},{16,8},{24,16},{32,24},{40,32},{48,40},{56,48},{64,56},{72,6... | collective-permute-start | bytes 786440 | tf_op jit(solution)/shard_map/ppermute | solution.py:120
  9.3 8.4 %collective-permute-start = (bf16[4,8,256]{2,1,0:T(8,128)(2,1)S(1)}, bf16[4,8,256]{2,1,0:T(8,128)(2,1)S(1)}, u32[]{:S(2)}, u32[]{:S(2)}) collective-permute-start(bf16[4,8,256]{2,1,0:T(8,128)(2,1)S(1)} %get-tuple-element.10), channel_id=1, source_target_pairs={{0,12},{4,8},{8,20},{12,16},{16,28},{20,24},{24,36},{28,32},{32,44... | collective-permute-start | bytes 49160 | tf_op jit(solution)/shard_map/ppermute | solution.py:129
  16.5 3.2 %collective-permute-start.6 = (bf16[4,128,256]{2,1,0:T(8,128)(2,1)S(1)}, bf16[4,128,256]{2,1,0:T(8,128)(2,1)S(1)}, u32[]{:S(2)}, u32[]{:S(2)}) collective-permute-start(bf16[4,128,256]{2,1,0:T(8,128)(2,1)S(1)} %get-tuple-element.5), channel_id=1, source_target_pairs={{0,4},{4,0},{1,5},{5,1},{2,6},{6,2},{3,7},{7,3},{8,12},{12,8},{9,1... | collective-permute-start | bytes 786440 | tf_op jit(solution)/shard_map/ppermute | solution.py:148
  17.7 13.6 %collective-permute-start.1 = (bf16[4,128,256]{2,1,0:T(8,128)(2,1)S(1)}, bf16[4,128,256]{2,1,0:T(8,128)(2,1)S(1)}, u32[]{:S(2)}, u32[]{:S(2)}) collective-permute-start(bf16[4,128,256]{2,1,0:T(8,128)(2,1)S(1)} %get-tuple-element.7), channel_id=1, source_target_pairs={{0,8},{8,16},{16,24},{24,32},{32,40},{40,48},{48,56},{56,64},{64,7... | collective-permute-start | bytes 786440 | tf_op jit(solution)/shard_map/ppermute | solution.py:119
  19.7 12.3 %copy-start.1 = (bf16[4,256,256]{2,1,0:T(8,128)(2,1)S(1)}, bf16[4,256,256]{2,1,0:T(8,128)(2,1)}, u32[]{:S(2)}) copy-start(bf16[4,256,256]{2,1,0:T(8,128)(2,1)} %param.13) | copy-start | bytes 1572868

commit v5 on v3

v5 whole, which is shorter than its diff:
```python
import functools

import jax
import jax.numpy as jnp
from jax import lax
from jax.experimental import pallas as pl
from jax.experimental.pallas import tpu as pltpu
from jax.sharding import PartitionSpec as P

HALO = 4
LANES = 128
SENT_ROWS = 144


def banded(vec, rows, upper):
    rolled = pltpu.roll(jnp.broadcast_to(vec, (rows, LANES)), 0, 1, stride=1, stride_axis=0)
    row = lax.broadcasted_iota(jnp.int32, (rows, LANES), 0)
    col = lax.broadcasted_iota(jnp.int32, (rows, LANES), 1)
    keep = col >= row if upper else col < row
    return jnp.where(keep, rolled, 0.0)


def conv_kernel(basis, out_rows, band_len,
                idx_ref, wgt_ref, own_ref, tap_ref, fields_ref, mix_ref,
                polar_ref, crev_ref, out_ref,
                top_ref, bot_ref, f_ref, h_ref, send_sem, recv_sem):
    cols = out_ref.shape[1]
    chans = out_ref.shape[2]
    polar_count = polar_ref.shape[0]
    lat = lax.axis_index("lat")
    last = lax.axis_size("lat") - 1
    has_up = lat < last
    has_down = lat > 0

    pad_rows = top_ref.shape[1] - SENT_ROWS
    zeros = jnp.zeros((HALO, pad_rows, chans), top_ref.dtype)
    top_ref[:, pl.ds(SENT_ROWS, pad_rows), :] = zeros
    bot_ref[:, pl.ds(SENT_ROWS, pad_rows), :] = zeros

    barrier = pltpu.get_barrier_semaphore()

    @pl.when(has_up)
    def _():
        pl.semaphore_signal(barrier, 1, device_id={"lat": lat + 1},
                            device_id_type=pl.DeviceIdType.MESH)

    @pl.when(has_down)
    def _():
        pl.semaphore_signal(barrier, 1, device_id={"lat": lat - 1},
                            device_id_type=pl.DeviceIdType.MESH)

    pl.semaphore_wait(barrier, has_up.astype(jnp.int32) + has_down.astype(jnp.int32))

    up_copy = pltpu.make_async_remote_copy(
        src_ref=own_ref.at[pl.ds(out_rows - HALO, HALO), pl.ds(0, SENT_ROWS)],
        dst_ref=top_ref.at[:, pl.ds(0, SENT_ROWS)],
        send_sem=send_sem.at[0], recv_sem=recv_sem.at[0],
        device_id={"lat": jnp.minimum(lat + 1, last)}, device_id_type=pl.DeviceIdType.MESH)
    down_copy = pltpu.make_async_remote_copy(
        src_ref=own_ref.at[pl.ds(0, HALO), pl.ds(0, SENT_ROWS)],
        dst_ref=bot_ref.at[:, pl.ds(0, SENT_ROWS)],
        send_sem=send_sem.at[1], recv_sem=recv_sem.at[1],
        device_id={"lat": jnp.maximum(lat - 1, 0)}, device_id_type=pl.DeviceIdType.MESH)

    @pl.when(has_up)
    def _():
        up_copy.start()

    @pl.when(has_down)
    def _():
        down_copy.start()

    def filter_rows(src_ref, count, first):
        def filter_row(r, carry):
            x = src_ref[r]
            parts = []
            for k in range(basis):
                u = tap_ref[k, pl.ds(first + r, 1), :]
                u_hi = u.astype(jnp.bfloat16).astype(jnp.float32)
                for piece in (u_hi, u - u_hi):
                    left = banded(piece, cols, True)
                    right = banded(piece, cols, False)
                    parts.append(jnp.concatenate([left, right], axis=1).astype(jnp.bfloat16))
            tall = jnp.concatenate(parts, axis=0)
            y = jnp.dot(tall, x, preferred_element_type=jnp.float32)
            for k in range(basis):
                lo = 2 * k * cols
                v = y[lo : lo + cols] + y[lo + cols : lo + 2 * cols]
                f_ref[k, first + r] = v.astype(jnp.bfloat16).astype(jnp.float32)
            return carry

        lax.fori_loop(0, count, filter_row, 0)

    def zero_rows(first):
        f_ref[:, pl.ds(first, HALO)] = jnp.zeros((basis, HALO, cols, chans), jnp.float32)

    filter_rows(own_ref, out_rows, HALO)

    @pl.when((lat == 0) | (lat == last))
    def _polar():
        slot = HALO + jnp.minimum(lat, 1) * (out_rows - polar_count)
        for k in range(basis):
            for p in range(polar_count):
                va = crev_ref[k, p, pl.ds(0, 1), :]
                vb = crev_ref[k, p, pl.ds(1, 1), :]
                ra_u, ra_w = banded(va, cols, True), banded(va, cols, False)
                rb_u, rb_w = banded(vb, cols, True), banded(vb, cols, False)
                circ = jnp.concatenate([ra_u + rb_w, rb_u + ra_w], axis=1).astype(jnp.bfloat16)
                y = jnp.dot(circ, polar_ref[p], preferred_element_type=jnp.float32)
                f_ref[k, slot + p] = y.astype(jnp.bfloat16).astype(jnp.float32)

    @pl.when(has_up)
    def _():
        up_copy.wait_send()

    @pl.when(has_down)
    def _():
        down_copy.wait_send()

    @pl.when(has_down)
    def _():
        up_copy.wait_recv()
        filter_rows(top_ref, HALO, 0)

    @pl.when(lat == 0)
    def _():
        zero_rows(0)

    @pl.when(has_up)
    def _():
        down_copy.wait_recv()
        filter_rows(bot_ref, HALO, HALO + out_rows)

    @pl.when(lat == last)
    def _():
        zero_rows(HALO + out_rows)

    for k in range(basis):
        def band_row(i, carry):
            acc = jnp.zeros((cols, chans), jnp.float32)
            for t in range(band_len):
                r = idx_ref[i * band_len + t]
                w = wgt_ref[(k * out_rows + i) * band_len + t]
                acc = acc + w * f_ref[k, r]
            h_ref[i, :, k * chans : (k + 1) * chans] = acc.astype(jnp.bfloat16)
            return carry

        lax.fori_loop(0, out_rows, band_row, 0)

    def mix_row(i, carry):
        mixed = jnp.dot(h_ref[i], mix_ref[...], preferred_element_type=jnp.float32)
        out_ref[i] = (fields_ref[i].astype(jnp.float32) + mixed).astype(out_ref.dtype)
        return carry

    lax.fori_loop(0, out_rows, mix_row, 0)


def shards(fields, lon_taps, lat_taps, cycle_taps, band_start, band_width, mixing):
    row_count, col_count, chan_count = fields.shape
    basis_count = lon_taps.shape[1]
    taps_count = lon_taps.shape[2]
    reach_cells = (taps_count - 1) // 2
    band_len = lat_taps.shape[2]
    polar_rows = row_count // 2
    lat_count = lax.axis_size("lat")
    lon_count = lax.axis_size("lon")
    assert lon_count == 2
    cycle_len = lon_count * col_count
    lat_pos = lax.axis_index("lat")
    lon_pos = lax.axis_index("lon")
    ext_rows = row_count + 2 * HALO
    total_rows = lat_count * row_count

    at_top = lat_pos == 0
    at_bottom = lat_pos == lat_count - 1
    slot_start = jnp.where(at_top, 0, row_count - polar_rows).astype(jnp.int32)
    slot_rows = lax.dynamic_slice_in_dim(fields, slot_start, polar_rows, 0)
    edges = jnp.concatenate([fields[:, :reach_cells], fields[:, col_count - reach_cells :]], axis=1)
    payload = jnp.concatenate([edges.reshape(-1), slot_rows.reshape(-1)])
    got = lax.ppermute(payload, "lon", [(0, 1), (1, 0)])
    other_edges = got[: edges.size].reshape(edges.shape)
    other_rows = got[edges.size :].reshape(slot_rows.shape)
    pad_cols = 2 * col_count - col_count - 2 * reach_cells
    own = jnp.concatenate(
        [
            other_edges[:, reach_cells:],
            fields,
            other_edges[:, :reach_cells],
            jnp.zeros((row_count, pad_cols, chan_count), fields.dtype),
        ],
        axis=1,
    )
    pair = [slot_rows, other_rows]
    gathered = jnp.where(lon_pos == 0, jnp.concatenate(pair, axis=1), jnp.concatenate(pair[::-1], axis=1))

    taps_padded = jnp.pad(lon_taps, ((HALO, HALO), (0, 0), (0, 0)))
    taps_here = lax.dynamic_slice_in_dim(taps_padded, lat_pos * row_count, ext_rows, 0)
    taps_here = jnp.transpose(taps_here, (1, 0, 2))
    tap_vec = jnp.pad(taps_here, ((0, 0), (0, 0), (0, LANES - taps_count)))

    col_start = lon_pos * col_count
    coef_start = jnp.where(at_top, 0, polar_rows).astype(jnp.int32)
    coef = lax.dynamic_slice_in_dim(cycle_taps, coef_start, polar_rows, 1).astype(jnp.float32)
    rev = jnp.roll(jnp.flip(coef, axis=-1), 1, axis=-1)
    rev = jnp.roll(rev, col_start, axis=-1)
    crev = rev.reshape(basis_count, polar_rows, cycle_len // LANES, LANES)

    base_row = lat_pos * row_count
    steps_band = jnp.arange(band_len, dtype=jnp.int32)
    source = band_start[:, None] + steps_band[None, :]
    usable = (steps_band[None, :] < band_width[:, None]) & (source >= 0) & (source < total_rows)
    idx = jnp.clip(source - base_row + HALO, 0, ext_rows - 1).reshape(-1)
    wgt = jnp.where(usable[:, None, :], lat_taps.astype(jnp.float32), 0.0)
    wgt = jnp.transpose(wgt, (1, 0, 2)).reshape(-1)
    mix_flat = mixing.reshape(basis_count * chan_count, chan_count)

    smem = pl.BlockSpec(memory_space=pltpu.SMEM)
    vmem = pl.BlockSpec(memory_space=pltpu.VMEM)
    kernel = functools.partial(conv_kernel, basis_count, row_count, band_len)
    return pl.pallas_call(
        kernel,
        out_shape=jax.ShapeDtypeStruct(fields.shape, fields.dtype),
        in_specs=[smem, smem] + [vmem] * 6,
        out_specs=vmem,
        scratch_shapes=[
            pltpu.VMEM((HALO, 2 * col_count, chan_count), fields.dtype),
            pltpu.VMEM((HALO, 2 * col_count, chan_count), fields.dtype),
            pltpu.VMEM((basis_count, ext_rows, col_count, chan_count), jnp.float32),
            pltpu.VMEM((row_count, col_count, basis_count * chan_count), jnp.bfloat16),
            pltpu.SemaphoreType.DMA((2,)),
            pltpu.SemaphoreType.DMA((2,)),
        ],
        compiler_params=pltpu.CompilerParams(
            vmem_limit_bytes=48 * 1024 * 1024, collective_id=0, has_side_effects=True
        ),
    )(idx, wgt, own, tap_vec, fields, mix_flat, gathered, crev)


def solution(mesh):
    in_specs = (
        P(("ens", "lat"), "lon", None),
        P(),
        P("lat", None, None),
        P(),
        P("lat"),
        P("lat"),
        P(),
    )
    out_specs = P(("ens", "lat"), "lon", None)
    return jax.shard_map(shards, mesh=mesh, in_specs=in_specs, out_specs=out_specs, check_vma=False)
```

time: 34.3 us -> 26.2 us (0.76)
  the two profiles are of different devices: /device:TPU:136 before, /device:TPU:145 now
where the time goes in v5:
time: 26.2 us; the launch traced here: 25.7 us
  Pallas kernels  19.1 us (73%)
  local copies, waits for them, and re-layouts  4.86 us (19%)
  other arithmetic  0.82 us (3%)
  starting transfers between devices  0.76 us (3%)
    pallas_call x1, Pallas kernels, shards(): pl.pallas_call(kernel, out_shape=jax.ShapeDtypeStruct(fields.shape, field...  19.1 us
    unnamed x20, local copies, waits for them, and re-layouts  2.34 us
    dynamic_slice x1, local copies, waits for them, and re-layouts, shards(): slot_rows = lax.dynamic_slice_in_dim(fields, slot_start, polar_rows, 0)  0.97 us
    slice x1, local copies, waits for them, and re-layouts, shards(): fields[:, :reach_cells]  0.83 us
    ppermute x1, starting transfers between devices, shards(): got = lax.ppermute(payload, 'lon', [(0, 1), (1, 0)])  0.76 us
  transfers between devices with their start and end apart: 1, of which 0 were waited for; matrix products, arithmetic and copies ran while one was open for 5% of the time, Pallas kernels for 0%

profile of v5, /device:TPU:145, one launch (start us, length us, event | category | flops | bytes accessed | tf_op | source)
XLA Modules:
  0.0 25.7 jit_solution(9132189501631857574)
XLA Ops:
  0.0 0.0 copy-start.5
  0.0 0.0 copy-start.6
  0.0 0.0 copy-start.3
  0.0 0.0 copy-start.4
  0.0 0.8 %fusion.8 = (bf16[8,4,256]{2,1,0:T(4,128)(2,1)S(1)}, bf16[8,4,256]{2,1,0:T(4,128)(2,1)S(1)}) fusion(bf16[8,128,256]{2,1,0:T(8,128)(2,1)} %fields_ref.1), kind=kLoop, calls=%fused_computation.23 | loop fusion | bytes 65536 | tf_op jit(solution)/shard_map/slice | solution.py:178
  0.9 0.0 copy-start.2
  0.9 1.0 %constant_dynamic-slice_fusion = bf16[4,128,256]{2,1,0:T(8,128)(2,1)S(1)} fusion(bf16[8,128,256]{2,1,0:T(8,128)(2,1)} %fields_ref.1, s32[]{:T(128)S(6)} %select_n.36), kind=kLoop, calls=%fused_computation.22 | loop fusion | bytes 524292 | tf_op jit(solution)/shard_map/dynamic_slice | solution.py:177
  1.9 0.2 copy.14
  2.2 0.8 %collective-permute-start = (bf16[147456]{0:T(1024)(128)(2,1)S(1)}, bf16[147456]{0:T(1024)(128)(2,1)S(1)}, u32[]{:S(2)}, u32[]{:S(2)}) collective-permute-start(bf16[147456]{0:T(1024)(128)(2,1)S(1)} %pad_maximum_fusion), channel_id=1, source_target_pairs={{0,4},{4,0},{1,5},{5,1},{2,6},{6,2},{3,7},{7,3},{8,12},{12,8},{9,1... | collective-permute-start | bytes 884744 | tf_op jit(solution)/shard_map/ppermute | solution.py:180
  2.9 0.0 copy-done.5
  2.9 0.1 add_clamp_fusion
  3.0 0.0 copy-done.6
  3.0 0.1 fusion.7
  3.1 0.1 copy.10
  3.2 0.0 copy-done.3
  3.2 0.0 copy-done.4
  3.2 0.1 slice.55
  3.3 0.1 min.12.idx_ref
  3.4 0.1 copy.11
  3.5 0.1 reshape.75.wgt_ref
  3.6 0.2 reverse.2
  3.8 0.1 slice.56
  3.9 0.1 fusion.3
  4.0 0.0 copy-done.2
  4.0 0.2 copy.12
  4.3 0.1 pad.21.clone
  4.4 0.0 copy-start
  4.4 0.0 collective-permute-done
  4.4 0.1 reshape.79
  4.6 0.2 maximum_select_fusion.polar_ref
  4.8 0.0 copy-start.1
  4.8 0.6 %copy-done = bf16[8,128,256]{2,1,0:T(8,128)(2,1)S(1)} copy-done((bf16[8,128,256]{2,1,0:T(8,128)(2,1)S(1)}, bf16[8,128,256]{2,1,0:T(8,128)(2,1)}, u32[]{:S(2)}) %copy-start) | copy-done | bytes 524312
  5.4 0.3 %maximum_maximum_fusion.own_ref = bf16[8,256,256]{2,1,0:T(8,128)(2,1)S(1)} fusion(bf16[8,4,256]{2,1,0:T(4,128)(2,1)S(1)} %get-tuple-element.8, bf16[8,128,256]{2,1,0:T(8,128)(2,1)S(1)} %copy-done, bf16[8,4,256]{2,1,0:T(4,128)(2,1)S(1)} %get-tuple-element.7, bf16[256]{0:T(256)(128)(2,1)S(1)} %pad.21.clone), kind=kLoop, calls=%fused_computation | loop fusion | flops 4194304 | bytes 1606144 | tf_op jit(solution)/shard_map/concatenate | solution.py:184
  5.7 0.2 copy-done.1
  5.9 19.1 %shard_map.73 = bf16[8,128,256]{2,1,0:T(8,128)(2,1)S(1)} custom-call(s32[48]{0:T(128)S(1)} %min.12.idx_ref, f32[192]{0:T(256)S(1)} %reshape.75.wgt_ref, bf16[8,256,256]{2,1,0:T(8,128)(2,1)S(1)} %maximum_maximum_fusion.own_ref, f32[4,16,128]{2,1,0:T(8,128)S(1)} %pad.9.tap_ref, bf16[8,128,256]{2,1,0:T(8,128)(2,1)S(1)} %copy-done, ...), custom_call_target="tpu_custom_call" | custom-call | tf_op jit(solution)/shard_map/pallas_call | solution.py:220
  25.0 0.8 %copy.16 = bf16[8,128,256]{2,1,0:T(8,128)(2,1)} copy(bf16[8,128,256]{2,1,0:T(8,128)(2,1)S(1)} %shard_map.73) | data formatting | bytes 1048576
  (14 shorter events, 0.2 us)
Async XLA Ops:
  0.0 2.9 %copy-start.5 = (s32[8]{0:T(128)S(1)}, s32[8]{0:T(128)}, u32[]{:S(2)}) copy-start(s32[8]{0:T(128)} %param.11) | copy-start | bytes 100
  0.0 3.0 %copy-start.6 = (s32[8]{0:T(128)S(1)}, s32[8]{0:T(128)}, u32[]{:S(2)}) copy-start(s32[8]{0:T(128)} %param.12) | copy-start | bytes 100
  0.0 3.2 %copy-start.3 = (bf16[8,4,6]{0,1,2:T(4,128)(2,1)S(1)}, bf16[8,4,6]{0,1,2:T(4,128)(2,1)}, u32[]{:S(2)}) copy-start(bf16[8,4,6]{0,1,2:T(4,128)(2,1)} %param.9) | copy-start | bytes 1156
  0.0 3.2 %copy-start.4 = (bf16[4,8,256]{2,1,0:T(8,128)(2,1)S(1)}, bf16[4,8,256]{2,1,0:T(8,128)(2,1)}, u32[]{:S(2)}) copy-start(bf16[4,8,256]{2,1,0:T(8,128)(2,1)} %param.10) | copy-start | bytes 49156
  0.9 3.1 %copy-start.2 = (f32[256,4,9]{0,1,2:T(4,128)S(1)}, f32[256,4,9]{0,1,2:T(4,128)}, u32[]{:S(2)}) copy-start(f32[256,4,9]{0,1,2:T(4,128)} %param.8) | copy-start | bytes 110596
  2.2 2.2 %collective-permute-start = (bf16[147456]{0:T(1024)(128)(2,1)S(1)}, bf16[147456]{0:T(1024)(128)(2,1)S(1)}, u32[]{:S(2)}, u32[]{:S(2)}) collective-permute-start(bf16[147456]{0:T(1024)(128)(2,1)S(1)} %pad_maximum_fusion), channel_id=1, source_target_pairs={{0,4},{4,0},{1,5},{5,1},{2,6},{6,2},{3,7},{7,3},{8,12},{12,8},{9,1... | collective-permute-start | bytes 884744 | tf_op jit(solution)/shard_map/ppermute | solution.py:180
  4.4 1.0 %copy-start = (bf16[8,128,256]{2,1,0:T(8,128)(2,1)S(1)}, bf16[8,128,256]{2,1,0:T(8,128)(2,1)}, u32[]{:S(2)}) copy-start(bf16[8,128,256]{2,1,0:T(8,128)(2,1)} %fields_ref.1) | copy-start | bytes 1572868
  4.8 1.1 %copy-start.1 = (bf16[4,256,256]{2,1,0:T(8,128)(2,1)S(1)}, bf16[4,256,256]{2,1,0:T(8,128)(2,1)}, u32[]{:S(2)}) copy-start(bf16[4,256,256]{2,1,0:T(8,128)(2,1)} %param.13) | copy-start | bytes 1572868

commit v6 on v5

v6 whole, which is shorter than its diff:
```python
import functools

import jax
import jax.numpy as jnp
from jax import lax
from jax.experimental import pallas as pl
from jax.experimental.pallas import tpu as pltpu
from jax.sharding import PartitionSpec as P

HALO = 4
LANES = 128
EDGE = 16
MESH = pl.DeviceIdType.MESH


def rolled(vec, rows):
    return pltpu.roll(jnp.broadcast_to(vec, (rows, LANES)), 0, 1, stride=1, stride_axis=0)


def conv_kernel(basis, out_rows, band_len, polar_count,
                idx_ref, wgt_ref, fields_ref, tap_ref, mix_ref, crev_ref, out_ref,
                top_c, bot_c, top_h, bot_h, own_h, polar_o, f_ref, h_ref, send_sem, recv_sem):
    cols = out_ref.shape[1]
    chans = out_ref.shape[2]
    lat = lax.axis_index("lat")
    lon = lax.axis_index("lon")
    last = lax.axis_size("lat") - 1
    has_up = lat < last
    has_down = lat > 0
    is_polar = (lat == 0) | (lat == last)
    slot = jnp.minimum(lat, 1) * (out_rows - polar_count)
    up = jnp.minimum(lat + 1, last)
    down = jnp.maximum(lat - 1, 0)
    side = 1 - lon

    barrier = pltpu.get_barrier_semaphore()

    def greet(where):
        pl.semaphore_signal(barrier, 1, device_id=where, device_id_type=MESH)

    greet({"lat": lat, "lon": side})

    @pl.when(has_up)
    def _():
        greet({"lat": up, "lon": lon})
        greet({"lat": up, "lon": side})

    @pl.when(has_down)
    def _():
        greet({"lat": down, "lon": lon})
        greet({"lat": down, "lon": side})

    pl.semaphore_wait(barrier, 1 + 2 * (has_up.astype(jnp.int32) + has_down.astype(jnp.int32)))

    def copy(n, src, dst, where):
        return pltpu.make_async_remote_copy(
            src_ref=src, dst_ref=dst, send_sem=send_sem.at[n], recv_sem=recv_sem.at[n],
            device_id=where, device_id_type=MESH)

    lo_rows = pl.ds(0, HALO)
    hi_rows = pl.ds(out_rows - HALO, HALO)
    first_cols = pl.ds(0, EDGE)
    last_cols = pl.ds(cols - EDGE, EDGE)
    c_up = copy(0, fields_ref.at[hi_rows], top_c, {"lat": up, "lon": lon})
    c_dn = copy(1, fields_ref.at[lo_rows], bot_c, {"lat": down, "lon": lon})
    h_up = [
        copy(2, fields_ref.at[hi_rows, first_cols], top_h.at[:, first_cols], {"lat": up, "lon": side}),
        copy(3, fields_ref.at[hi_rows, last_cols], top_h.at[:, last_cols], {"lat": up, "lon": side}),
    ]
    h_dn = [
        copy(4, fields_ref.at[lo_rows, first_cols], bot_h.at[:, first_cols], {"lat": down, "lon": side}),
        copy(5, fields_ref.at[lo_rows, last_cols], bot_h.at[:, last_cols], {"lat": down, "lon": side}),
    ]
    h_side = [
        copy(6, fields_ref.at[:, first_cols], own_h.at[:, first_cols], {"lat": lat, "lon": side}),
        copy(7, fields_ref.at[:, last_cols], own_h.at[:, last_cols], {"lat": lat, "lon": side}),
    ]
    pol = copy(8, fields_ref.at[pl.ds(slot, polar_count)], polar_o, {"lat": lat, "lon": side})

    for c in h_side:
        c.start()

    @pl.when(has_up)
    def _():
        c_up.start()
        for c in h_up:
            c.start()

    @pl.when(has_down)
    def _():
        c_dn.start()
        for c in h_dn:
            c.start()

    @pl.when(is_polar)
    def _():
        pol.start()

    row_id = lax.broadcasted_iota(jnp.int32, (cols, LANES), 0)
    col_id = lax.broadcasted_iota(jnp.int32, (cols, LANES), 1)
    near = jnp.abs(col_id - row_id) <= HALO
    edge_row = lax.broadcasted_iota(jnp.int32, (cols, chans), 0)
    edge_keep = (edge_row < HALO) | (edge_row >= cols - HALO)

    def filter_rows(c_ref, e_ref, count, first):
        def filter_row(r, carry):
            x = jnp.concatenate(
                [c_ref[r], jnp.where(edge_keep, e_ref[r], jnp.zeros_like(e_ref[r]))], axis=0
            )
            parts = []
            for k in range(basis):
                u = tap_ref[k, pl.ds(first + r, 1), :]
                u_hi = u.astype(jnp.bfloat16).astype(jnp.float32)
                for piece in (u_hi, u - u_hi):
                    w = rolled(piece, cols)
                    band = jnp.where(near, w, 0.0)
                    wrap = jnp.where(near, 0.0, w)
                    parts.append(jnp.concatenate([band, wrap], axis=1).astype(jnp.bfloat16))
            tall = jnp.concatenate(parts, axis=0)
            y = jnp.dot(tall, x, preferred_element_type=jnp.float32)
            for k in range(basis):
                lo = 2 * k * cols
                v = y[lo : lo + cols] + y[lo + cols : lo + 2 * cols]
                f_ref[k, first + r] = v.astype(jnp.bfloat16).astype(jnp.float32)
            return carry

        lax.fori_loop(0, count, filter_row, 0)

    def zero_rows(first):
        f_ref[:, pl.ds(first, HALO)] = jnp.zeros((basis, HALO, cols, chans), jnp.float32)

    for c in h_side:
        c.wait_recv()
    filter_rows(fields_ref, own_h, out_rows, HALO)

    @pl.when(is_polar)
    def _polar():
        pol.wait_recv()
        upper = col_id >= row_id
        for k in range(basis):
            for p in range(polar_count):
                ra = rolled(crev_ref[k, p, pl.ds(0, 1), :], cols)
                rb = rolled(crev_ref[k, p, pl.ds(1, 1), :], cols)
                circ = jnp.concatenate(
                    [jnp.where(upper, ra, rb), jnp.where(upper, rb, ra)], axis=1
                ).astype(jnp.bfloat16)
                g = jnp.concatenate([fields_ref[slot + p], polar_o[p]], axis=0)
                y = jnp.dot(circ, g, preferred_element_type=jnp.float32)
                f_ref[k, HALO + slot + p] = y.astype(jnp.bfloat16).astype(jnp.float32)

    @pl.when(has_down)
    def _():
        c_up.wait_recv()
        for c in h_up:
            c.wait_recv()
        filter_rows(top_c, top_h, HALO, 0)

    @pl.when(lat == 0)
    def _():
        zero_rows(0)

    @pl.when(has_up)
    def _():
        c_dn.wait_recv()
        for c in h_dn:
            c.wait_recv()
        filter_rows(bot_c, bot_h, HALO, HALO + out_rows)

    @pl.when(lat == last)
    def _():
        zero_rows(HALO + out_rows)

    for k in range(basis):
        def band_row(i, carry):
            acc = jnp.zeros((cols, chans), jnp.float32)
            for t in range(band_len):
                r = idx_ref[i * band_len + t]
                w = wgt_ref[(k * out_rows + i) * band_len + t]
                acc = acc + w * f_ref[k, r]
            h_ref[i, :, k * chans : (k + 1) * chans] = acc.astype(jnp.bfloat16)
            return carry

        lax.fori_loop(0, out_rows, band_row, 0)

    def mix_row(i, carry):
        mixed = jnp.dot(h_ref[i], mix_ref[...], preferred_element_type=jnp.float32)
        out_ref[i] = (fields_ref[i].astype(jnp.float32) + mixed).astype(out_ref.dtype)
        return carry

    lax.fori_loop(0, out_rows, mix_row, 0)

    for c in h_side:
        c.wait_send()

    @pl.when(has_up)
    def _():
        c_up.wait_send()
        for c in h_up:
            c.wait_send()

    @pl.when(has_down)
    def _():
        c_dn.wait_send()
        for c in h_dn:
            c.wait_send()

    @pl.when(is_polar)
    def _():
        pol.wait_send()


def shards(fields, lon_taps, lat_taps, cycle_taps, band_start, band_width, mixing):
    row_count, col_count, chan_count = fields.shape
    basis_count = lon_taps.shape[1]
    taps_count = lon_taps.shape[2]
    reach_cells = (taps_count - 1) // 2
    band_len = lat_taps.shape[2]
    polar_rows = row_count // 2
    lat_count = lax.axis_size("lat")
    lon_count = lax.axis_size("lon")
    assert lon_count == 2 and reach_cells == HALO
    cycle_len = lon_count * col_count
    lat_pos = lax.axis_index("lat")
    ext_rows = row_count + 2 * HALO
    total_rows = lat_count * row_count

    taps_padded = jnp.pad(lon_taps, ((HALO, HALO), (0, 0), (0, 0)))
    taps_here = lax.dynamic_slice_in_dim(taps_padded, lat_pos * row_count, ext_rows, 0)
    taps_here = jnp.transpose(taps_here, (1, 0, 2))
    tap_vec = jnp.concatenate(
        [
            taps_here[..., reach_cells:],
            jnp.zeros(taps_here.shape[:2] + (LANES - taps_count,), jnp.float32),
            taps_here[..., :reach_cells],
        ],
        axis=-1,
    )

    at_top = lat_pos == 0
    coef_start = jnp.where(at_top, 0, polar_rows).astype(jnp.int32)
    coef = lax.dynamic_slice_in_dim(cycle_taps, coef_start, polar_rows, 1).astype(jnp.float32)
    rev = jnp.roll(jnp.flip(coef, axis=-1), 1, axis=-1)
    crev = rev.reshape(basis_count, polar_rows, cycle_len // LANES, LANES)

    base_row = lat_pos * row_count
    steps_band = jnp.arange(band_len, dtype=jnp.int32)
    source = band_start[:, None] + steps_band[None, :]
    usable = (steps_band[None, :] < band_width[:, None]) & (source >= 0) & (source < total_rows)
    idx = jnp.clip(source - base_row + HALO, 0, ext_rows - 1).reshape(-1)
    wgt = jnp.where(usable[:, None, :], lat_taps.astype(jnp.float32), 0.0)
    wgt = jnp.transpose(wgt, (1, 0, 2)).reshape(-1)
    mix_flat = mixing.reshape(basis_count * chan_count, chan_count)

    smem = pl.BlockSpec(memory_space=pltpu.SMEM)
    vmem = pl.BlockSpec(memory_space=pltpu.VMEM)
    kernel = functools.partial(conv_kernel, basis_count, row_count, band_len, polar_rows)
    halo_block = pltpu.VMEM((HALO, col_count, chan_count), fields.dtype)
    return pl.pallas_call(
        kernel,
        out_shape=jax.ShapeDtypeStruct(fields.shape, fields.dtype),
        in_specs=[smem, smem] + [vmem] * 4,
        out_specs=vmem,
        scratch_shapes=[
            halo_block,
            halo_block,
            halo_block,
            halo_block,
            pltpu.VMEM(fields.shape, fields.dtype),
            pltpu.VMEM((polar_rows, col_count, chan_count), fields.dtype),
            pltpu.VMEM((basis_count, ext_rows, col_count, chan_count), jnp.float32),
            pltpu.VMEM((row_count, col_count, basis_count * chan_count), jnp.bfloat16),
            pltpu.SemaphoreType.DMA((9,)),
            pltpu.SemaphoreType.DMA((9,)),
        ],
        compiler_params=pltpu.CompilerParams(
            vmem_limit_bytes=48 * 1024 * 1024, collective_id=0, has_side_effects=True
        ),
    )(idx, wgt, fields, tap_vec, mix_flat, crev)


def solution(mesh):
    in_specs = (
        P(("ens", "lat"), "lon", None),
        P(),
        P("lat", None, None),
        P(),
        P("lat"),
        P("lat"),
        P(),
    )
    out_specs = P(("ens", "lat"), "lon", None)
    return jax.shard_map(shards, mesh=mesh, in_specs=in_specs, out_specs=out_specs, check_vma=False)
```

time: 26.2 us -> 27.6 us (1.053)
  Pallas kernels: 19.1 us -> 20.8 us
  local copies, waits for them, and re-layouts: 4.86 us -> 6.14 us
  starting transfers between devices: 0.76 us -> 0 us
  other arithmetic: 0.82 us -> 0.32 us
    unnamed x20, local copies, waits for them, and re-layouts: 2.34 us -> 4.87 us
    pallas_call x1, Pallas kernels: 19.1 us -> 20.8 us  [shards(): pl.pallas_call(kernel, out_shape=jax.ShapeDtypeStruct(fields.shape, field...]
    dynamic_slice x1 -> x0, local copies, waits for them, and re-layouts: 0.97 us -> none  [shards(): slot_rows = lax.dynamic_slice_in_dim(fields, slot_start, polar_rows, 0)]
    slice x5 -> x1, local copies, waits for them, and re-layouts: 0.88 us -> 0.07 us  [shards(): taps_here[..., reach_cells:]]
    ppermute x1 -> x0, starting transfers between devices: 0.76 us -> none  [shards(): got = lax.ppermute(payload, 'lon', [(0, 1), (1, 0)])]
    slice x2 -> x3, local copies, waits for them, and re-layouts: 0.08 us -> 0.7 us  [shards(): rev = jnp.roll(jnp.flip(coef, axis=-1), 1, axis=-1)]
  transfers between devices with their start and end apart: 1 -> 0, of which waited for: 0 -> 0; matrix products, arithmetic and copies ran while one was open for 5% -> 0% of each run, Pallas kernels for 0% -> 0%
where the time goes in v6:
time: 27.6 us; the launch traced here: 27.3 us
  Pallas kernels  20.8 us (75%)
  local copies, waits for them, and re-layouts  6.14 us (22%)
  other arithmetic  0.32 us (1%)
    pallas_call x1, Pallas kernels, shards(): pl.pallas_call(kernel, out_shape=jax.ShapeDtypeStruct(fields.shape, field...  20.8 us
    unnamed x20, local copies, waits for them, and re-layouts  4.87 us
    slice x3, local copies, waits for them, and re-layouts, shards(): rev = jnp.roll(jnp.flip(coef, axis=-1), 1, axis=-1)  0.7 us

profile of v6, /device:TPU:145, one launch (start us, length us, event | category | flops | bytes accessed | tf_op | source)
XLA Modules:
  0.0 27.3 jit_solution(4641443736596955545)
XLA Ops:
  0.0 0.0 copy-start.6
  0.0 0.0 copy-start.7
  0.0 0.1 pad.8.clone
  0.1 0.6 %copy-done.6 = s32[8]{0:T(128)S(1)} copy-done((s32[8]{0:T(128)S(1)}, s32[8]{0:T(128)}, u32[]{:S(2)}) %copy-start.6) | copy-done | bytes 56
  0.7 0.0 copy-done.7
  0.7 0.1 fusion.4
  0.7 0.0 copy-start.4
  0.8 0.1 copy.10
  0.8 0.1 add_clamp_fusion
  0.9 0.1 min.12.idx_ref
  1.0 0.4 %copy-done.4 = bf16[8,4,6]{0,1,2:T(4,128)(2,1)S(1)} copy-done((bf16[8,4,6]{0,1,2:T(4,128)(2,1)S(1)}, bf16[8,4,6]{0,1,2:T(4,128)(2,1)}, u32[]{:S(2)}) %copy-start.4) | copy-done | bytes 408
  1.4 0.0 copy-start.5
  1.5 0.1 copy.11
  1.6 0.1 reshape.57.wgt_ref
  1.7 0.5 %copy-done.5 = bf16[4,8,256]{2,1,0:T(8,128)(2,1)S(1)} copy-done((bf16[4,8,256]{2,1,0:T(8,128)(2,1)S(1)}, bf16[4,8,256]{2,1,0:T(8,128)(2,1)}, u32[]{:S(2)}) %copy-start.5) | copy-done | bytes 16408
  2.2 0.0 copy-start.2
  2.2 0.6 %copy-done.2 = f32[4,4,256]{2,1,0:T(4,128)} copy-done((f32[4,4,256]{2,1,0:T(4,128)}, f32[4,4,256]{2,1,0:T(4,128)S(1)}, u32[]{:S(2)}) %copy-start.2) | copy-done | bytes 16408
  2.8 0.1 slice.26
  2.9 0.2 reverse.2
  3.0 0.0 slice-start
  3.0 0.1 slice.27
  3.1 0.6 %slice-done = f32[4,4,1]{2,1,0:T(4,128)S(1)} async-done(((f32[4,4,256]{2,1,0:T(4,128)}), f32[4,4,1]{2,1,0:T(4,128)S(1)}, s32[]{:S(2)}) %slice-start) | async-done | bytes 88 | tf_op jit(solution)/shard_map/jit(_roll_static)/slice | solution.py:242
  3.7 0.0 copy-start.3
  3.8 0.1 pad_maximum_fusion.1
  3.9 0.7 %copy-done.3 = f32[256,4,9]{0,1,2:T(4,128)S(1)} copy-done((f32[256,4,9]{0,1,2:T(4,128)S(1)}, f32[256,4,9]{0,1,2:T(4,128)}, u32[]{:S(2)}) %copy-start.3) | copy-done | bytes 36888
  4.5 0.0 copy-start
  4.5 0.0 copy-start.1
  4.5 0.2 copy.12
  4.8 0.1 slice.23
  4.8 0.1 pad_maximum_fusion.tap_ref
  4.9 0.6 %copy-done = bf16[8,128,256]{2,1,0:T(8,128)(2,1)S(1)} copy-done((bf16[8,128,256]{2,1,0:T(8,128)(2,1)S(1)}, bf16[8,128,256]{2,1,0:T(8,128)(2,1)}, u32[]{:S(2)}) %copy-start) | copy-done | bytes 524312
  5.6 0.2 copy-done.1
  5.7 20.8 %shard_map.73 = bf16[8,128,256]{2,1,0:T(8,128)(2,1)S(1)} custom-call(s32[48]{0:T(128)S(1)} %min.12.idx_ref, f32[192]{0:T(256)S(1)} %reshape.57.wgt_ref, bf16[8,128,256]{2,1,0:T(8,128)(2,1)S(1)} %copy-done, f32[4,16,128]{2,1,0:T(8,128)S(1)} %pad_maximum_fusion.tap_ref, bf16[1024,256]{1,0:T(8,128)(2,1)S(1)} %bitcast.7, f32[4,4,2,128]{3,2,1,0:T(2,128)S(1)} %reshape.59.crev_ref), custom_call_target="tpu_custom_call" | custom-call | tf_op jit(solution)/shard_map/pallas_call | solution.py:258
  26.5 0.8 %copy.14 = bf16[8,128,256]{2,1,0:T(8,128)(2,1)} copy(bf16[8,128,256]{2,1,0:T(8,128)(2,1)S(1)} %shard_map.73) | data formatting | bytes 1048576
  (5 shorter events, 0.1 us)
Async XLA Ops:
  0.0 0.7 %copy-start.6 = (s32[8]{0:T(128)S(1)}, s32[8]{0:T(128)}, u32[]{:S(2)}) copy-start(s32[8]{0:T(128)} %param.11) | copy-start | bytes 100
  0.0 0.7 %copy-start.7 = (s32[8]{0:T(128)S(1)}, s32[8]{0:T(128)}, u32[]{:S(2)}) copy-start(s32[8]{0:T(128)} %param.12) | copy-start | bytes 100
  0.7 0.7 %copy-start.4 = (bf16[8,4,6]{0,1,2:T(4,128)(2,1)S(1)}, bf16[8,4,6]{0,1,2:T(4,128)(2,1)}, u32[]{:S(2)}) copy-start(bf16[8,4,6]{0,1,2:T(4,128)(2,1)} %param.9) | copy-start | bytes 1156
  1.4 0.7 %copy-start.5 = (bf16[4,8,256]{2,1,0:T(8,128)(2,1)S(1)}, bf16[4,8,256]{2,1,0:T(8,128)(2,1)}, u32[]{:S(2)}) copy-start(bf16[4,8,256]{2,1,0:T(8,128)(2,1)} %param.10) | copy-start | bytes 49156
  2.2 0.6 %copy-start.2 = (f32[4,4,256]{2,1,0:T(4,128)}, f32[4,4,256]{2,1,0:T(4,128)S(1)}, u32[]{:S(2)}) copy-start(f32[4,4,256]{2,1,0:T(4,128)S(1)} %dynamic-slice_convert_fusion) | copy-start | bytes 49156
  3.0 0.7 %slice-start = ((f32[4,4,256]{2,1,0:T(4,128)}), f32[4,4,1]{2,1,0:T(4,128)S(1)}, s32[]{:S(2)}) async-start(f32[4,4,256]{2,1,0:T(4,128)} %copy-done.2), calls=%async_computation | async-start | bytes 16384 | tf_op jit(solution)/shard_map/jit(_roll_static)/slice | solution.py:242
  3.7 0.8 %copy-start.3 = (f32[256,4,9]{0,1,2:T(4,128)S(1)}, f32[256,4,9]{0,1,2:T(4,128)}, u32[]{:S(2)}) copy-start(f32[256,4,9]{0,1,2:T(4,128)} %param.8) | copy-start | bytes 110596
  4.5 1.0 %copy-start = (bf16[8,128,256]{2,1,0:T(8,128)(2,1)S(1)}, bf16[8,128,256]{2,1,0:T(8,128)(2,1)}, u32[]{:S(2)}) copy-start(bf16[8,128,256]{2,1,0:T(8,128)(2,1)} %fields_ref.1) | copy-start | bytes 1572868
  4.5 1.2 %copy-start.1 = (bf16[4,256,256]{2,1,0:T(8,128)(2,1)S(1)}, bf16[4,256,256]{2,1,0:T(8,128)(2,1)}, u32[]{:S(2)}) copy-start(bf16[4,256,256]{2,1,0:T(8,128)(2,1)} %param.13) | copy-start | bytes 1572868

commit v7 on v6

--- a/solution.py
+++ b/solution.py
@@ -17,12 +17,26 @@
     return pltpu.roll(jnp.broadcast_to(vec, (rows, LANES)), 0, 1, stride=1, stride_axis=0)
 
 
-def conv_kernel(basis, out_rows, band_len, polar_count,
-                idx_ref, wgt_ref, fields_ref, tap_ref, mix_ref, crev_ref, out_ref,
-                top_c, bot_c, top_h, bot_h, own_h, polar_o, f_ref, h_ref, send_sem, recv_sem):
+def conv_kernel(basis, out_rows, band_len, polar_count, total_rows,
+                start_hbm, width_hbm, lat_hbm, lon_hbm, cyc_hbm, fields_hbm, mix_hbm, out_ref,
+                start_s, width_s, lat_v, tap_v, cyc_v, fields_ref, mix_ref,
+                top_c, bot_c, top_h, bot_h, own_h, polar_o, f_ref, h_ref, send_sem, recv_sem, load_sem):
     cols = out_ref.shape[1]
     chans = out_ref.shape[2]
+    ext_rows = out_rows + 2 * HALO
     lat = lax.axis_index("lat")
+    tap_first = jnp.clip(lat * out_rows - HALO, 0, total_rows - ext_rows)
+    loads = [
+        pltpu.make_async_copy(fields_hbm, fields_ref, load_sem.at[0]),
+        pltpu.make_async_copy(lon_hbm.at[pl.ds(tap_first, ext_rows)], tap_v, load_sem.at[1]),
+        pltpu.make_async_copy(start_hbm, start_s, load_sem.at[2]),
+        pltpu.make_async_copy(width_hbm, width_s, load_sem.at[3]),
+        pltpu.make_async_copy(lat_hbm, lat_v, load_sem.at[4]),
+        pltpu.make_async_copy(cyc_hbm, cyc_v, load_sem.at[5]),
+        pltpu.make_async_copy(mix_hbm, mix_ref, load_sem.at[6]),
+    ]
+    for c in loads:
+        c.start()
     lon = lax.axis_index("lon")
     last = lax.axis_size("lat") - 1
     has_up = lat < last
@@ -77,6 +91,9 @@
     ]
     pol = copy(8, fields_ref.at[pl.ds(slot, polar_count)], polar_o, {"lat": lat, "lon": side})
 
+    for c in loads:
+        c.wait()
+
     for c in h_side:
         c.start()
 
@@ -108,8 +125,14 @@
                 [c_ref[r], jnp.where(edge_keep, e_ref[r], jnp.zeros_like(e_ref[r]))], axis=0
             )
             parts = []
+            local = jnp.clip(lat * out_rows - HALO + first + r - tap_first, 0, ext_rows - 1)
+            t9 = tap_v[local]
+            t128 = jnp.concatenate(
+                [t9, jnp.zeros((basis, LANES - t9.shape[1]), jnp.float32)], axis=1
+            )
+            centred = pltpu.roll(t128, LANES - HALO, 1)
             for k in range(basis):
-                u = tap_ref[k, pl.ds(first + r, 1), :]
+                u = centred[k : k + 1]
                 u_hi = u.astype(jnp.bfloat16).astype(jnp.float32)
                 for piece in (u_hi, u - u_hi):
                     w = rolled(piece, cols)
@@ -133,20 +156,29 @@
         c.wait_recv()
     filter_rows(fields_ref, own_h, out_rows, HALO)
 
-    @pl.when(is_polar)
-    def _polar():
+    def polar_rows(pole):
         pol.wait_recv()
         upper = col_id >= row_id
         for k in range(basis):
             for p in range(polar_count):
-                ra = rolled(crev_ref[k, p, pl.ds(0, 1), :], cols)
-                rb = rolled(crev_ref[k, p, pl.ds(1, 1), :], cols)
-                circ = jnp.concatenate(
-                    [jnp.where(upper, ra, rb), jnp.where(upper, rb, ra)], axis=1
-                ).astype(jnp.bfloat16)
+                a = cyc_v[k, pl.ds(pole * polar_count + p, 1), :].astype(jnp.float32)
+                ra = rolled(a[:, :LANES], cols)
+                rb = rolled(a[:, LANES:], cols)
+                circ_t = jnp.concatenate(
+                    [jnp.where(upper, ra, rb), jnp.where(upper, rb, ra)], axis=0
+                )
+                circ = jnp.transpose(circ_t).astype(jnp.bfloat16)
                 g = jnp.concatenate([fields_ref[slot + p], polar_o[p]], axis=0)
                 y = jnp.dot(circ, g, preferred_element_type=jnp.float32)
                 f_ref[k, HALO + slot + p] = y.astype(jnp.bfloat16).astype(jnp.float32)
+
+    @pl.when(lat == 0)
+    def _():
+        polar_rows(0)
+
+    @pl.when(lat == last)
+    def _():
+        polar_rows(1)
 
     @pl.when(has_down)
     def _():
@@ -170,17 +202,26 @@
     def _():
         zero_rows(HALO + out_rows)
 
-    for k in range(basis):
-        def band_row(i, carry):
+    base_row = lat * out_rows
+
+    def band_row(i, carry):
+        lw = lat_v[i].astype(jnp.float32)
+        begin = start_s[i]
+        width = width_s[i]
+        rows = []
+        for t in range(band_len):
+            source = begin + t
+            ok = (t < width) & (source >= 0) & (source < total_rows)
+            rows.append((ok, jnp.clip(source - base_row + HALO, 0, ext_rows - 1)))
+        for k in range(basis):
             acc = jnp.zeros((cols, chans), jnp.float32)
-            for t in range(band_len):
-                r = idx_ref[i * band_len + t]
-                w = wgt_ref[(k * out_rows + i) * band_len + t]
+            for t, (ok, r) in enumerate(rows):
+                w = jnp.where(ok, lw[k : k + 1, t : t + 1], 0.0)
                 acc = acc + w * f_ref[k, r]
             h_ref[i, :, k * chans : (k + 1) * chans] = acc.astype(jnp.bfloat16)
-            return carry
-
-        lax.fori_loop(0, out_rows, band_row, 0)
+        return carry
+
+    lax.fori_loop(0, out_rows, band_row, 0)
 
     def mix_row(i, carry):
         mixed = jnp.dot(h_ref[i], mix_ref[...], preferred_element_type=jnp.float32)
@@ -224,43 +265,26 @@
     ext_rows = row_count + 2 * HALO
     total_rows = lat_count * row_count
 
-    taps_padded = jnp.pad(lon_taps, ((HALO, HALO), (0, 0), (0, 0)))
-    taps_here = lax.dynamic_slice_in_dim(taps_padded, lat_pos * row_count, ext_rows, 0)
-    taps_here = jnp.transpose(taps_here, (1, 0, 2))
-    tap_vec = jnp.concatenate(
-        [
-            taps_here[..., reach_cells:],
-            jnp.zeros(taps_here.shape[:2] + (LANES - taps_count,), jnp.float32),
-            taps_here[..., :reach_cells],
-        ],
-        axis=-1,
+    mix_flat = mixing.reshape(basis_count * chan_count, chan_count)
+
+    hbm = pl.BlockSpec(memory_space=pl.ANY)
+    kernel = functools.partial(
+        conv_kernel, basis_count, row_count, band_len, polar_rows, total_rows
     )
-
-    at_top = lat_pos == 0
-    coef_start = jnp.where(at_top, 0, polar_rows).astype(jnp.int32)
-    coef = lax.dynamic_slice_in_dim(cycle_taps, coef_start, polar_rows, 1).astype(jnp.float32)
-    rev = jnp.roll(jnp.flip(coef, axis=-1), 1, axis=-1)
-    crev = rev.reshape(basis_count, polar_rows, cycle_len // LANES, LANES)
-
-    base_row = lat_pos * row_count
-    steps_band = jnp.arange(band_len, dtype=jnp.int32)
-    source = band_start[:, None] + steps_band[None, :]
-    usable = (steps_band[None, :] < band_width[:, None]) & (source >= 0) & (source < total_rows)
-    idx = jnp.clip(source - base_row + HALO, 0, ext_rows - 1).reshape(-1)
-    wgt = jnp.where(usable[:, None, :], lat_taps.astype(jnp.float32), 0.0)
-    wgt = jnp.transpose(wgt, (1, 0, 2)).reshape(-1)
-    mix_flat = mixing.reshape(basis_count * chan_count, chan_count)
-
-    smem = pl.BlockSpec(memory_space=pltpu.SMEM)
-    vmem = pl.BlockSpec(memory_space=pltpu.VMEM)
-    kernel = functools.partial(conv_kernel, basis_count, row_count, band_len, polar_rows)
     halo_block = pltpu.VMEM((HALO, col_count, chan_count), fields.dtype)
     return pl.pallas_call(
         kernel,
         out_shape=jax.ShapeDtypeStruct(fields.shape, fields.dtype),
-        in_specs=[smem, smem] + [vmem] * 4,
-        out_specs=vmem,
+        in_specs=[hbm] * 7,
+        out_specs=pl.BlockSpec(memory_space=pltpu.VMEM),
         scratch_shapes=[
+            pltpu.SMEM(band_start.shape, band_start.dtype),
+            pltpu.SMEM(band_width.shape, band_width.dtype),
+            pltpu.VMEM(lat_taps.shape, lat_taps.dtype),
+            pltpu.VMEM((ext_rows,) + lon_taps.shape[1:], lon_taps.dtype),
+            pltpu.VMEM(cycle_taps.shape, cycle_taps.dtype),
+            pltpu.VMEM(fields.shape, fields.dtype),
+            pltpu.VMEM(mix_flat.shape, mix_flat.dtype),
             halo_block,
             halo_block,
             halo_block,
@@ -271,11 +295,12 @@
             pltpu.VMEM((row_count, col_count, basis_count * chan_count), jnp.bfloat16),
             pltpu.SemaphoreType.DMA((9,)),
             pltpu.SemaphoreType.DMA((9,)),
+            pltpu.SemaphoreType.DMA((7,)),
         ],
         compiler_params=pltpu.CompilerParams(
-            vmem_limit_bytes=48 * 1024 * 1024, collective_id=0, has_side_effects=True
+            vmem_limit_bytes=67043328, collective_id=0, has_side_effects=True
         ),
-    )(idx, wgt, fields, tap_vec, mix_flat, crev)
+    )(band_start, band_width, lat_taps, lon_taps, cycle_taps, fields, mix_flat)
 
 
 def solution(mesh):

time: 27.6 us -> 28.2 us (1.022)
  Pallas kernels: 20.8 us -> 22.9 us
  local copies, waits for them, and re-layouts: 6.14 us -> 5.04 us
  other arithmetic: 0.32 us -> 0 us
    pallas_call x1, Pallas kernels: 20.8 us -> 22.9 us  [shards(): pl.pallas_call(kernel, out_shape=jax.ShapeDtypeStruct(fields.shape, field...]
    slice x4 -> x0, local copies, waits for them, and re-layouts: 0.78 us -> none  [the longest x3 0.7 us: shards(): rev = jnp.roll(jnp.flip(coef, axis=-1), 1, axis=-1)]
    unnamed x20 -> x3, local copies, waits for them, and re-layouts: 4.87 us -> 5.04 us
where the time goes in v7:
time: 28.2 us; the launch traced here: 28 us
  Pallas kernels  22.9 us (81%)
  local copies, waits for them, and re-layouts  5.04 us (18%)
    pallas_call x1, Pallas kernels, shards(): pl.pallas_call(kernel, out_shape=jax.ShapeDtypeStruct(fields.shape, field...  22.9 us
    unnamed x3, local copies, waits for them, and re-layouts  5.04 us

profile of v7, /device:TPU:145, one launch (start us, length us, event | category | flops | bytes accessed | tf_op | source)
XLA Modules:
  0.0 28.0 jit_solution(2330443866566579788)
XLA Ops:
  0.0 1.4 %copy.8.lat_hbm = bf16[8,4,6]{2,1,0:T(4,128)(2,1)} copy(bf16[8,4,6]{0,1,2:T(4,128)(2,1)} %param.9) | data formatting | bytes 768 | tf_op args[2]
  1.4 1.8 %copy.9.lon_hbm = f32[256,4,9]{2,1,0:T(4,128)} copy(f32[256,4,9]{0,1,2:T(4,128)} %param.8) | data formatting | bytes 73728 | tf_op args[1]
  3.2 22.9 %shard_map.73 = bf16[8,128,256]{2,1,0:T(8,128)(2,1)} custom-call(s32[8]{0:T(128)} %start_hbm.1, s32[8]{0:T(128)} %width_hbm.1, bf16[8,4,6]{2,1,0:T(4,128)(2,1)} %copy.8.lat_hbm, f32[256,4,9]{2,1,0:T(4,128)} %copy.9.lon_hbm, bf16[4,8,256]{2,1,0:T(8,128)(2,1)} %cyc_hbm.1, bf16[8,128,256]{2,1,0:T(8,128)(2,1)} %fields_hbm.1, bf16[1024,256]{1,0:T(8,128)(2,1)} %bitcast.1), custom_call_target="tpu_custom_call" | custom-call | tf_op jit(solution)/shard_map/pallas_call | solution.py:275
  26.1 1.9 %copy.11 = bf16[8,128,256]{2,1,0:T(8,128)(2,1)} copy(bf16[8,128,256]{2,1,0:T(8,128)(2,1)} %shard_map.73) | data formatting | bytes 1048576

commit v8 on v7

--- a/solution.py
+++ b/solution.py
@@ -47,6 +47,10 @@
     down = jnp.maximum(lat - 1, 0)
     side = 1 - lon
 
+    middle = pl.ds(EDGE, cols - 2 * EDGE)
+    for buf in (top_h, bot_h, own_h):
+        buf[:, middle] = jnp.zeros((buf.shape[0], cols - 2 * EDGE, chans), buf.dtype)
+
     barrier = pltpu.get_barrier_semaphore()
 
     def greet(where):
@@ -75,24 +79,21 @@
     hi_rows = pl.ds(out_rows - HALO, HALO)
     first_cols = pl.ds(0, EDGE)
     last_cols = pl.ds(cols - EDGE, EDGE)
-    c_up = copy(0, fields_ref.at[hi_rows], top_c, {"lat": up, "lon": lon})
-    c_dn = copy(1, fields_ref.at[lo_rows], bot_c, {"lat": down, "lon": lon})
+    c_up = copy(0, fields_hbm.at[hi_rows], top_c, {"lat": up, "lon": lon})
+    c_dn = copy(1, fields_hbm.at[lo_rows], bot_c, {"lat": down, "lon": lon})
     h_up = [
-        copy(2, fields_ref.at[hi_rows, first_cols], top_h.at[:, first_cols], {"lat": up, "lon": side}),
-        copy(3, fields_ref.at[hi_rows, last_cols], top_h.at[:, last_cols], {"lat": up, "lon": side}),
+        copy(2, fields_hbm.at[hi_rows, first_cols], top_h.at[:, first_cols], {"lat": up, "lon": side}),
+        copy(3, fields_hbm.at[hi_rows, last_cols], top_h.at[:, last_cols], {"lat": up, "lon": side}),
     ]
     h_dn = [
-        copy(4, fields_ref.at[lo_rows, first_cols], bot_h.at[:, first_cols], {"lat": down, "lon": side}),
-        copy(5, fields_ref.at[lo_rows, last_cols], bot_h.at[:, last_cols], {"lat": down, "lon": side}),
+        copy(4, fields_hbm.at[lo_rows, first_cols], bot_h.at[:, first_cols], {"lat": down, "lon": side}),
+        copy(5, fields_hbm.at[lo_rows, last_cols], bot_h.at[:, last_cols], {"lat": down, "lon": side}),
     ]
     h_side = [
-        copy(6, fields_ref.at[:, first_cols], own_h.at[:, first_cols], {"lat": lat, "lon": side}),
-        copy(7, fields_ref.at[:, last_cols], own_h.at[:, last_cols], {"lat": lat, "lon": side}),
+        copy(6, fields_hbm.at[:, first_cols], own_h.at[:, first_cols], {"lat": lat, "lon": side}),
+        copy(7, fields_hbm.at[:, last_cols], own_h.at[:, last_cols], {"lat": lat, "lon": side}),
     ]
-    pol = copy(8, fields_ref.at[pl.ds(slot, polar_count)], polar_o, {"lat": lat, "lon": side})
-
-    for c in loads:
-        c.wait()
+    pol = copy(8, fields_hbm.at[pl.ds(slot, polar_count)], polar_o, {"lat": lat, "lon": side})
 
     for c in h_side:
         c.start()
@@ -116,34 +117,45 @@
     row_id = lax.broadcasted_iota(jnp.int32, (cols, LANES), 0)
     col_id = lax.broadcasted_iota(jnp.int32, (cols, LANES), 1)
     near = jnp.abs(col_id - row_id) <= HALO
-    edge_row = lax.broadcasted_iota(jnp.int32, (cols, chans), 0)
-    edge_keep = (edge_row < HALO) | (edge_row >= cols - HALO)
+
+    near_edge = jnp.concatenate([near[:8], near[cols - 8 :]], axis=0)
 
     def filter_rows(c_ref, e_ref, count, first):
         def filter_row(r, carry):
-            x = jnp.concatenate(
-                [c_ref[r], jnp.where(edge_keep, e_ref[r], jnp.zeros_like(e_ref[r]))], axis=0
-            )
-            parts = []
+            xc = c_ref[r]
+            xe = e_ref[r]
+            rhs_c = jnp.concatenate([xc, xc], axis=0)
+            rhs_e = jnp.concatenate([xe, xe], axis=0)
             local = jnp.clip(lat * out_rows - HALO + first + r - tap_first, 0, ext_rows - 1)
             t9 = tap_v[local]
             t128 = jnp.concatenate(
                 [t9, jnp.zeros((basis, LANES - t9.shape[1]), jnp.float32)], axis=1
             )
             centred = pltpu.roll(t128, LANES - HALO, 1)
+            main, corr = [], []
             for k in range(basis):
                 u = centred[k : k + 1]
                 u_hi = u.astype(jnp.bfloat16).astype(jnp.float32)
-                for piece in (u_hi, u - u_hi):
-                    w = rolled(piece, cols)
-                    band = jnp.where(near, w, 0.0)
-                    wrap = jnp.where(near, 0.0, w)
-                    parts.append(jnp.concatenate([band, wrap], axis=1).astype(jnp.bfloat16))
-            tall = jnp.concatenate(parts, axis=0)
-            y = jnp.dot(tall, x, preferred_element_type=jnp.float32)
+                w_hi = rolled(u_hi, cols)
+                w_lo = rolled(u - u_hi, cols)
+                main.append(
+                    jnp.concatenate(
+                        [jnp.where(near, w_hi, 0.0), jnp.where(near, w_lo, 0.0)], axis=1
+                    ).astype(jnp.bfloat16)
+                )
+                e_hi = jnp.concatenate([w_hi[:8], w_hi[cols - 8 :]], axis=0)
+                e_lo = jnp.concatenate([w_lo[:8], w_lo[cols - 8 :]], axis=0)
+                corr.append(
+                    jnp.concatenate(
+                        [jnp.where(near_edge, 0.0, e_hi), jnp.where(near_edge, 0.0, e_lo)], axis=1
+                    ).astype(jnp.bfloat16)
+                )
+            y = jnp.dot(jnp.concatenate(main, axis=0), rhs_c, preferred_element_type=jnp.float32)
+            yc = jnp.dot(jnp.concatenate(corr, axis=0), rhs_e, preferred_element_type=jnp.float32)
             for k in range(basis):
-                lo = 2 * k * cols
-                v = y[lo : lo + cols] + y[lo + cols : lo + 2 * cols]
+                v = y[k * cols : (k + 1) * cols]
+                c = yc[k * 16 : (k + 1) * 16]
+                v = jnp.concatenate([v[:8] + c[:8], v[8 : cols - 8], v[cols - 8 :] + c[8:]], axis=0)
                 f_ref[k, first + r] = v.astype(jnp.bfloat16).astype(jnp.float32)
             return carry
 
@@ -152,9 +164,13 @@
     def zero_rows(first):
         f_ref[:, pl.ds(first, HALO)] = jnp.zeros((basis, HALO, cols, chans), jnp.float32)
 
+    for n in (0, 1):
+        loads[n].wait()
     for c in h_side:
         c.wait_recv()
     filter_rows(fields_ref, own_h, out_rows, HALO)
+
+    loads[5].wait()
 
     def polar_rows(pole):
         pol.wait_recv()
@@ -202,6 +218,8 @@
     def _():
         zero_rows(HALO + out_rows)
 
+    for n in (2, 3, 4, 6):
+        loads[n].wait()
     base_row = lat * out_rows
 
     def band_row(i, carry):
@@ -223,12 +241,14 @@
 
     lax.fori_loop(0, out_rows, band_row, 0)
 
-    def mix_row(i, carry):
-        mixed = jnp.dot(h_ref[i], mix_ref[...], preferred_element_type=jnp.float32)
-        out_ref[i] = (fields_ref[i].astype(jnp.float32) + mixed).astype(out_ref.dtype)
-        return carry
-
-    lax.fori_loop(0, out_rows, mix_row, 0)
+    flat = (out_rows * cols, chans)
+    mixed = jnp.dot(
+        h_ref[...].reshape(out_rows * cols, basis * chans), mix_ref[...],
+        preferred_element_type=jnp.float32,
+    )
+    out_ref[...] = (fields_ref[...].astype(jnp.float32).reshape(flat) + mixed).astype(
+        out_ref.dtype
+    ).reshape(out_ref.shape)
 
     for c in h_side:
         c.wait_send()

time: 28.2 us -> 26.8 us (0.950)
  Pallas kernels: 22.9 us -> 21.5 us
    pallas_call x1, Pallas kernels: 22.9 us -> 21.5 us  [shards(): pl.pallas_call(kernel, out_shape=jax.ShapeDtypeStruct(fields.shape, field...]
where the time goes in v8:
time: 26.8 us; the launch traced here: 26.6 us
  Pallas kernels  21.5 us (80%)
  local copies, waits for them, and re-layouts  5.04 us (19%)
    pallas_call x1, Pallas kernels, shards(): pl.pallas_call(kernel, out_shape=jax.ShapeDtypeStruct(fields.shape, field...  21.5 us
    unnamed x3, local copies, waits for them, and re-layouts  5.04 us

profile of v8, /device:TPU:145, one launch (start us, length us, event | category | flops | bytes accessed | tf_op | source)
XLA Modules:
  0.0 26.6 jit_solution(4144467533691416630)
XLA Ops:
  0.0 1.4 %copy.8.lat_hbm = bf16[8,4,6]{2,1,0:T(4,128)(2,1)} copy(bf16[8,4,6]{0,1,2:T(4,128)(2,1)} %param.9) | data formatting | bytes 768 | tf_op args[2]
  1.4 1.8 %copy.9.lon_hbm = f32[256,4,9]{2,1,0:T(4,128)} copy(f32[256,4,9]{0,1,2:T(4,128)} %param.8) | data formatting | bytes 73728 | tf_op args[1]
  3.2 21.5 %shard_map.73 = bf16[8,128,256]{2,1,0:T(8,128)(2,1)} custom-call(s32[8]{0:T(128)} %start_hbm.1, s32[8]{0:T(128)} %width_hbm.1, bf16[8,4,6]{2,1,0:T(4,128)(2,1)} %copy.8.lat_hbm, f32[256,4,9]{2,1,0:T(4,128)} %copy.9.lon_hbm, bf16[4,8,256]{2,1,0:T(8,128)(2,1)} %cyc_hbm.1, bf16[8,128,256]{2,1,0:T(8,128)(2,1)} %fields_hbm.1, bf16[1024,256]{1,0:T(8,128)(2,1)} %bitcast.1), custom_call_target="tpu_custom_call" | custom-call | tf_op jit(solution)/shard_map/pallas_call | solution.py:295
  24.7 1.9 %copy.11 = bf16[8,128,256]{2,1,0:T(8,128)(2,1)} copy(bf16[8,128,256]{2,1,0:T(8,128)(2,1)} %shard_map.73) | data formatting | bytes 1048576

commit v9 on v8

--- a/solution.py
+++ b/solution.py
@@ -318,7 +318,7 @@
             pltpu.SemaphoreType.DMA((7,)),
         ],
         compiler_params=pltpu.CompilerParams(
-            vmem_limit_bytes=67043328, collective_id=0, has_side_effects=True
+            vmem_limit_bytes=40 * 1024 * 1024, collective_id=0, has_side_effects=True
         ),
     )(band_start, band_width, lat_taps, lon_taps, cycle_taps, fields, mix_flat)
 

time: 26.8 us -> 24.7 us (0.922)
  local copies, waits for them, and re-layouts: 5.04 us -> 3.76 us
  Pallas kernels: 21.5 us -> 20.7 us
    unnamed x3 -> x13, local copies, waits for them, and re-layouts: 5.04 us -> 3.76 us
    pallas_call x1, Pallas kernels: 21.5 us -> 20.7 us  [shards(): pl.pallas_call(kernel, out_shape=jax.ShapeDtypeStruct(fields.shape, field...]
where the time goes in v9:
time: 24.7 us; the launch traced here: 24.5 us
  Pallas kernels  20.7 us (84%)
  local copies, waits for them, and re-layouts  3.76 us (15%)
    pallas_call x1, Pallas kernels, shards(): pl.pallas_call(kernel, out_shape=jax.ShapeDtypeStruct(fields.shape, field...  20.7 us
    unnamed x13, local copies, waits for them, and re-layouts  3.76 us

profile of v9, /device:TPU:145, one launch (start us, length us, event | category | flops | bytes accessed | tf_op | source)
XLA Modules:
  0.0 24.5 jit_solution(3464421756857195638)
XLA Ops:
  0.0 0.0 copy-start
  0.0 0.9 %copy.8.lat_hbm = bf16[8,4,6]{2,1,0:T(4,128)(2,1)S(1)} copy(bf16[8,4,6]{0,1,2:T(4,128)(2,1)} %param.9) | data formatting | bytes 768 | tf_op args[2]
  0.9 0.0 copy-start.2
  0.9 0.0 copy-start.3
  0.9 0.0 copy-start.4
  0.9 1.1 %copy.9.lon_hbm = f32[256,4,9]{2,1,0:T(4,128)S(1)} copy(f32[256,4,9]{0,1,2:T(4,128)} %param.8) | data formatting | bytes 73728 | tf_op args[1]
  1.9 0.0 copy-done
  1.9 0.0 copy-done.2
  2.0 0.0 copy-done.3
  2.0 0.0 copy-done.4
  2.0 0.0 copy-start.1
  2.0 1.0 %copy-done.1 = bf16[4,256,256]{2,1,0:T(8,128)(2,1)S(1)} copy-done((bf16[4,256,256]{2,1,0:T(8,128)(2,1)S(1)}, bf16[4,256,256]{2,1,0:T(8,128)(2,1)}, u32[]{:S(2)}) %copy-start.1) | copy-done | bytes 524312
  3.0 20.7 %shard_map.73 = bf16[8,128,256]{2,1,0:T(8,128)(2,1)S(1)} custom-call(s32[8]{0:T(128)S(1)} %copy-done.3, s32[8]{0:T(128)S(1)} %copy-done.4, bf16[8,4,6]{2,1,0:T(4,128)(2,1)S(1)} %copy.8.lat_hbm, f32[256,4,9]{2,1,0:T(4,128)S(1)} %copy.9.lon_hbm, bf16[4,8,256]{2,1,0:T(8,128)(2,1)S(1)} %copy-done.2, bf16[8,128,256]{2,1,0:T(8,128)(2,1)S(1)} %copy-done, ...), custom_call_target="tpu_custom_call" | custom-call | tf_op jit(solution)/shard_map/pallas_call | solution.py:295
  23.7 0.8 %copy.11 = bf16[8,128,256]{2,1,0:T(8,128)(2,1)} copy(bf16[8,128,256]{2,1,0:T(8,128)(2,1)S(1)} %shard_map.73) | data formatting | bytes 1048576
Async XLA Ops:
  0.0 1.9 %copy-start = (bf16[8,128,256]{2,1,0:T(8,128)(2,1)S(1)}, bf16[8,128,256]{2,1,0:T(8,128)(2,1)}, u32[]{:S(2)}) copy-start(bf16[8,128,256]{2,1,0:T(8,128)(2,1)} %fields_hbm.1) | copy-start | bytes 1572868
  0.9 1.1 %copy-start.2 = (bf16[4,8,256]{2,1,0:T(8,128)(2,1)S(1)}, bf16[4,8,256]{2,1,0:T(8,128)(2,1)}, u32[]{:S(2)}) copy-start(bf16[4,8,256]{2,1,0:T(8,128)(2,1)} %cyc_hbm.1) | copy-start | bytes 49156
  0.9 1.1 %copy-start.3 = (s32[8]{0:T(128)S(1)}, s32[8]{0:T(128)}, u32[]{:S(2)}) copy-start(s32[8]{0:T(128)} %start_hbm.1) | copy-start | bytes 100
  0.9 1.1 %copy-start.4 = (s32[8]{0:T(128)S(1)}, s32[8]{0:T(128)}, u32[]{:S(2)}) copy-start(s32[8]{0:T(128)} %width_hbm.1) | copy-start | bytes 100
  2.0 1.0 %copy-start.1 = (bf16[4,256,256]{2,1,0:T(8,128)(2,1)S(1)}, bf16[4,256,256]{2,1,0:T(8,128)(2,1)}, u32[]{:S(2)}) copy-start(bf16[4,256,256]{2,1,0:T(8,128)(2,1)} %param.13) | copy-start | bytes 1572868

commit v10 on v8

--- a/solution.py
+++ b/solution.py
@@ -19,16 +19,15 @@
 
 def conv_kernel(basis, out_rows, band_len, polar_count, total_rows,
                 start_hbm, width_hbm, lat_hbm, lon_hbm, cyc_hbm, fields_hbm, mix_hbm, out_ref,
-                start_s, width_s, lat_v, tap_v, cyc_v, fields_ref, mix_ref,
+                start_s, width_s, lat_v, tap_v, tap_u, cyc_v, fields_ref, mix_ref,
                 top_c, bot_c, top_h, bot_h, own_h, polar_o, f_ref, h_ref, send_sem, recv_sem, load_sem):
     cols = out_ref.shape[1]
     chans = out_ref.shape[2]
     ext_rows = out_rows + 2 * HALO
     lat = lax.axis_index("lat")
-    tap_first = jnp.clip(lat * out_rows - HALO, 0, total_rows - ext_rows)
     loads = [
         pltpu.make_async_copy(fields_hbm, fields_ref, load_sem.at[0]),
-        pltpu.make_async_copy(lon_hbm.at[pl.ds(tap_first, ext_rows)], tap_v, load_sem.at[1]),
+        pltpu.make_async_copy(lon_hbm, tap_v, load_sem.at[1]),
         pltpu.make_async_copy(start_hbm, start_s, load_sem.at[2]),
         pltpu.make_async_copy(width_hbm, width_s, load_sem.at[3]),
         pltpu.make_async_copy(lat_hbm, lat_v, load_sem.at[4]),
@@ -126,12 +125,7 @@
             xe = e_ref[r]
             rhs_c = jnp.concatenate([xc, xc], axis=0)
             rhs_e = jnp.concatenate([xe, xe], axis=0)
-            local = jnp.clip(lat * out_rows - HALO + first + r - tap_first, 0, ext_rows - 1)
-            t9 = tap_v[local]
-            t128 = jnp.concatenate(
-                [t9, jnp.zeros((basis, LANES - t9.shape[1]), jnp.float32)], axis=1
-            )
-            centred = pltpu.roll(t128, LANES - HALO, 1)
+            centred = tap_u[:, first + r]
             main, corr = [], []
             for k in range(basis):
                 u = centred[k : k + 1]
@@ -166,6 +160,15 @@
 
     for n in (0, 1):
         loads[n].wait()
+    taps_count = tap_v.shape[0]
+    shift = lax.rem(total_rows - (lat * out_rows - HALO) + total_rows, total_rows)
+    for k in range(basis):
+        a = tap_v[:, k, :]
+        a = jnp.concatenate([a, jnp.zeros((2 * 8 - taps_count, total_rows), jnp.float32)], axis=0)
+        a = pltpu.roll(a, shift, 1)[:, :LANES]
+        a = jnp.transpose(a)
+        a = jnp.concatenate([a, jnp.zeros((LANES, LANES - 2 * 8), jnp.float32)], axis=1)
+        tap_u[k] = pltpu.roll(a, LANES - HALO, 1)[:ext_rows]
     for c in h_side:
         c.wait_recv()
     filter_rows(fields_ref, own_h, out_rows, HALO)
@@ -222,8 +225,8 @@
         loads[n].wait()
     base_row = lat * out_rows
 
-    def band_row(i, carry):
-        lw = lat_v[i].astype(jnp.float32)
+    lw_all = lat_v[...].astype(jnp.float32)
+    for i in range(out_rows):
         begin = start_s[i]
         width = width_s[i]
         rows = []
@@ -234,12 +237,9 @@
         for k in range(basis):
             acc = jnp.zeros((cols, chans), jnp.float32)
             for t, (ok, r) in enumerate(rows):
-                w = jnp.where(ok, lw[k : k + 1, t : t + 1], 0.0)
+                w = jnp.where(ok, lw_all[t, k : k + 1, i : i + 1], 0.0)
                 acc = acc + w * f_ref[k, r]
             h_ref[i, :, k * chans : (k + 1) * chans] = acc.astype(jnp.bfloat16)
-        return carry
-
-    lax.fori_loop(0, out_rows, band_row, 0)
 
     flat = (out_rows * cols, chans)
     mixed = jnp.dot(
@@ -286,6 +286,8 @@
     total_rows = lat_count * row_count
 
     mix_flat = mixing.reshape(basis_count * chan_count, chan_count)
+    lon_t = jnp.transpose(lon_taps, (2, 1, 0))
+    lat_t = jnp.transpose(lat_taps, (2, 1, 0))
 
     hbm = pl.BlockSpec(memory_space=pl.ANY)
     kernel = functools.partial(
@@ -295,13 +297,14 @@
     return pl.pallas_call(
         kernel,
         out_shape=jax.ShapeDtypeStruct(fields.shape, fields.dtype),
-        in_specs=[hbm] * 7,
+        in_specs=[hbm] * 6 + [pl.BlockSpec(memory_space=pltpu.HBM)],
         out_specs=pl.BlockSpec(memory_space=pltpu.VMEM),
         scratch_shapes=[
             pltpu.SMEM(band_start.shape, band_start.dtype),
             pltpu.SMEM(band_width.shape, band_width.dtype),
-            pltpu.VMEM(lat_taps.shape, lat_taps.dtype),
-            pltpu.VMEM((ext_rows,) + lon_taps.shape[1:], lon_taps.dtype),
+            pltpu.VMEM(lat_t.shape, lat_t.dtype),
+            pltpu.VMEM(lon_t.shape, lon_t.dtype),
+            pltpu.VMEM((basis_count, ext_rows, LANES), jnp.float32),
             pltpu.VMEM(cycle_taps.shape, cycle_taps.dtype),
             pltpu.VMEM(fields.shape, fields.dtype),
             pltpu.VMEM(mix_flat.shape, mix_flat.dtype),
@@ -320,7 +323,7 @@
         compiler_params=pltpu.CompilerParams(
             vmem_limit_bytes=67043328, collective_id=0, has_side_effects=True
         ),
-    )(band_start, band_width, lat_taps, lon_taps, cycle_taps, fields, mix_flat)
+    )(band_start, band_width, lat_t, lon_t, cycle_taps, fields, mix_flat)
 
 
 def solution(mesh):

time: 26.8 us -> 21 us (0.78)
  local copies, waits for them, and re-layouts: 5.04 us -> 1.87 us
  Pallas kernels: 21.5 us -> 19 us
    unnamed x3 -> x1, local copies, waits for them, and re-layouts: 5.04 us -> 1.87 us
    pallas_call x1, Pallas kernels: 21.5 us -> 19 us  [shards(): pl.pallas_call(kernel, out_shape=jax.ShapeDtypeStruct(fields.shape, field...]
where the time goes in v10:
time: 21 us; the launch traced here: 20.9 us
  Pallas kernels  19 us (90%)
  local copies, waits for them, and re-layouts  1.87 us (9%)
    pallas_call x1, Pallas kernels, shards(): pl.pallas_call(kernel, out_shape=jax.ShapeDtypeStruct(fields.shape, field...  19 us
    unnamed x1, local copies, waits for them, and re-layouts  1.87 us

profile of v10, /device:TPU:145, one launch (start us, length us, event | category | flops | bytes accessed | tf_op | source)
XLA Modules:
  0.0 20.9 jit_solution(17560164690414896872)
XLA Ops:
  0.0 19.0 %shard_map.73 = bf16[8,128,256]{2,1,0:T(8,128)(2,1)} custom-call(s32[8]{0:T(128)} %start_hbm.1, s32[8]{0:T(128)} %width_hbm.1, bf16[6,4,8]{2,1,0:T(4,128)(2,1)} %bitcast.5, f32[9,4,256]{2,1,0:T(4,128)} %bitcast.4, bf16[4,8,256]{2,1,0:T(8,128)(2,1)} %cyc_hbm.1, bf16[8,128,256]{2,1,0:T(8,128)(2,1)} %fields_hbm.1, bf16[1024,256]{1,0:T(8,128)(2,1)} %bitcast.3), custom_call_target="tpu_custom_call" | custom-call | tf_op jit(solution)/shard_map/pallas_call | solution.py:297
  19.0 1.9 %copy.9 = bf16[8,128,256]{2,1,0:T(8,128)(2,1)} copy(bf16[8,128,256]{2,1,0:T(8,128)(2,1)} %shard_map.73) | data formatting | bytes 1048576

commit v11 on v10

--- a/solution.py
+++ b/solution.py
@@ -20,7 +20,8 @@
 def conv_kernel(basis, out_rows, band_len, polar_count, total_rows,
                 start_hbm, width_hbm, lat_hbm, lon_hbm, cyc_hbm, fields_hbm, mix_hbm, out_ref,
                 start_s, width_s, lat_v, tap_v, tap_u, cyc_v, fields_ref, mix_ref,
-                top_c, bot_c, top_h, bot_h, own_h, polar_o, f_ref, h_ref, send_sem, recv_sem, load_sem):
+                top_c, bot_c, top_h, bot_h, own_h, polar_o, f_ref, acc_ref, h_ref,
+                send_sem, recv_sem, load_sem):
     cols = out_ref.shape[1]
     chans = out_ref.shape[2]
     ext_rows = out_rows + 2 * HALO
@@ -199,6 +200,57 @@
     def _():
         polar_rows(1)
 
+    for n in (2, 3, 4, 6):
+        loads[n].wait()
+    base_row = lat * out_rows
+    lw_all = lat_v[...].astype(jnp.float32)
+    terms = []
+    for i in range(out_rows):
+        begin = start_s[i]
+        width = width_s[i]
+        row_terms = []
+        for t in range(band_len):
+            source = begin + t
+            ok = (t < width) & (source >= 0) & (source < total_rows)
+            r = jnp.clip(source - base_row + HALO, 0, ext_rows - 1)
+            row_terms.append((ok, r))
+        terms.append(row_terms)
+
+    def weight(i, k, t, keep):
+        ok, r = terms[i][t]
+        return jnp.where(ok & keep(r), lw_all[t, k : k + 1, i : i + 1], 0.0)
+
+    def own(r):
+        return (r >= HALO) & (r < HALO + out_rows)
+
+    for i in range(out_rows):
+        for k in range(basis):
+            acc = jnp.zeros((cols, chans), jnp.float32)
+            for t in range(band_len):
+                r = jnp.clip(terms[i][t][1], HALO, HALO + out_rows - 1)
+                acc = acc + weight(i, k, t, own) * f_ref[k, r]
+            acc_ref[i, k] = acc
+
+    def finish(rows, steps, keep):
+        for i in rows:
+            for k in range(basis):
+                acc = acc_ref[i, k]
+                for t in steps(i):
+                    acc = acc + weight(i, k, t, keep) * f_ref[k, terms[i][t][1]]
+                h_ref[i, :, k * chans : (k + 1) * chans] = acc.astype(jnp.bfloat16)
+        first, count = rows[0], len(rows)
+        flat = (count * cols, chans)
+        mixed = jnp.dot(
+            h_ref[pl.ds(first, count)].reshape(count * cols, basis * chans), mix_ref[...],
+            preferred_element_type=jnp.float32,
+        )
+        own_rows = fields_ref[pl.ds(first, count)].astype(jnp.float32).reshape(flat)
+        out_ref[pl.ds(first, count)] = (own_rows + mixed).astype(out_ref.dtype).reshape(
+            (count, cols, chans)
+        )
+
+    half = out_rows // 2
+
     @pl.when(has_down)
     def _():
         c_up.wait_recv()
@@ -210,6 +262,8 @@
     def _():
         zero_rows(0)
 
+    finish(list(range(half)), lambda i: range(0, HALO - i), lambda r: r < HALO)
+
     @pl.when(has_up)
     def _():
         c_dn.wait_recv()
@@ -221,34 +275,11 @@
     def _():
         zero_rows(HALO + out_rows)
 
-    for n in (2, 3, 4, 6):
-        loads[n].wait()
-    base_row = lat * out_rows
-
-    lw_all = lat_v[...].astype(jnp.float32)
-    for i in range(out_rows):
-        begin = start_s[i]
-        width = width_s[i]
-        rows = []
-        for t in range(band_len):
-            source = begin + t
-            ok = (t < width) & (source >= 0) & (source < total_rows)
-            rows.append((ok, jnp.clip(source - base_row + HALO, 0, ext_rows - 1)))
-        for k in range(basis):
-            acc = jnp.zeros((cols, chans), jnp.float32)
-            for t, (ok, r) in enumerate(rows):
-                w = jnp.where(ok, lw_all[t, k : k + 1, i : i + 1], 0.0)
-                acc = acc + w * f_ref[k, r]
-            h_ref[i, :, k * chans : (k + 1) * chans] = acc.astype(jnp.bfloat16)
-
-    flat = (out_rows * cols, chans)
-    mixed = jnp.dot(
-        h_ref[...].reshape(out_rows * cols, basis * chans), mix_ref[...],
-        preferred_element_type=jnp.float32,
+    finish(
+        list(range(half, out_rows)),
+        lambda i: range(out_rows + 1 - i, band_len),
+        lambda r: r >= HALO + out_rows,
     )
-    out_ref[...] = (fields_ref[...].astype(jnp.float32).reshape(flat) + mixed).astype(
-        out_ref.dtype
-    ).reshape(out_ref.shape)
 
     for c in h_side:
         c.wait_send()
@@ -315,6 +346,7 @@
             pltpu.VMEM(fields.shape, fields.dtype),
             pltpu.VMEM((polar_rows, col_count, chan_count), fields.dtype),
             pltpu.VMEM((basis_count, ext_rows, col_count, chan_count), jnp.float32),
+            pltpu.VMEM((row_count, basis_count, col_count, chan_count), jnp.float32),
             pltpu.VMEM((row_count, col_count, basis_count * chan_count), jnp.bfloat16),
             pltpu.SemaphoreType.DMA((9,)),
             pltpu.SemaphoreType.DMA((9,)),

time: 21 us -> 20.5 us (0.976)
  Pallas kernels: 19 us -> 18.5 us
    pallas_call x1, Pallas kernels: 19 us -> 18.5 us  [shards(): pl.pallas_call(kernel, out_shape=jax.ShapeDtypeStruct(fields.shape, field...]
where the time goes in v11:
time: 20.5 us; the launch traced here: 20.4 us
  Pallas kernels  18.5 us (90%)
  local copies, waits for them, and re-layouts  1.87 us (9%)
    pallas_call x1, Pallas kernels, shards(): pl.pallas_call(kernel, out_shape=jax.ShapeDtypeStruct(fields.shape, field...  18.5 us
    unnamed x1, local copies, waits for them, and re-layouts  1.87 us

profile of v11, /device:TPU:145, one launch (start us, length us, event | category | flops | bytes accessed | tf_op | source)
XLA Modules:
  0.0 20.4 jit_solution(15122140040518680507)
XLA Ops:
  0.0 18.5 %shard_map.73 = bf16[8,128,256]{2,1,0:T(8,128)(2,1)} custom-call(s32[8]{0:T(128)} %start_hbm.1, s32[8]{0:T(128)} %width_hbm.1, bf16[6,4,8]{2,1,0:T(4,128)(2,1)} %bitcast.5, f32[9,4,256]{2,1,0:T(4,128)} %bitcast.4, bf16[4,8,256]{2,1,0:T(8,128)(2,1)} %cyc_hbm.1, bf16[8,128,256]{2,1,0:T(8,128)(2,1)} %fields_hbm.1, bf16[1024,256]{1,0:T(8,128)(2,1)} %bitcast.3), custom_call_target="tpu_custom_call" | custom-call | tf_op jit(solution)/shard_map/pallas_call | solution.py:328
  18.5 1.9 %copy.9 = bf16[8,128,256]{2,1,0:T(8,128)(2,1)} copy(bf16[8,128,256]{2,1,0:T(8,128)(2,1)} %shard_map.73) | data formatting | bytes 1048576

commit v12 on v11

--- a/solution.py
+++ b/solution.py
@@ -325,7 +325,7 @@
         conv_kernel, basis_count, row_count, band_len, polar_rows, total_rows
     )
     halo_block = pltpu.VMEM((HALO, col_count, chan_count), fields.dtype)
-    return pl.pallas_call(
+    return copy_out(pl.pallas_call(
         kernel,
         out_shape=jax.ShapeDtypeStruct(fields.shape, fields.dtype),
         in_specs=[hbm] * 6 + [pl.BlockSpec(memory_space=pltpu.HBM)],
@@ -355,7 +355,23 @@
         compiler_params=pltpu.CompilerParams(
             vmem_limit_bytes=67043328, collective_id=0, has_side_effects=True
         ),
-    )(band_start, band_width, lat_t, lon_t, cycle_taps, fields, mix_flat)
+    )(band_start, band_width, lat_t, lon_t, cycle_taps, fields, mix_flat))
+
+
+def copy_out(block):
+    def body(src, dst):
+        dst[...] = src[...]
+
+    rows = block.shape[0]
+    step = 2
+    spec = pl.BlockSpec((step,) + block.shape[1:], lambda i: (i, 0, 0))
+    return pl.pallas_call(
+        body,
+        out_shape=jax.ShapeDtypeStruct(block.shape, block.dtype),
+        grid=(rows // step,),
+        in_specs=[spec],
+        out_specs=spec,
+    )(block)
 
 
 def solution(mesh):

time: 20.5 us -> 21.8 us (1.063)
  Pallas kernels: 18.5 us -> 21.6 us
  local copies, waits for them, and re-layouts: 1.87 us -> 0 us
    pallas_call x0 -> x1, Pallas kernels: none -> 3.16 us  [copy_out(): pl.pallas_call(body, out_shape=jax.ShapeDtypeStruct(block.shape, block.dt...]
    unnamed x1 -> x0, local copies, waits for them, and re-layouts: 1.87 us -> none
where the time goes in v12:
time: 21.8 us; the launch traced here: 21.6 us
  Pallas kernels  21.6 us (99%)
    pallas_call x1, Pallas kernels, shards(): pl.pallas_call(kernel, out_shape=jax.ShapeDtypeStruct(fields.shape, field...  18.5 us
    pallas_call x1, Pallas kernels, copy_out(): pl.pallas_call(body, out_shape=jax.ShapeDtypeStruct(block.shape, block.dt...  3.16 us

profile of v12, /device:TPU:145, one launch (start us, length us, event | category | flops | bytes accessed | tf_op | source)
XLA Modules:
  0.0 21.6 jit_solution(3089432185396669789)
XLA Ops:
  0.0 18.5 %shard_map.73.src = bf16[8,128,256]{2,1,0:T(8,128)(2,1)} custom-call(s32[8]{0:T(128)} %start_hbm.1, s32[8]{0:T(128)} %width_hbm.1, bf16[6,4,8]{2,1,0:T(4,128)(2,1)} %bitcast.5, f32[9,4,256]{2,1,0:T(4,128)} %bitcast.4, bf16[4,8,256]{2,1,0:T(8,128)(2,1)} %cyc_hbm.1, bf16[8,128,256]{2,1,0:T(8,128)(2,1)} %fields_hbm.1, bf16[1024,256]{1,0:T(8,128)(2,1)} %bitcast.3), custom_call_target="tpu_custom_call" | custom-call | tf_op jit(solution)/shard_map/pallas_call | solution.py:328
  18.5 3.2 %shard_map.74 = bf16[8,128,256]{2,1,0:T(8,128)(2,1)} custom-call(bf16[8,128,256]{2,1,0:T(8,128)(2,1)} %shard_map.73.src), custom_call_target="tpu_custom_call" | custom-call | tf_op jit(solution)/shard_map/pallas_call | solution.py:368

commit v13 on v12

--- a/solution.py
+++ b/solution.py
@@ -359,18 +359,37 @@
 
 
 def copy_out(block):
-    def body(src, dst):
-        dst[...] = src[...]
-
-    rows = block.shape[0]
-    step = 2
-    spec = pl.BlockSpec((step,) + block.shape[1:], lambda i: (i, 0, 0))
+    pieces = 4
+    step = block.shape[0] // pieces
+
+    def body(src, dst, stage, sem_in, sem_out):
+        ins = [
+            pltpu.make_async_copy(src.at[pl.ds(n * step, step)], stage.at[pl.ds(n * step, step)], sem_in.at[n])
+            for n in range(pieces)
+        ]
+        outs = [
+            pltpu.make_async_copy(stage.at[pl.ds(n * step, step)], dst.at[pl.ds(n * step, step)], sem_out.at[n])
+            for n in range(pieces)
+        ]
+        for c in ins:
+            c.start()
+        for c_in, c_out in zip(ins, outs):
+            c_in.wait()
+            c_out.start()
+        for c in outs:
+            c.wait()
+
+    hbm = pl.BlockSpec(memory_space=pl.ANY)
     return pl.pallas_call(
         body,
         out_shape=jax.ShapeDtypeStruct(block.shape, block.dtype),
-        grid=(rows // step,),
-        in_specs=[spec],
-        out_specs=spec,
+        in_specs=[hbm],
+        out_specs=hbm,
+        scratch_shapes=[
+            pltpu.VMEM(block.shape, block.dtype),
+            pltpu.SemaphoreType.DMA((pieces,)),
+            pltpu.SemaphoreType.DMA((pieces,)),
+        ],
     )(block)
 
 

time: 21.8 us -> 20.4 us (0.936)
  Pallas kernels: 21.6 us -> 20.3 us
    pallas_call x1, Pallas kernels: 3.16 us -> 1.82 us  [copy_out(): pl.pallas_call(body, out_shape=jax.ShapeDtypeStruct(block.shape, block.dt...]
where the time goes in v13:
time: 20.4 us; the launch traced here: 20.3 us
  Pallas kernels  20.3 us (100%)
    pallas_call x1, Pallas kernels, shards(): pl.pallas_call(kernel, out_shape=jax.ShapeDtypeStruct(fields.shape, field...  18.5 us
    pallas_call x1, Pallas kernels, copy_out(): pl.pallas_call(body, out_shape=jax.ShapeDtypeStruct(block.shape, block.dt...  1.82 us

profile of v13, /device:TPU:145, one launch (start us, length us, event | category | flops | bytes accessed | tf_op | source)
XLA Modules:
  0.0 20.3 jit_solution(18243608162429836314)
XLA Ops:
  0.0 18.5 %shard_map.73.src = bf16[8,128,256]{2,1,0:T(8,128)(2,1)} custom-call(s32[8]{0:T(128)} %start_hbm.1, s32[8]{0:T(128)} %width_hbm.1, bf16[6,4,8]{2,1,0:T(4,128)(2,1)} %bitcast.5, f32[9,4,256]{2,1,0:T(4,128)} %bitcast.4, bf16[4,8,256]{2,1,0:T(8,128)(2,1)} %cyc_hbm.1, bf16[8,128,256]{2,1,0:T(8,128)(2,1)} %fields_hbm.1, bf16[1024,256]{1,0:T(8,128)(2,1)} %bitcast.3), custom_call_target="tpu_custom_call" | custom-call | tf_op jit(solution)/shard_map/pallas_call | solution.py:328
  18.5 1.8 %shard_map.74 = bf16[8,128,256]{2,1,0:T(8,128)(2,1)} custom-call(bf16[8,128,256]{2,1,0:T(8,128)(2,1)} %shard_map.73.src), custom_call_target="tpu_custom_call" | custom-call | tf_op jit(solution)/shard_map/pallas_call | solution.py:383

commit v14 on v13

--- a/solution.py
+++ b/solution.py
@@ -10,6 +10,7 @@
 HALO = 4
 LANES = 128
 EDGE = 16
+X_CHIPS = 4
 MESH = pl.DeviceIdType.MESH
 
 
@@ -251,35 +252,49 @@
 
     half = out_rows // 2
 
-    @pl.when(has_down)
-    def _():
-        c_up.wait_recv()
-        for c in h_up:
-            c.wait_recv()
-        filter_rows(top_c, top_h, HALO, 0)
-
-    @pl.when(lat == 0)
-    def _():
-        zero_rows(0)
-
-    finish(list(range(half)), lambda i: range(0, HALO - i), lambda r: r < HALO)
-
-    @pl.when(has_up)
-    def _():
-        c_dn.wait_recv()
-        for c in h_dn:
-            c.wait_recv()
-        filter_rows(bot_c, bot_h, HALO, HALO + out_rows)
-
-    @pl.when(lat == last)
-    def _():
-        zero_rows(HALO + out_rows)
-
-    finish(
-        list(range(half, out_rows)),
-        lambda i: range(out_rows + 1 - i, band_len),
-        lambda r: r >= HALO + out_rows,
-    )
+    def top_half():
+        @pl.when(has_down)
+        def _():
+            c_up.wait_recv()
+            for c in h_up:
+                c.wait_recv()
+            filter_rows(top_c, top_h, HALO, 0)
+
+        @pl.when(lat == 0)
+        def _():
+            zero_rows(0)
+
+        finish(list(range(half)), lambda i: range(0, HALO - i), lambda r: r < HALO)
+
+    def bottom_half():
+        @pl.when(has_up)
+        def _():
+            c_dn.wait_recv()
+            for c in h_dn:
+                c.wait_recv()
+            filter_rows(bot_c, bot_h, HALO, HALO + out_rows)
+
+        @pl.when(lat == last)
+        def _():
+            zero_rows(HALO + out_rows)
+
+        finish(
+            list(range(half, out_rows)),
+            lambda i: range(out_rows + 1 - i, band_len),
+            lambda r: r >= HALO + out_rows,
+        )
+
+    far_above = lax.rem(lat, X_CHIPS) == 0
+
+    @pl.when(jnp.logical_not(far_above))
+    def _():
+        top_half()
+        bottom_half()
+
+    @pl.when(far_above)
+    def _():
+        bottom_half()
+        top_half()
 
     for c in h_side:
         c.wait_send()

time: 20.4 us -> 18.8 us (0.922)
  the two profiles are of different devices: /device:TPU:145 before, /device:TPU:195 now
where the time goes in v14:
time: 18.8 us; the launch traced here: 18.7 us
  Pallas kernels  18.7 us (99%)
    pallas_call x1, Pallas kernels, shards(): pl.pallas_call(kernel, out_shape=jax.ShapeDtypeStruct(fields.shape, field...  16.9 us
    pallas_call x1, Pallas kernels, copy_out(): pl.pallas_call(body, out_shape=jax.ShapeDtypeStruct(block.shape, block.dt...  1.82 us

profile of v14, /device:TPU:195, one launch (start us, length us, event | category | flops | bytes accessed | tf_op | source)
XLA Modules:
  0.0 18.7 jit_solution(6021791485003295710)
XLA Ops:
  0.0 16.9 %shard_map.73.src = bf16[8,128,256]{2,1,0:T(8,128)(2,1)} custom-call(s32[8]{0:T(128)} %start_hbm.1, s32[8]{0:T(128)} %width_hbm.1, bf16[6,4,8]{2,1,0:T(4,128)(2,1)} %bitcast.5, f32[9,4,256]{2,1,0:T(4,128)} %bitcast.4, bf16[4,8,256]{2,1,0:T(8,128)(2,1)} %cyc_hbm.1, bf16[8,128,256]{2,1,0:T(8,128)(2,1)} %fields_hbm.1, bf16[1024,256]{1,0:T(8,128)(2,1)} %bitcast.3), custom_call_target="tpu_custom_call" | custom-call | tf_op jit(solution)/shard_map/pallas_call | solution.py:343
  16.9 1.8 %shard_map.74 = bf16[8,128,256]{2,1,0:T(8,128)(2,1)} custom-call(bf16[8,128,256]{2,1,0:T(8,128)(2,1)} %shard_map.73.src), custom_call_target="tpu_custom_call" | custom-call | tf_op jit(solution)/shard_map/pallas_call | solution.py:398

commit v15 on v14

--- a/solution.py
+++ b/solution.py
@@ -119,16 +119,24 @@
     col_id = lax.broadcasted_iota(jnp.int32, (cols, LANES), 1)
     near = jnp.abs(col_id - row_id) <= HALO
 
-    near_edge = jnp.concatenate([near[:8], near[cols - 8 :]], axis=0)
+    row8 = lax.broadcasted_iota(jnp.int32, (8, chans), 0)
 
     def filter_rows(c_ref, e_ref, count, first):
         def filter_row(r, carry):
             xc = c_ref[r]
             xe = e_ref[r]
             rhs_c = jnp.concatenate([xc, xc], axis=0)
-            rhs_e = jnp.concatenate([xe, xe], axis=0)
+            lt = xe[cols - 8 :].astype(jnp.float32)
+            rt = xe[:8].astype(jnp.float32)
+            left = [
+                jnp.where(row8 < HALO - d, pltpu.roll(lt, HALO - d, 0), 0.0) for d in range(HALO)
+            ]
+            right = [
+                jnp.where(row8 >= HALO + e, pltpu.roll(rt, (HALO + e) % 8, 0), 0.0)
+                for e in range(HALO)
+            ]
             centred = tap_u[:, first + r]
-            main, corr = [], []
+            main = []
             for k in range(basis):
                 u = centred[k : k + 1]
                 u_hi = u.astype(jnp.bfloat16).astype(jnp.float32)
@@ -139,19 +147,18 @@
                         [jnp.where(near, w_hi, 0.0), jnp.where(near, w_lo, 0.0)], axis=1
                     ).astype(jnp.bfloat16)
                 )
-                e_hi = jnp.concatenate([w_hi[:8], w_hi[cols - 8 :]], axis=0)
-                e_lo = jnp.concatenate([w_lo[:8], w_lo[cols - 8 :]], axis=0)
-                corr.append(
-                    jnp.concatenate(
-                        [jnp.where(near_edge, 0.0, e_hi), jnp.where(near_edge, 0.0, e_lo)], axis=1
-                    ).astype(jnp.bfloat16)
-                )
             y = jnp.dot(jnp.concatenate(main, axis=0), rhs_c, preferred_element_type=jnp.float32)
-            yc = jnp.dot(jnp.concatenate(corr, axis=0), rhs_e, preferred_element_type=jnp.float32)
             for k in range(basis):
+                u = centred[k : k + 1]
+
+                def tap(d):
+                    lane = (d - HALO) % LANES
+                    return jnp.broadcast_to(u[:, lane : lane + 1], (8, chans))
+
+                top = sum(tap(d) * left[d] for d in range(HALO))
+                bottom = sum(tap(2 * HALO - e) * right[e] for e in range(HALO))
                 v = y[k * cols : (k + 1) * cols]
-                c = yc[k * 16 : (k + 1) * 16]
-                v = jnp.concatenate([v[:8] + c[:8], v[8 : cols - 8], v[cols - 8 :] + c[8:]], axis=0)
+                v = jnp.concatenate([v[:8] + top, v[8 : cols - 8], v[cols - 8 :] + bottom], axis=0)
                 f_ref[k, first + r] = v.astype(jnp.bfloat16).astype(jnp.float32)
             return carry
 

time: 18.8 us -> 18.8 us (level)
  the two profiles are of different devices: /device:TPU:195 before, /device:TPU:163 now
where the time goes in v15:
time: 18.8 us; the launch traced here: 18.7 us
  Pallas kernels  18.7 us (99%)
    pallas_call x1, Pallas kernels, shards(): pl.pallas_call(kernel, out_shape=jax.ShapeDtypeStruct(fields.shape, field...  16.9 us
    pallas_call x1, Pallas kernels, copy_out(): pl.pallas_call(body, out_shape=jax.ShapeDtypeStruct(block.shape, block.dt...  1.82 us

profile of v15, /device:TPU:163, one launch (start us, length us, event | category | flops | bytes accessed | tf_op | source)
XLA Modules:
  0.0 18.7 jit_solution(11395243162804106425)
XLA Ops:
  0.0 16.9 %shard_map.73.src = bf16[8,128,256]{2,1,0:T(8,128)(2,1)} custom-call(s32[8]{0:T(128)} %start_hbm.1, s32[8]{0:T(128)} %width_hbm.1, bf16[6,4,8]{2,1,0:T(4,128)(2,1)} %bitcast.5, f32[9,4,256]{2,1,0:T(4,128)} %bitcast.4, bf16[4,8,256]{2,1,0:T(8,128)(2,1)} %cyc_hbm.1, bf16[8,128,256]{2,1,0:T(8,128)(2,1)} %fields_hbm.1, bf16[1024,256]{1,0:T(8,128)(2,1)} %bitcast.3), custom_call_target="tpu_custom_call" | custom-call | tf_op jit(solution)/shard_map/pallas_call | solution.py:350
  16.9 1.8 %shard_map.74 = bf16[8,128,256]{2,1,0:T(8,128)(2,1)} custom-call(bf16[8,128,256]{2,1,0:T(8,128)(2,1)} %shard_map.73.src), custom_call_target="tpu_custom_call" | custom-call | tf_op jit(solution)/shard_map/pallas_call | solution.py:405

commit v16 on v15

--- a/solution.py
+++ b/solution.py
@@ -80,8 +80,16 @@
     hi_rows = pl.ds(out_rows - HALO, HALO)
     first_cols = pl.ds(0, EDGE)
     last_cols = pl.ds(cols - EDGE, EDGE)
-    c_up = copy(0, fields_hbm.at[hi_rows], top_c, {"lat": up, "lon": lon})
-    c_dn = copy(1, fields_hbm.at[lo_rows], bot_c, {"lat": down, "lon": lon})
+    c_up = [
+        copy(9 + j, fields_hbm.at[pl.ds(out_rows - HALO + j, 1)], top_c.at[pl.ds(j, 1)],
+             {"lat": up, "lon": lon})
+        for j in range(HALO)
+    ]
+    c_dn = [
+        copy(9 + HALO + j, fields_hbm.at[pl.ds(j, 1)], bot_c.at[pl.ds(j, 1)],
+             {"lat": down, "lon": lon})
+        for j in range(HALO)
+    ]
     h_up = [
         copy(2, fields_hbm.at[hi_rows, first_cols], top_h.at[:, first_cols], {"lat": up, "lon": side}),
         copy(3, fields_hbm.at[hi_rows, last_cols], top_h.at[:, last_cols], {"lat": up, "lon": side}),
@@ -101,13 +109,15 @@
 
     @pl.when(has_up)
     def _():
-        c_up.start()
+        for c in c_up:
+            c.start()
         for c in h_up:
             c.start()
 
     @pl.when(has_down)
     def _():
-        c_dn.start()
+        for c in c_dn:
+            c.start()
         for c in h_dn:
             c.start()
 
@@ -121,7 +131,7 @@
 
     row8 = lax.broadcasted_iota(jnp.int32, (8, chans), 0)
 
-    def filter_rows(c_ref, e_ref, count, first):
+    def filter_rows(c_ref, e_ref, count, first, arrivals=None):
         def filter_row(r, carry):
             xc = c_ref[r]
             xe = e_ref[r]
@@ -162,7 +172,12 @@
                 f_ref[k, first + r] = v.astype(jnp.bfloat16).astype(jnp.float32)
             return carry
 
-        lax.fori_loop(0, count, filter_row, 0)
+        if arrivals is None:
+            lax.fori_loop(0, count, filter_row, 0)
+        else:
+            for j in range(count):
+                arrivals[j].wait_recv()
+                filter_row(j, 0)
 
     def zero_rows(first):
         f_ref[:, pl.ds(first, HALO)] = jnp.zeros((basis, HALO, cols, chans), jnp.float32)
@@ -262,10 +277,9 @@
     def top_half():
         @pl.when(has_down)
         def _():
-            c_up.wait_recv()
             for c in h_up:
                 c.wait_recv()
-            filter_rows(top_c, top_h, HALO, 0)
+            filter_rows(top_c, top_h, HALO, 0, c_up)
 
         @pl.when(lat == 0)
         def _():
@@ -276,10 +290,9 @@
     def bottom_half():
         @pl.when(has_up)
         def _():
-            c_dn.wait_recv()
             for c in h_dn:
                 c.wait_recv()
-            filter_rows(bot_c, bot_h, HALO, HALO + out_rows)
+            filter_rows(bot_c, bot_h, HALO, HALO + out_rows, c_dn)
 
         @pl.when(lat == last)
         def _():
@@ -308,13 +321,15 @@
 
     @pl.when(has_up)
     def _():
-        c_up.wait_send()
+        for c in c_up:
+            c.wait_send()
         for c in h_up:
             c.wait_send()
 
     @pl.when(has_down)
     def _():
-        c_dn.wait_send()
+        for c in c_dn:
+            c.wait_send()
         for c in h_dn:
             c.wait_send()
 
@@ -370,8 +385,8 @@
             pltpu.VMEM((basis_count, ext_rows, col_count, chan_count), jnp.float32),
             pltpu.VMEM((row_count, basis_count, col_count, chan_count), jnp.float32),
             pltpu.VMEM((row_count, col_count, basis_count * chan_count), jnp.bfloat16),
-            pltpu.SemaphoreType.DMA((9,)),
-            pltpu.SemaphoreType.DMA((9,)),
+            pltpu.SemaphoreType.DMA((9 + 2 * HALO,)),
+            pltpu.SemaphoreType.DMA((9 + 2 * HALO,)),
             pltpu.SemaphoreType.DMA((7,)),
         ],
         compiler_params=pltpu.CompilerParams(

time: 18.8 us -> 19.3 us (1.027)
  the two profiles are of different devices: /device:TPU:163 before, /device:TPU:227 now
where the time goes in v16:
time: 19.3 us; the launch traced here: 19.2 us
  Pallas kernels  19.2 us (99%)
    pallas_call x1, Pallas kernels, shards(): pl.pallas_call(kernel, out_shape=jax.ShapeDtypeStruct(fields.shape, field...  17.4 us
    pallas_call x1, Pallas kernels, copy_out(): pl.pallas_call(body, out_shape=jax.ShapeDtypeStruct(block.shape, block.dt...  1.82 us

profile of v16, /device:TPU:227, one launch (start us, length us, event | category | flops | bytes accessed | tf_op | source)
XLA Modules:
  0.0 19.2 jit_solution(4026154019465188683)
XLA Ops:
  0.0 17.4 %shard_map.73.src = bf16[8,128,256]{2,1,0:T(8,128)(2,1)} custom-call(s32[8]{0:T(128)} %start_hbm.1, s32[8]{0:T(128)} %width_hbm.1, bf16[6,4,8]{2,1,0:T(4,128)(2,1)} %bitcast.5, f32[9,4,256]{2,1,0:T(4,128)} %bitcast.4, bf16[4,8,256]{2,1,0:T(8,128)(2,1)} %cyc_hbm.1, bf16[8,128,256]{2,1,0:T(8,128)(2,1)} %fields_hbm.1, bf16[1024,256]{1,0:T(8,128)(2,1)} %bitcast.3), custom_call_target="tpu_custom_call" | custom-call | tf_op jit(solution)/shard_map/pallas_call | solution.py:365
  17.4 1.8 %shard_map.74 = bf16[8,128,256]{2,1,0:T(8,128)(2,1)} custom-call(bf16[8,128,256]{2,1,0:T(8,128)(2,1)} %shard_map.73.src), custom_call_target="tpu_custom_call" | custom-call | tf_op jit(solution)/shard_map/pallas_call | solution.py:420

commit v17 on v14

--- a/solution.py
+++ b/solution.py
@@ -245,10 +245,7 @@
             h_ref[pl.ds(first, count)].reshape(count * cols, basis * chans), mix_ref[...],
             preferred_element_type=jnp.float32,
         )
-        own_rows = fields_ref[pl.ds(first, count)].astype(jnp.float32).reshape(flat)
-        out_ref[pl.ds(first, count)] = (own_rows + mixed).astype(out_ref.dtype).reshape(
-            (count, cols, chans)
-        )
+        out_ref[pl.ds(first, count)] = mixed.reshape((count, cols, chans))
 
     half = out_rows // 2
 
@@ -340,9 +337,9 @@
         conv_kernel, basis_count, row_count, band_len, polar_rows, total_rows
     )
     halo_block = pltpu.VMEM((HALO, col_count, chan_count), fields.dtype)
-    return copy_out(pl.pallas_call(
+    mixed = pl.pallas_call(
         kernel,
-        out_shape=jax.ShapeDtypeStruct(fields.shape, fields.dtype),
+        out_shape=jax.ShapeDtypeStruct(fields.shape, jnp.float32),
         in_specs=[hbm] * 6 + [pl.BlockSpec(memory_space=pltpu.HBM)],
         out_specs=pl.BlockSpec(memory_space=pltpu.VMEM),
         scratch_shapes=[
@@ -370,42 +367,8 @@
         compiler_params=pltpu.CompilerParams(
             vmem_limit_bytes=67043328, collective_id=0, has_side_effects=True
         ),
-    )(band_start, band_width, lat_t, lon_t, cycle_taps, fields, mix_flat))
-
-
-def copy_out(block):
-    pieces = 4
-    step = block.shape[0] // pieces
-
-    def body(src, dst, stage, sem_in, sem_out):
-        ins = [
-            pltpu.make_async_copy(src.at[pl.ds(n * step, step)], stage.at[pl.ds(n * step, step)], sem_in.at[n])
-            for n in range(pieces)
-        ]
-        outs = [
-            pltpu.make_async_copy(stage.at[pl.ds(n * step, step)], dst.at[pl.ds(n * step, step)], sem_out.at[n])
-            for n in range(pieces)
-        ]
-        for c in ins:
-            c.start()
-        for c_in, c_out in zip(ins, outs):
-            c_in.wait()
-            c_out.start()
-        for c in outs:
-            c.wait()
-
-    hbm = pl.BlockSpec(memory_space=pl.ANY)
-    return pl.pallas_call(
-        body,
-        out_shape=jax.ShapeDtypeStruct(block.shape, block.dtype),
-        in_specs=[hbm],
-        out_specs=hbm,
-        scratch_shapes=[
-            pltpu.VMEM(block.shape, block.dtype),
-            pltpu.SemaphoreType.DMA((pieces,)),
-            pltpu.SemaphoreType.DMA((pieces,)),
-        ],
-    )(block)
+    )(band_start, band_width, lat_t, lon_t, cycle_taps, fields, mix_flat)
+    return (fields.astype(jnp.float32) + mixed).astype(fields.dtype)
 
 
 def solution(mesh):

time: 18.8 us -> 19.5 us (1.037)
  the two profiles are of different devices: /device:TPU:195 before, /device:TPU:235 now
where the time goes in v17:
time: 19.5 us; the launch traced here: 19.3 us
  Pallas kernels  17.1 us (88%)
  other arithmetic  2.27 us (12%)
    pallas_call x1, Pallas kernels, shards(): pl.pallas_call(kernel, out_shape=jax.ShapeDtypeStruct(fields.shape, jnp.f...  17.1 us
    convert_element_type x1, other arithmetic, shards(): return (fields.astype(jnp.float32) + mixed).astype(fields.dtype)  2.27 us

profile of v17, /device:TPU:235, one launch (start us, length us, event | category | flops | bytes accessed | tf_op | source)
XLA Modules:
  0.0 19.3 jit_solution(11669163416524856432)
XLA Ops:
  0.0 17.1 %shard_map.73 = f32[8,128,256]{2,1,0:T(8,128)} custom-call(s32[8]{0:T(128)} %start_hbm.1, s32[8]{0:T(128)} %width_hbm.1, bf16[6,4,8]{2,1,0:T(4,128)(2,1)} %bitcast.5, f32[9,4,256]{2,1,0:T(4,128)} %bitcast.4, bf16[4,8,256]{2,1,0:T(8,128)(2,1)} %cyc_hbm.1, bf16[8,128,256]{2,1,0:T(8,128)(2,1)} %fields_hbm.1, bf16[1024,256]{1,0:T(8,128)(2,1)} %bitcast.3), custom_call_target="tpu_custom_call" | custom-call | tf_op jit(solution)/shard_map/pallas_call | solution.py:340
  17.1 2.3 %add_convert_fusion = bf16[8,128,256]{2,1,0:T(8,128)(2,1)} fusion(f32[8,128,256]{2,1,0:T(8,128)} %shard_map.73, bf16[8,128,256]{2,1,0:T(8,128)(2,1)} %fields_hbm.1), kind=kLoop, calls=%fused_computation | loop fusion | flops 786432 | bytes 2097152 | tf_op jit(solution)/shard_map/convert_element_type | solution.py:371

commit v18 on v14

--- a/solution.py
+++ b/solution.py
@@ -21,7 +21,7 @@
 def conv_kernel(basis, out_rows, band_len, polar_count, total_rows,
                 start_hbm, width_hbm, lat_hbm, lon_hbm, cyc_hbm, fields_hbm, mix_hbm, out_ref,
                 start_s, width_s, lat_v, tap_v, tap_u, cyc_v, fields_ref, mix_ref,
-                top_c, bot_c, top_h, bot_h, own_h, polar_o, f_ref, acc_ref, h_ref,
+                top_c, bot_c, top_h, bot_h, own_h, polar_o, f_ref, acc_ref, h_ref, tm_ref, tc_ref,
                 send_sem, recv_sem, load_sem):
     cols = out_ref.shape[1]
     chans = out_ref.shape[2]
@@ -121,41 +121,62 @@
 
     near_edge = jnp.concatenate([near[:8], near[cols - 8 :]], axis=0)
 
+    def build(e):
+        centred = tap_u[:, e]
+        main, corr = [], []
+        for k in range(basis):
+            u = centred[k : k + 1]
+            u_hi = u.astype(jnp.bfloat16).astype(jnp.float32)
+            w_hi = rolled(u_hi, cols)
+            w_lo = rolled(u - u_hi, cols)
+            main.append(
+                jnp.concatenate(
+                    [jnp.where(near, w_hi, 0.0), jnp.where(near, w_lo, 0.0)], axis=1
+                ).astype(jnp.bfloat16)
+            )
+            e_hi = jnp.concatenate([w_hi[:8], w_hi[cols - 8 :]], axis=0)
+            e_lo = jnp.concatenate([w_lo[:8], w_lo[cols - 8 :]], axis=0)
+            corr.append(
+                jnp.concatenate(
+                    [jnp.where(near_edge, 0.0, e_hi), jnp.where(near_edge, 0.0, e_lo)], axis=1
+                ).astype(jnp.bfloat16)
+            )
+        return jnp.concatenate(main, axis=0), jnp.concatenate(corr, axis=0)
+
+    def apply(xc, xe, tall, tall_e, e):
+        rhs_c = jnp.concatenate([xc, xc], axis=0)
+        rhs_e = jnp.concatenate([xe, xe], axis=0)
+        y = jnp.dot(tall, rhs_c, preferred_element_type=jnp.float32)
+        yc = jnp.dot(tall_e, rhs_e, preferred_element_type=jnp.float32)
+        for k in range(basis):
+            v = y[k * cols : (k + 1) * cols]
+            c = yc[k * 16 : (k + 1) * 16]
+            v = jnp.concatenate([v[:8] + c[:8], v[8 : cols - 8], v[cols - 8 :] + c[8:]], axis=0)
+            f_ref[k, e] = v.astype(jnp.bfloat16).astype(jnp.float32)
+
     def filter_rows(c_ref, e_ref, count, first):
         def filter_row(r, carry):
-            xc = c_ref[r]
-            xe = e_ref[r]
-            rhs_c = jnp.concatenate([xc, xc], axis=0)
-            rhs_e = jnp.concatenate([xe, xe], axis=0)
-            centred = tap_u[:, first + r]
-            main, corr = [], []
-            for k in range(basis):
-                u = centred[k : k + 1]
-                u_hi = u.astype(jnp.bfloat16).astype(jnp.float32)
-                w_hi = rolled(u_hi, cols)
-                w_lo = rolled(u - u_hi, cols)
-                main.append(
-                    jnp.concatenate(
-                        [jnp.where(near, w_hi, 0.0), jnp.where(near, w_lo, 0.0)], axis=1
-                    ).astype(jnp.bfloat16)
-                )
-                e_hi = jnp.concatenate([w_hi[:8], w_hi[cols - 8 :]], axis=0)
-                e_lo = jnp.concatenate([w_lo[:8], w_lo[cols - 8 :]], axis=0)
-                corr.append(
-                    jnp.concatenate(
-                        [jnp.where(near_edge, 0.0, e_hi), jnp.where(near_edge, 0.0, e_lo)], axis=1
-                    ).astype(jnp.bfloat16)
-                )
-            y = jnp.dot(jnp.concatenate(main, axis=0), rhs_c, preferred_element_type=jnp.float32)
-            yc = jnp.dot(jnp.concatenate(corr, axis=0), rhs_e, preferred_element_type=jnp.float32)
-            for k in range(basis):
-                v = y[k * cols : (k + 1) * cols]
-                c = yc[k * 16 : (k + 1) * 16]
-                v = jnp.concatenate([v[:8] + c[:8], v[8 : cols - 8], v[cols - 8 :] + c[8:]], axis=0)
-                f_ref[k, first + r] = v.astype(jnp.bfloat16).astype(jnp.float32)
+            tall, tall_e = build(first + r)
+            apply(c_ref[r], e_ref[r], tall, tall_e, first + r)
             return carry
 
         lax.fori_loop(0, count, filter_row, 0)
+
+    def build_halo(slot, first):
+        def one(r, carry):
+            tall, tall_e = build(first + r)
+            tm_ref[slot + r] = tall
+            tc_ref[slot + r] = tall_e
+            return carry
+
+        lax.fori_loop(0, HALO, one, 0)
+
+    def filter_halo(c_ref, e_ref, slot, first):
+        def one(r, carry):
+            apply(c_ref[r], e_ref[r], tm_ref[slot + r], tc_ref[slot + r], first + r)
+            return carry
+
+        lax.fori_loop(0, HALO, one, 0)
 
     def zero_rows(first):
         f_ref[:, pl.ds(first, HALO)] = jnp.zeros((basis, HALO, cols, chans), jnp.float32)
@@ -175,6 +196,8 @@
         c.wait_recv()
     filter_rows(fields_ref, own_h, out_rows, HALO)
 
+    build_halo(0, 0)
+    build_halo(HALO, HALO + out_rows)
     loads[5].wait()
 
     def polar_rows(pole):
@@ -258,7 +281,7 @@
             c_up.wait_recv()
             for c in h_up:
                 c.wait_recv()
-            filter_rows(top_c, top_h, HALO, 0)
+            filter_halo(top_c, top_h, 0, 0)
 
         @pl.when(lat == 0)
         def _():
@@ -272,7 +295,7 @@
             c_dn.wait_recv()
             for c in h_dn:
                 c.wait_recv()
-            filter_rows(bot_c, bot_h, HALO, HALO + out_rows)
+            filter_halo(bot_c, bot_h, HALO, HALO + out_rows)
 
         @pl.when(lat == last)
         def _():
@@ -363,6 +386,8 @@
             pltpu.VMEM((basis_count, ext_rows, col_count, chan_count), jnp.float32),
             pltpu.VMEM((row_count, basis_count, col_count, chan_count), jnp.float32),
             pltpu.VMEM((row_count, col_count, basis_count * chan_count), jnp.bfloat16),
+            pltpu.VMEM((2 * HALO, basis_count * col_count, 2 * col_count), jnp.bfloat16),
+            pltpu.VMEM((2 * HALO, basis_count * 16, 2 * col_count), jnp.bfloat16),
             pltpu.SemaphoreType.DMA((9,)),
             pltpu.SemaphoreType.DMA((9,)),
             pltpu.SemaphoreType.DMA((7,)),

time: 18.8 us -> 18.4 us (0.979)
  the two profiles are of different devices: /device:TPU:195 before, /device:TPU:145 now
where the time goes in v18:
time: 18.4 us; the launch traced here: 18.2 us
  Pallas kernels  18.1 us (98%)
    pallas_call x1, Pallas kernels, shards(): pl.pallas_call(kernel, out_shape=jax.ShapeDtypeStruct(fields.shape, field...  16.3 us
    pallas_call x1, Pallas kernels, copy_out(): pl.pallas_call(body, out_shape=jax.ShapeDtypeStruct(block.shape, block.dt...  1.82 us

profile of v18, /device:TPU:145, one launch (start us, length us, event | category | flops | bytes accessed | tf_op | source)
XLA Modules:
  0.0 18.2 jit_solution(3261126528904549541)
XLA Ops:
  0.0 16.3 %shard_map.73.src = bf16[8,128,256]{2,1,0:T(8,128)(2,1)} custom-call(s32[8]{0:T(128)} %start_hbm.1, s32[8]{0:T(128)} %width_hbm.1, bf16[6,4,8]{2,1,0:T(4,128)(2,1)} %bitcast.5, f32[9,4,256]{2,1,0:T(4,128)} %bitcast.4, bf16[4,8,256]{2,1,0:T(8,128)(2,1)} %cyc_hbm.1, bf16[8,128,256]{2,1,0:T(8,128)(2,1)} %fields_hbm.1, bf16[1024,256]{1,0:T(8,128)(2,1)} %bitcast.3), custom_call_target="tpu_custom_call" | custom-call | tf_op jit(solution)/shard_map/pallas_call | solution.py:366
  16.3 1.8 %shard_map.74 = bf16[8,128,256]{2,1,0:T(8,128)(2,1)} custom-call(bf16[8,128,256]{2,1,0:T(8,128)(2,1)} %shard_map.73.src), custom_call_target="tpu_custom_call" | custom-call | tf_op jit(solution)/shard_map/pallas_call | solution.py:423

commit v19 on v18

--- a/solution.py
+++ b/solution.py
@@ -247,10 +247,17 @@
     def own(r):
         return (r >= HALO) & (r < HALO + out_rows)
 
+    def own_steps(i):
+        shifts = [0] if i == 0 else [HALO - 1] if i == out_rows - 1 else range(HALO)
+        return [
+            t for t in range(band_len)
+            if any(HALO <= i + s + t < HALO + out_rows for s in shifts)
+        ]
+
     for i in range(out_rows):
         for k in range(basis):
             acc = jnp.zeros((cols, chans), jnp.float32)
-            for t in range(band_len):
+            for t in own_steps(i):
                 r = jnp.clip(terms[i][t][1], HALO, HALO + out_rows - 1)
                 acc = acc + weight(i, k, t, own) * f_ref[k, r]
             acc_ref[i, k] = acc

time: 18.4 us -> 18.4 us (level)
  no operation moved by 1% of the time
where the time goes in v19:
time: 18.4 us; the launch traced here: 18.2 us
  Pallas kernels  18.1 us (98%)
    pallas_call x1, Pallas kernels, shards(): pl.pallas_call(kernel, out_shape=jax.ShapeDtypeStruct(fields.shape, field...  16.3 us
    pallas_call x1, Pallas kernels, copy_out(): pl.pallas_call(body, out_shape=jax.ShapeDtypeStruct(block.shape, block.dt...  1.82 us

profile of v19, /device:TPU:145, one launch (start us, length us, event | category | flops | bytes accessed | tf_op | source)
XLA Modules:
  0.0 18.2 jit_solution(2241028436412950441)
XLA Ops:
  0.0 16.3 %shard_map.73.src = bf16[8,128,256]{2,1,0:T(8,128)(2,1)} custom-call(s32[8]{0:T(128)} %start_hbm.1, s32[8]{0:T(128)} %width_hbm.1, bf16[6,4,8]{2,1,0:T(4,128)(2,1)} %bitcast.5, f32[9,4,256]{2,1,0:T(4,128)} %bitcast.4, bf16[4,8,256]{2,1,0:T(8,128)(2,1)} %cyc_hbm.1, bf16[8,128,256]{2,1,0:T(8,128)(2,1)} %fields_hbm.1, bf16[1024,256]{1,0:T(8,128)(2,1)} %bitcast.3), custom_call_target="tpu_custom_call" | custom-call | tf_op jit(solution)/shard_map/pallas_call | solution.py:373
  16.3 1.8 %shard_map.74 = bf16[8,128,256]{2,1,0:T(8,128)(2,1)} custom-call(bf16[8,128,256]{2,1,0:T(8,128)(2,1)} %shard_map.73.src), custom_call_target="tpu_custom_call" | custom-call | tf_op jit(solution)/shard_map/pallas_call | solution.py:430

commit v20 on v18

--- a/solution.py
+++ b/solution.py
@@ -22,7 +22,7 @@
                 start_hbm, width_hbm, lat_hbm, lon_hbm, cyc_hbm, fields_hbm, mix_hbm, out_ref,
                 start_s, width_s, lat_v, tap_v, tap_u, cyc_v, fields_ref, mix_ref,
                 top_c, bot_c, top_h, bot_h, own_h, polar_o, f_ref, acc_ref, h_ref, tm_ref, tc_ref,
-                send_sem, recv_sem, load_sem):
+                out_v, send_sem, recv_sem, load_sem, out_sem):
     cols = out_ref.shape[1]
     chans = out_ref.shape[2]
     ext_rows = out_rows + 2 * HALO
@@ -269,11 +269,18 @@
             preferred_element_type=jnp.float32,
         )
         own_rows = fields_ref[pl.ds(first, count)].astype(jnp.float32).reshape(flat)
-        out_ref[pl.ds(first, count)] = (own_rows + mixed).astype(out_ref.dtype).reshape(
+        out_v[pl.ds(first, count)] = (own_rows + mixed).astype(out_v.dtype).reshape(
             (count, cols, chans)
         )
+        stores[first // half].start()
 
     half = out_rows // 2
+    stores = [
+        pltpu.make_async_copy(
+            out_v.at[pl.ds(n * half, half)], out_ref.at[pl.ds(n * half, half)], out_sem.at[n]
+        )
+        for n in range(2)
+    ]
 
     def top_half():
         @pl.when(has_down)
@@ -318,6 +325,9 @@
     def _():
         bottom_half()
         top_half()
+
+    for c in stores:
+        c.wait()
 
     for c in h_side:
         c.wait_send()
@@ -367,7 +377,7 @@
         kernel,
         out_shape=jax.ShapeDtypeStruct(fields.shape, fields.dtype),
         in_specs=[hbm] * 6 + [pl.BlockSpec(memory_space=pltpu.HBM)],
-        out_specs=pl.BlockSpec(memory_space=pltpu.VMEM),
+        out_specs=pl.BlockSpec(memory_space=pl.ANY),
         scratch_shapes=[
             pltpu.SMEM(band_start.shape, band_start.dtype),
             pltpu.SMEM(band_width.shape, band_width.dtype),
@@ -388,9 +398,11 @@
             pltpu.VMEM((row_count, col_count, basis_count * chan_count), jnp.bfloat16),
             pltpu.VMEM((2 * HALO, basis_count * col_count, 2 * col_count), jnp.bfloat16),
             pltpu.VMEM((2 * HALO, basis_count * 16, 2 * col_count), jnp.bfloat16),
+            pltpu.VMEM(fields.shape, fields.dtype),
             pltpu.SemaphoreType.DMA((9,)),
             pltpu.SemaphoreType.DMA((9,)),
             pltpu.SemaphoreType.DMA((7,)),
+            pltpu.SemaphoreType.DMA((2,)),
         ],
         compiler_params=pltpu.CompilerParams(
             vmem_limit_bytes=67043328, collective_id=0, has_side_effects=True

time: 18.4 us -> 18.3 us (level)
  no operation moved by 1% of the time
where the time goes in v20:
time: 18.3 us; the launch traced here: 18.1 us
  Pallas kernels  18.1 us (99%)
    pallas_call x1, Pallas kernels, shards(): pl.pallas_call(kernel, out_shape=jax.ShapeDtypeStruct(fields.shape, field...  16.2 us
    pallas_call x1, Pallas kernels, copy_out(): pl.pallas_call(body, out_shape=jax.ShapeDtypeStruct(block.shape, block.dt...  1.82 us

profile of v20, /device:TPU:145, one launch (start us, length us, event | category | flops | bytes accessed | tf_op | source)
XLA Modules:
  0.0 18.1 jit_solution(5925107896125066983)
XLA Ops:
  0.0 16.2 %shard_map.73.src = bf16[8,128,256]{2,1,0:T(8,128)(2,1)} custom-call(s32[8]{0:T(128)} %start_hbm.1, s32[8]{0:T(128)} %width_hbm.1, bf16[6,4,8]{2,1,0:T(4,128)(2,1)} %bitcast.5, f32[9,4,256]{2,1,0:T(4,128)} %bitcast.4, bf16[4,8,256]{2,1,0:T(8,128)(2,1)} %cyc_hbm.1, bf16[8,128,256]{2,1,0:T(8,128)(2,1)} %fields_hbm.1, bf16[1024,256]{1,0:T(8,128)(2,1)} %bitcast.3), custom_call_target="tpu_custom_call" | custom-call | tf_op jit(solution)/shard_map/pallas_call | solution.py:376
  16.3 1.8 %shard_map.74 = bf16[8,128,256]{2,1,0:T(8,128)(2,1)} custom-call(bf16[8,128,256]{2,1,0:T(8,128)(2,1)} %shard_map.73.src), custom_call_target="tpu_custom_call" | custom-call | tf_op jit(solution)/shard_map/pallas_call | solution.py:435

commit v21 on v18

--- a/solution.py
+++ b/solution.py
@@ -21,7 +21,7 @@
 def conv_kernel(basis, out_rows, band_len, polar_count, total_rows,
                 start_hbm, width_hbm, lat_hbm, lon_hbm, cyc_hbm, fields_hbm, mix_hbm, out_ref,
                 start_s, width_s, lat_v, tap_v, tap_u, cyc_v, fields_ref, mix_ref,
-                top_c, bot_c, top_h, bot_h, own_h, polar_o, f_ref, acc_ref, h_ref, tm_ref, tc_ref,
+                top_c, bot_c, top_h, bot_h, own_h, polar_o, f_ref, acc_ref, h_ref, tm_ref,
                 send_sem, recv_sem, load_sem):
     cols = out_ref.shape[1]
     chans = out_ref.shape[2]
@@ -48,9 +48,6 @@
     down = jnp.maximum(lat - 1, 0)
     side = 1 - lon
 
-    middle = pl.ds(EDGE, cols - 2 * EDGE)
-    for buf in (top_h, bot_h, own_h):
-        buf[:, middle] = jnp.zeros((buf.shape[0], cols - 2 * EDGE, chans), buf.dtype)
 
     barrier = pltpu.get_barrier_semaphore()
 
@@ -119,11 +116,11 @@
     col_id = lax.broadcasted_iota(jnp.int32, (cols, LANES), 1)
     near = jnp.abs(col_id - row_id) <= HALO
 
-    near_edge = jnp.concatenate([near[:8], near[cols - 8 :]], axis=0)
+    row8 = lax.broadcasted_iota(jnp.int32, (8, chans), 0)
 
     def build(e):
         centred = tap_u[:, e]
-        main, corr = [], []
+        main = []
         for k in range(basis):
             u = centred[k : k + 1]
             u_hi = u.astype(jnp.bfloat16).astype(jnp.float32)
@@ -134,46 +131,51 @@
                     [jnp.where(near, w_hi, 0.0), jnp.where(near, w_lo, 0.0)], axis=1
                 ).astype(jnp.bfloat16)
             )
-            e_hi = jnp.concatenate([w_hi[:8], w_hi[cols - 8 :]], axis=0)
-            e_lo = jnp.concatenate([w_lo[:8], w_lo[cols - 8 :]], axis=0)
-            corr.append(
-                jnp.concatenate(
-                    [jnp.where(near_edge, 0.0, e_hi), jnp.where(near_edge, 0.0, e_lo)], axis=1
-                ).astype(jnp.bfloat16)
-            )
-        return jnp.concatenate(main, axis=0), jnp.concatenate(corr, axis=0)
-
-    def apply(xc, xe, tall, tall_e, e):
+        return jnp.concatenate(main, axis=0)
+
+    def apply(xc, e_row, tall, e):
         rhs_c = jnp.concatenate([xc, xc], axis=0)
-        rhs_e = jnp.concatenate([xe, xe], axis=0)
         y = jnp.dot(tall, rhs_c, preferred_element_type=jnp.float32)
-        yc = jnp.dot(tall_e, rhs_e, preferred_element_type=jnp.float32)
+        lt = e_row[pl.ds(cols - EDGE, EDGE)].astype(jnp.float32)[EDGE - 8 :]
+        rt = e_row[pl.ds(0, EDGE)].astype(jnp.float32)[:8]
+        left = [
+            jnp.where(row8 < HALO - d, pltpu.roll(lt, HALO - d, 0), 0.0) for d in range(HALO)
+        ]
+        right = [
+            jnp.where(row8 >= HALO + q, pltpu.roll(rt, (HALO + q) % 8, 0), 0.0)
+            for q in range(HALO)
+        ]
+        centred = tap_u[:, e]
         for k in range(basis):
+            u = centred[k : k + 1]
+
+            def tap(d):
+                lane = (d - HALO) % LANES
+                return jnp.broadcast_to(u[:, lane : lane + 1], (8, chans))
+
+            top = sum(tap(d) * left[d] for d in range(HALO))
+            bottom = sum(tap(2 * HALO - q) * right[q] for q in range(HALO))
             v = y[k * cols : (k + 1) * cols]
-            c = yc[k * 16 : (k + 1) * 16]
-            v = jnp.concatenate([v[:8] + c[:8], v[8 : cols - 8], v[cols - 8 :] + c[8:]], axis=0)
+            v = jnp.concatenate([v[:8] + top, v[8 : cols - 8], v[cols - 8 :] + bottom], axis=0)
             f_ref[k, e] = v.astype(jnp.bfloat16).astype(jnp.float32)
 
     def filter_rows(c_ref, e_ref, count, first):
         def filter_row(r, carry):
-            tall, tall_e = build(first + r)
-            apply(c_ref[r], e_ref[r], tall, tall_e, first + r)
+            apply(c_ref[r], e_ref.at[r], build(first + r), first + r)
             return carry
 
         lax.fori_loop(0, count, filter_row, 0)
 
     def build_halo(slot, first):
         def one(r, carry):
-            tall, tall_e = build(first + r)
-            tm_ref[slot + r] = tall
-            tc_ref[slot + r] = tall_e
+            tm_ref[slot + r] = build(first + r)
             return carry
 
         lax.fori_loop(0, HALO, one, 0)
 
     def filter_halo(c_ref, e_ref, slot, first):
         def one(r, carry):
-            apply(c_ref[r], e_ref[r], tm_ref[slot + r], tc_ref[slot + r], first + r)
+            apply(c_ref[r], e_ref.at[r], tm_ref[slot + r], first + r)
             return carry
 
         lax.fori_loop(0, HALO, one, 0)
@@ -387,7 +389,6 @@
             pltpu.VMEM((row_count, basis_count, col_count, chan_count), jnp.float32),
             pltpu.VMEM((row_count, col_count, basis_count * chan_count), jnp.bfloat16),
             pltpu.VMEM((2 * HALO, basis_count * col_count, 2 * col_count), jnp.bfloat16),
-            pltpu.VMEM((2 * HALO, basis_count * 16, 2 * col_count), jnp.bfloat16),
             pltpu.SemaphoreType.DMA((9,)),
             pltpu.SemaphoreType.DMA((9,)),
             pltpu.SemaphoreType.DMA((7,)),

time: 18.4 us -> 18.3 us (level)
  no operation moved by 1% of the time
where the time goes in v21:
time: 18.3 us; the launch traced here: 18.1 us
  Pallas kernels  18.1 us (99%)
    pallas_call x1, Pallas kernels, shards(): pl.pallas_call(kernel, out_shape=jax.ShapeDtypeStruct(fields.shape, field...  16.2 us
    pallas_call x1, Pallas kernels, copy_out(): pl.pallas_call(body, out_shape=jax.ShapeDtypeStruct(block.shape, block.dt...  1.82 us

profile of v21, /device:TPU:145, one launch (start us, length us, event | category | flops | bytes accessed | tf_op | source)
XLA Modules:
  0.0 18.1 jit_solution(4426192868571864768)
XLA Ops:
  0.0 16.2 %shard_map.73.src = bf16[8,128,256]{2,1,0:T(8,128)(2,1)} custom-call(s32[8]{0:T(128)} %start_hbm.1, s32[8]{0:T(128)} %width_hbm.1, bf16[6,4,8]{2,1,0:T(4,128)(2,1)} %bitcast.5, f32[9,4,256]{2,1,0:T(4,128)} %bitcast.4, bf16[4,8,256]{2,1,0:T(8,128)(2,1)} %cyc_hbm.1, bf16[8,128,256]{2,1,0:T(8,128)(2,1)} %fields_hbm.1, bf16[1024,256]{1,0:T(8,128)(2,1)} %bitcast.3), custom_call_target="tpu_custom_call" | custom-call | tf_op jit(solution)/shard_map/pallas_call | solution.py:368
  16.2 1.8 %shard_map.74 = bf16[8,128,256]{2,1,0:T(8,128)(2,1)} custom-call(bf16[8,128,256]{2,1,0:T(8,128)(2,1)} %shard_map.73.src), custom_call_target="tpu_custom_call" | custom-call | tf_op jit(solution)/shard_map/pallas_call | solution.py:424

commit v22 on v18

--- a/solution.py
+++ b/solution.py
@@ -96,20 +96,26 @@
     ]
     pol = copy(8, fields_hbm.at[pl.ds(slot, polar_count)], polar_o, {"lat": lat, "lon": side})
 
+    @pl.when(has_up)
+    def _():
+        c_up.start()
+
+    @pl.when(has_down)
+    def _():
+        c_dn.start()
+
+    @pl.when(has_up)
+    def _():
+        for c in h_up:
+            c.start()
+
+    @pl.when(has_down)
+    def _():
+        for c in h_dn:
+            c.start()
+
     for c in h_side:
         c.start()
-
-    @pl.when(has_up)
-    def _():
-        c_up.start()
-        for c in h_up:
-            c.start()
-
-    @pl.when(has_down)
-    def _():
-        c_dn.start()
-        for c in h_dn:
-            c.start()
 
     @pl.when(is_polar)
     def _():

time: 18.4 us -> 18.4 us (level)
  no operation moved by 1% of the time
where the time goes in v22:
time: 18.4 us; the launch traced here: 18.2 us
  Pallas kernels  18.1 us (98%)
    pallas_call x1, Pallas kernels, shards(): pl.pallas_call(kernel, out_shape=jax.ShapeDtypeStruct(fields.shape, field...  16.3 us
    pallas_call x1, Pallas kernels, copy_out(): pl.pallas_call(body, out_shape=jax.ShapeDtypeStruct(block.shape, block.dt...  1.82 us

profile of v22, /device:TPU:145, one launch (start us, length us, event | category | flops | bytes accessed | tf_op | source)
XLA Modules:
  0.0 18.2 jit_solution(14285088044468373994)
XLA Ops:
  0.0 16.3 %shard_map.73.src = bf16[8,128,256]{2,1,0:T(8,128)(2,1)} custom-call(s32[8]{0:T(128)} %start_hbm.1, s32[8]{0:T(128)} %width_hbm.1, bf16[6,4,8]{2,1,0:T(4,128)(2,1)} %bitcast.5, f32[9,4,256]{2,1,0:T(4,128)} %bitcast.4, bf16[4,8,256]{2,1,0:T(8,128)(2,1)} %cyc_hbm.1, bf16[8,128,256]{2,1,0:T(8,128)(2,1)} %fields_hbm.1, bf16[1024,256]{1,0:T(8,128)(2,1)} %bitcast.3), custom_call_target="tpu_custom_call" | custom-call | tf_op jit(solution)/shard_map/pallas_call | solution.py:372
  16.3 1.8 %shard_map.74 = bf16[8,128,256]{2,1,0:T(8,128)(2,1)} custom-call(bf16[8,128,256]{2,1,0:T(8,128)(2,1)} %shard_map.73.src), custom_call_target="tpu_custom_call" | custom-call | tf_op jit(solution)/shard_map/pallas_call | solution.py:429

commit v23 on v18

--- a/solution.py
+++ b/solution.py
@@ -172,11 +172,8 @@
         lax.fori_loop(0, HALO, one, 0)
 
     def filter_halo(c_ref, e_ref, slot, first):
-        def one(r, carry):
+        for r in range(HALO):
             apply(c_ref[r], e_ref[r], tm_ref[slot + r], tc_ref[slot + r], first + r)
-            return carry
-
-        lax.fori_loop(0, HALO, one, 0)
 
     def zero_rows(first):
         f_ref[:, pl.ds(first, HALO)] = jnp.zeros((basis, HALO, cols, chans), jnp.float32)

time: 18.4 us -> 17.9 us (0.973)
  Pallas kernels: 18.1 us -> 17.7 us
    pallas_call x1, Pallas kernels: 16.3 us -> 15.9 us  [shards(): pl.pallas_call(kernel, out_shape=jax.ShapeDtypeStruct(fields.shape, field...]
where the time goes in v23:
time: 17.9 us; the launch traced here: 17.7 us
  Pallas kernels  17.7 us (99%)
    pallas_call x1, Pallas kernels, shards(): pl.pallas_call(kernel, out_shape=jax.ShapeDtypeStruct(fields.shape, field...  15.9 us
    pallas_call x1, Pallas kernels, copy_out(): pl.pallas_call(body, out_shape=jax.ShapeDtypeStruct(block.shape, block.dt...  1.82 us

profile of v23, /device:TPU:145, one launch (start us, length us, event | category | flops | bytes accessed | tf_op | source)
XLA Modules:
  0.0 17.7 jit_solution(14091460941307022155)
XLA Ops:
  0.0 15.9 %shard_map.73.src = bf16[8,128,256]{2,1,0:T(8,128)(2,1)} custom-call(s32[8]{0:T(128)} %start_hbm.1, s32[8]{0:T(128)} %width_hbm.1, bf16[6,4,8]{2,1,0:T(4,128)(2,1)} %bitcast.5, f32[9,4,256]{2,1,0:T(4,128)} %bitcast.4, bf16[4,8,256]{2,1,0:T(8,128)(2,1)} %cyc_hbm.1, bf16[8,128,256]{2,1,0:T(8,128)(2,1)} %fields_hbm.1, bf16[1024,256]{1,0:T(8,128)(2,1)} %bitcast.3), custom_call_target="tpu_custom_call" | custom-call | tf_op jit(solution)/shard_map/pallas_call | solution.py:363
  15.9 1.8 %shard_map.74 = bf16[8,128,256]{2,1,0:T(8,128)(2,1)} custom-call(bf16[8,128,256]{2,1,0:T(8,128)(2,1)} %shard_map.73.src), custom_call_target="tpu_custom_call" | custom-call | tf_op jit(solution)/shard_map/pallas_call | solution.py:420

commit v24 on v23

--- a/solution.py
+++ b/solution.py
@@ -160,7 +160,8 @@
             apply(c_ref[r], e_ref[r], tall, tall_e, first + r)
             return carry
 
-        lax.fori_loop(0, count, filter_row, 0)
+        for r in range(count):
+            filter_row(r, 0)
 
     def build_halo(slot, first):
         def one(r, carry):

time: 17.9 us -> 17.9 us (level)
  no operation moved by 1% of the time
where the time goes in v24:
time: 17.9 us; the launch traced here: 17.7 us
  Pallas kernels  17.7 us (99%)
    pallas_call x1, Pallas kernels, shards(): pl.pallas_call(kernel, out_shape=jax.ShapeDtypeStruct(fields.shape, field...  15.9 us
    pallas_call x1, Pallas kernels, copy_out(): pl.pallas_call(body, out_shape=jax.ShapeDtypeStruct(block.shape, block.dt...  1.82 us

profile of v24, /device:TPU:145, one launch (start us, length us, event | category | flops | bytes accessed | tf_op | source)
XLA Modules:
  0.0 17.7 jit_solution(14264768255404974197)
XLA Ops:
  0.0 15.9 %shard_map.73.src = bf16[8,128,256]{2,1,0:T(8,128)(2,1)} custom-call(s32[8]{0:T(128)} %start_hbm.1, s32[8]{0:T(128)} %width_hbm.1, bf16[6,4,8]{2,1,0:T(4,128)(2,1)} %bitcast.5, f32[9,4,256]{2,1,0:T(4,128)} %bitcast.4, bf16[4,8,256]{2,1,0:T(8,128)(2,1)} %cyc_hbm.1, bf16[8,128,256]{2,1,0:T(8,128)(2,1)} %fields_hbm.1, bf16[1024,256]{1,0:T(8,128)(2,1)} %bitcast.3), custom_call_target="tpu_custom_call" | custom-call | tf_op jit(solution)/shard_map/pallas_call | solution.py:364
  15.9 1.8 %shard_map.74 = bf16[8,128,256]{2,1,0:T(8,128)(2,1)} custom-call(bf16[8,128,256]{2,1,0:T(8,128)(2,1)} %shard_map.73.src), custom_call_target="tpu_custom_call" | custom-call | tf_op jit(solution)/shard_map/pallas_call | solution.py:421
